TPU v7x, 32 devices: a whole 2x2x4 slice. The times are simulated.
32 devices in a mesh: slides: 2 (over y), tiles: 8 (over z, x), sub: 2 (over core).
Axes of the slice: x: 2, y: 2, z: 4, core: 2. Of those that a mesh axis runs over, the one named last changes fastest.
Arguments:
- tile_data: bfloat16 [96, 12, 12, 192], P(('slides', 'tiles'), None, None, 'sub'), parts along dimension 0, may hold values from -64 to 64
- cotangent: bfloat16 [96, 12, 12, 192], P(('slides', 'tiles'), None, None, 'sub'), parts along dimension 0, may hold values from -6 to 6
- neighbour: int32 [96, 8], P(('slides', 'tiles')), parts along dimension 0, may hold values from 0 to 47, as said below
- tissue: int32 [96, 8], P(('slides', 'tiles')), parts along dimension 0, may hold values from 0 to 1, as said below
- kernel: float32 [7, 7, 192], P(None, None, 'sub'), may hold values from -0.875 to 0.875
- conv_bias: float32 [192], P('sub'), may hold values from -3 to 3
- layer_norm_gain: float32 [192], P('sub'), may hold values from 0.5 to 2
- layer_norm_bias: float32 [192], P('sub'), may hold values from -3 to 3
- w_in: float32 [192, 768], P(None, 'sub'), may hold values from -0.4375 to 0.4375
- b_in: float32 [768], P('sub'), may hold values from -3 to 3
- w_out: float32 [768, 192], P('sub'), may hold values from -0.21875 to 0.21875
- b_out: float32 [192], P('sub'), may hold values from -3 to 3
- layer_scale: float32 [192], P('sub'), may hold values from 0.3 to 1
Outputs:
- block_out: bfloat16 [96, 12, 12, 192], P(('slides', 'tiles'), None, None, 'sub'), parts along dimension 0
- tile_grad: bfloat16 [96, 12, 12, 192], P(('slides', 'tiles'), None, None, 'sub'), parts along dimension 0
- grad_w_in: float32 [384, 768], P('slides', 'sub'), parts along dimension 0
- grad_w_out: float32 [1536, 192], P(('slides', 'sub')), parts along dimension 0
- grad_kernel: float32 [14, 7, 192], P('slides', None, 'sub'), parts along dimension 0
There are 2 independent parts, one for each index of `slides`. A program takes and returns all parts, laid end to end along the dimension named above; an argument that names none is the same for every part. Nothing has to cross between parts.
Inputs may be any that keep to these rules, and one draw needn't show every extreme that they name: Tile t is held by index t // 6 of tiles. If neighbour[t, d] = u then neighbour[u, e] = t for the opposite side e (north and south, west and east, north-west and south-east, north-east and south-west). The index of tiles that holds neighbour[t, d] is (t // 6 + an offset that depends only on d and t % 6) % 8. Over all eight sides, the tiles of one index of tiles name tiles of any one index at most 6 times, and every index reaches 6. tissue[t, d] = tissue[neighbour[t, d], e] for the opposite side e.
All inputs are finite; a program needn't handle non-finite values.
Results may differ from a plain program's by a relative error of at most 0.0079.
Values may be sent and summed in bfloat16 or wider, within the bound.
No kernel may reach another device: no remote copies, remote signals or barrier semaphores. Data moves between devices by JAX's collectives and lax.ppermute only.
A program may use at most 64 MiB of HBM per device.

v0:
```python
import math

import jax
import jax.numpy as jnp
from jax import lax
from jax.sharding import PartitionSpec as P

eps_norm = 1e-06
root_half = 0.7071067811865476
inv_root_tau = 0.3989422804014327


def edge_strip(block_data, kind_code):
    if kind_code == 0:
        return block_data[:, -3:]
    if kind_code == 1:
        return block_data[:, :3]
    if kind_code == 2:
        return jnp.swapaxes(block_data[:, :, -3:], 1, 2)
    return jnp.swapaxes(block_data[:, :, :3], 1, 2)


def all_strips(block_data):
    return jnp.stack([edge_strip(block_data, kind_code) for kind_code in range(4)], axis=1)


def assemble(inner, strips):
    top_band = jnp.concatenate(
        [strips[:, 4][:, :, -3:], strips[:, 0], strips[:, 5][:, :, :3]], axis=2
    )
    low_band = jnp.concatenate(
        [strips[:, 6][:, :, -3:], strips[:, 1], strips[:, 7][:, :, :3]], axis=2
    )
    mid_band = jnp.concatenate(
        [jnp.swapaxes(strips[:, 2], 1, 2), inner, jnp.swapaxes(strips[:, 3], 1, 2)], axis=2
    )
    return jnp.concatenate([top_band, mid_band, low_band], axis=1)


def depthwise(field, weights):
    return lax.conv_general_dilated(
        field,
        weights[:, :, None, :],
        (1, 1),
        "VALID",
        dimension_numbers=("NHWC", "HWIO", "NHWC"),
        feature_group_count=field.shape[3],
        precision=lax.Precision.HIGHEST,
    )


def rim_pieces(spread, tile_side):
    north = spread[:, 0:3, 3 : tile_side + 3]
    south = spread[:, tile_side + 3 :, 3 : tile_side + 3]
    west = jnp.swapaxes(spread[:, 3 : tile_side + 3, 0:3], 1, 2)
    east = jnp.swapaxes(spread[:, 3 : tile_side + 3, tile_side + 3 :], 1, 2)
    pad_front = ((0, 0), (0, 0), (tile_side - 3, 0), (0, 0))
    pad_back = ((0, 0), (0, 0), (0, tile_side - 3), (0, 0))
    north_west = jnp.pad(spread[:, 0:3, 0:3], pad_front)
    north_east = jnp.pad(spread[:, 0:3, tile_side + 3 :], pad_back)
    south_west = jnp.pad(spread[:, tile_side + 3 :, 0:3], pad_front)
    south_east = jnp.pad(spread[:, tile_side + 3 :, tile_side + 3 :], pad_back)
    return jnp.stack(
        [north, south, west, east, north_west, north_east, south_west, south_east], axis=1
    )


def spread_edges(edges, tile_side):
    lower = jnp.pad(edges[:, 0], ((0, 0), (tile_side - 3, 0), (0, 0), (0, 0)))
    upper = jnp.pad(edges[:, 1], ((0, 0), (0, tile_side - 3), (0, 0), (0, 0)))
    right_cols = jnp.pad(
        jnp.swapaxes(edges[:, 2], 1, 2), ((0, 0), (0, 0), (tile_side - 3, 0), (0, 0))
    )
    left_cols = jnp.pad(
        jnp.swapaxes(edges[:, 3], 1, 2), ((0, 0), (0, 0), (0, tile_side - 3), (0, 0))
    )
    return lower + upper + right_cols + left_cols


def local(
    tile_data,
    cotangent,
    neighbour,
    tissue,
    kernel,
    conv_bias,
    layer_norm_gain,
    layer_norm_bias,
    w_in,
    b_in,
    w_out,
    b_out,
    layer_scale,
):
    tile_dev = tile_data.shape[0]
    tile_side = tile_data.shape[1]
    local_ch = tile_data.shape[3]
    every_channel = w_in.shape[0]
    owners = lax.axis_size("tiles")
    capacity = max(2, 8 * tile_dev // owners)
    scale = 1.0 / math.sqrt(owners * tile_dev * tile_side * tile_side)
    slot_shape = (owners, capacity, 3, tile_side, local_ch)
    flat_shape = (owners * capacity, 3, tile_side, local_ch)
    links = neighbour.reshape(-1)
    target = links // tile_dev
    directions = jnp.tile(jnp.arange(8, dtype=jnp.int32), tile_dev)
    request = links % tile_dev * 8 + directions
    hits = (target[:, None] == jnp.arange(owners, dtype=jnp.int32)[None, :]).astype(jnp.int32)
    earlier = jnp.cumsum(hits, axis=0) - hits
    position = target * capacity + jnp.sum(earlier * hits, axis=1)
    asked = jnp.full((owners * capacity,), -1, jnp.int32).at[position].set(request)
    wanted = lax.all_to_all(
        asked.reshape(owners, capacity), "tiles", split_axis=0, concat_axis=0, tiled=True
    ).reshape(-1)
    served = wanted >= 0
    safe_code = jnp.where(served, wanted, 0)
    facing = safe_code % 8
    which = safe_code // 8 * 4 + jnp.where(facing < 4, facing, (facing - 4) // 2)
    keep_slot = served[:, None, None, None]
    keep_side = (tissue > 0)[:, :, None, None, None]
    strips = all_strips(tile_data).reshape(tile_dev * 4, 3, tile_side, local_ch)
    picked = jnp.where(keep_slot, strips[which], jnp.zeros_like(strips[which]))
    fetched_data = lax.all_to_all(
        picked.reshape(slot_shape), "tiles", split_axis=0, concat_axis=0, tiled=True
    )
    mine = fetched_data.reshape(flat_shape)[position].reshape(tile_dev, 8, 3, tile_side, local_ch)
    grown = assemble(tile_data, jnp.where(keep_side, mine, jnp.zeros_like(mine)))
    grown32 = grown.astype(jnp.float32)
    spatial = depthwise(grown32, kernel) + conv_bias
    flat = spatial.reshape(-1, local_ch)
    mean_row = lax.psum(jnp.sum(flat, axis=1), "sub") / every_channel
    centre_pixel = flat - mean_row[:, None]
    spread_var = (lax.psum(jnp.sum(centre_pixel * centre_pixel, axis=1), "sub") / every_channel)[
        :, None
    ]
    inverse_deviation = lax.rsqrt(spread_var + eps_norm)
    standardized_input = centre_pixel * inverse_deviation
    normed_rows = (standardized_input * layer_norm_gain + layer_norm_bias).astype(jnp.bfloat16)
    cot_flat = cotangent.reshape(flat.shape)
    g_branch = (layer_scale * cot_flat.astype(jnp.float32)).astype(jnp.bfloat16)
    normed_all, branch_all = (
        lax.all_gather(normed_rows, "sub", axis=1, tiled=True),
        lax.all_gather(g_branch, "sub", axis=1, tiled=True),
    )
    w_in16 = w_in.astype(jnp.bfloat16)
    w_out16 = w_out.astype(jnp.bfloat16)
    pre = jnp.dot(normed_all, w_in16, preferred_element_type=jnp.float32) + b_in
    act = jax.nn.gelu(pre, approximate=False).astype(jnp.bfloat16)
    branch_part = jnp.dot(act, w_out16, preferred_element_type=jnp.float32)
    g_act = jnp.dot(branch_all, w_out16.T, preferred_element_type=jnp.float32)
    slope = 0.5 * (1.0 + lax.erf(pre * root_half)) + pre * jnp.exp(-0.5 * pre * pre) * inv_root_tau
    g_pre = (g_act * slope).astype(jnp.bfloat16)
    part_out = jnp.dot(act.T, branch_all, preferred_element_type=jnp.float32)
    part_in = jnp.dot(normed_all.T, g_pre, preferred_element_type=jnp.float32)
    normed_part = jnp.dot(g_pre, w_in16.T, preferred_element_type=jnp.float32)
    branch_mine, g_normed = (
        lax.psum_scatter(branch_part, "sub", scatter_dimension=1, tiled=True),
        lax.psum_scatter(normed_part, "sub", scatter_dimension=1, tiled=True),
    )
    residual = tile_data.reshape(flat.shape).astype(jnp.float32)
    block_out = (
        (residual + layer_scale * (branch_mine + b_out))
        .astype(jnp.bfloat16)
        .reshape(tile_data.shape)
    )
    standardized_gradient = g_normed * layer_norm_gain
    leading_gradient, trailing_gradient = lax.psum(
        (
            jnp.sum(standardized_gradient, axis=1),
            jnp.sum(standardized_gradient * standardized_input, axis=1),
        ),
        "sub",
    )
    flattened_gradient = inverse_deviation * (
        standardized_gradient
        - (leading_gradient / every_channel)[:, None]
        - standardized_input * (trailing_gradient / every_channel)[:, None]
    )
    g_conv = flattened_gradient.astype(jnp.bfloat16).reshape(spatial.shape)
    unused, pull_back = jax.vjp(lambda weights: depthwise(grown32, weights), kernel)
    part_kernel = pull_back(g_conv.astype(jnp.float32))[0]
    flipped = kernel[::-1, ::-1]
    cot32 = cotangent.astype(jnp.float32)
    spread = depthwise(
        jnp.pad(g_conv.astype(jnp.float32), ((0, 0), (6, 6), (6, 6), (0, 0))), flipped
    )
    rims = jnp.where(keep_side, rim_pieces(spread, tile_side), 0.0).reshape(
        tile_dev * 8, 3, tile_side, local_ch
    )
    outbox = jnp.zeros(flat_shape, jnp.float32).at[position].set(rims)
    inbox = (
        lax.all_to_all(
            outbox.reshape(slot_shape).astype(jnp.bfloat16),
            "tiles",
            split_axis=0,
            concat_axis=0,
            tiled=True,
        )
        .astype(jnp.float32)
        .reshape(flat_shape)
    )
    inbox = jnp.where(keep_slot, inbox, 0.0)
    edges = jnp.zeros((tile_dev * 4, 3, tile_side, local_ch), jnp.float32).at[which].add(inbox)
    edges = edges.reshape(tile_dev, 4, 3, tile_side, local_ch)
    total = cot32 + spread[:, 3 : tile_side + 3, 3 : tile_side + 3] + spread_edges(edges, tile_side)
    tile_grad = total.astype(jnp.bfloat16)
    sum_in, sum_out, sum_kernel = lax.psum((part_in, part_out, part_kernel), "tiles")
    return (block_out, tile_grad, sum_in * scale, sum_out * scale, sum_kernel * scale)


def solution(mesh):
    placed = (
        P(("slides", "tiles"), None, None, "sub"),
        P(("slides", "tiles"), None, None, "sub"),
        P(("slides", "tiles"), None),
        P(("slides", "tiles"), None),
        P(None, None, "sub"),
        P("sub"),
        P("sub"),
        P("sub"),
        P(None, "sub"),
        P("sub"),
        P("sub", None),
        P("sub"),
        P("sub"),
    )
    return jax.shard_map(
        local,
        mesh=mesh,
        in_specs=placed,
        out_specs=(
            P(("slides", "tiles"), None, None, "sub"),
            P(("slides", "tiles"), None, None, "sub"),
            P("slides", "sub"),
            P(("slides", "sub"), None),
            P("slides", None, "sub"),
        ),
        check_vma=False,
    )
```

profile of v0, /device:TPU:0, one launch (start us, length us, event | category | flops | bytes accessed | tf_op | source)
XLA Modules:
  0.0 919.4 jit_solution(12505497066346320158)
XLA Ops:
  7.2 0.7 broadcast_remainder_fusion
  7.9 0.7 compare_and_fusion
  9.1 0.2 select_reduce_fusion
  9.4 0.7 scatter_custom_fusion
  10.2 0.7 all_to_all.12
  10.8 7.3 all-to-all-start
  18.1 0.9 fusion.46
  19.0 1.0 slice_bitcast_fusion.11
  20.1 0.3 pad_maximum_fusion
  20.6 3.8 all-to-all-done
  24.5 0.5 broadcast.370
  25.0 0.7 reduce.5
  25.8 0.7 gather_fusion
  26.6 0.9 copy.199
  27.5 3.5 all-to-all-start.1
  31.4 14.3 %all-to-all-done.1 = bf16[8,6,3,12,96]{4,1,3,2,0:T(8,128)(2,1)S(1)} async-done(((bf16[8,6,3,12,96]{4,1,3,2,0:T(8,128)(2,1)}), bf16[8,6,3,12,96]{4,1,3,2,0:T(8,128)(2,1)S(1)}, u32[]{:S(2)}, u32[]{:S(2)}) %all-to-all-start.1) | async-done | bytes 331808 | tf_op jit(solution)/shard_map/all_to_all | solution.py:123
  45.9 0.7 gather_fusion.1
  46.5 0.3 copy_select_fusion
  47.2 0.4 copy-done.10
  47.6 2.8 fusion.47
  50.4 0.2 copy.209
  50.7 2.5 psum.49
  53.6 0.4 multiply_reduce_fusion
  54.0 0.2 copy.212
  54.3 2.5 psum.50
  56.9 0.2 copy.210
  57.2 2.1 all_gather.6
  59.3 4.1 fusion.3
  63.3 1.3 fusion.26
  64.7 0.2 all-reduce.12.cloned.1.call-start
  65.3 0.2 copy.217
  65.5 0.2 copy.213
  65.7 6.4 reduce-scatter.3.cloned.1.call-done
  72.1 1.2 multiply_convert_fusion.1
  73.3 2.1 all_gather.7
  75.4 1.1 fusion.49
  76.4 0.7 fusion
  77.1 1.1 fusion.48
  78.3 1.3 fusion.28
  79.7 0.2 copy.214
  79.9 0.8 reshape.335
  80.7 71.7 %all-reduce.12.cloned.1.call-done = (f32[192,384]{1,0:T(8,128)}, f32[384,192]{0,1:T(8,128)}) async-done(((f32[192,384]{1,0:T(8,128)}, f32[384,192]{0,1:T(8,128)}), (f32[192,384]{1,0:T(8,128)}, f32[384,192]{0,1:T(8,128)})) %all-reduce.12.cloned.1.call-update) | async-done | bytes 589840 | tf_op jit(solution)/shard_map/psum | solution.py:207
  152.4 1.7 broadcast_multiply_fusion
  154.1 1.7 broadcast_multiply_fusion.1
  155.8 6.1 reduce-scatter.5.cloned.1.call-done
  162.0 1.1 multiply_reduce_fusion.2
  163.1 2.5 all-reduce.9
  165.6 1.1 multiply_convert_fusion
  167.0 685.4 %fusion.19 = f32[6,18,18,96]{3,0,2,1:T(8,128)S(1)} fusion(bf16[6,12,12,96]{3,2,1,0:T(8,128)(2,1)S(1)} %reshape.336, f32[7,7,1,96]{3,1,0,2:T(8,128)S(1)} %bitcast.129), kind=kOutput, calls=%fused_computation.55 | convolution fusion | flops 48771072 | bytes 931200 | tf_op jit(solution)/shard_map/conv_general_dilated | solution.py:41
  852.6 0.2 copy.241
  852.8 1.2 bitcast_select_fusion.1
  854.1 5.0 scatter_fusion
  859.0 0.3 copy.282
  859.3 0.2 convert_element_type.89
  859.5 0.9 copy.226
  860.5 5.7 all-to-all-start.2
  866.2 2.7 fusion.17
  868.9 38.1 %psum.55 = f32[7,7,96]{2,1,0:T(8,128)S(1)} all-reduce(f32[7,7,96]{2,1,0:T(8,128)S(1)} %bitcast.128), channel_id=1, replica_groups=mesh['slides'=2,'tiles'=8,'sub'=2] {'tiles'}, use_global_device_ids=true, to_apply=%region_17.18 | all-reduce | flops 4704 | bytes 37632 | tf_op jit(solution)/shard_map/psum | solution.py:207
  907.0 0.6 broadcast_multiply_fusion.2
  907.7 0.2 copy.242
  908.1 3.2 scatter_fusion.1
  911.5 0.3 fusion.45
  911.9 0.2 fusion.16
  912.2 0.8 copy.236
  (114 shorter events, 4.4 us)
Async XLA Ops:
  10.8 13.6 %all-to-all-start = ((s32[8,1,6]{2,1,0:T(1,128)}), s32[8,1,6]{2,1,0:T(1,128)S(1)}, u32[]{:S(2)}, u32[]{:S(2)}) async-start(s32[8,1,6]{2,1,0:T(1,128)} %bitcast.2), calls=%async_computation | async-start | bytes 8192 | tf_op jit(solution)/shard_map/all_to_all | solution.py:112
  26.6 4.5 copy-start
  26.6 4.7 copy-start.12
  27.5 18.2 %all-to-all-start.1 = ((bf16[8,6,3,12,96]{4,1,3,2,0:T(8,128)(2,1)}), bf16[8,6,3,12,96]{4,1,3,2,0:T(8,128)(2,1)S(1)}, u32[]{:S(2)}, u32[]{:S(2)}) async-start(bf16[8,6,3,12,96]{4,1,3,2,0:T(8,128)(2,1)} %copy.199), calls=%async_computation.1 | async-start | bytes 1179648 | tf_op jit(solution)/shard_map/all_to_all | solution.py:123
  31.1 41.0 %reduce-scatter.3.cloned.1.call-start = ((), (), s32[]{:S(2)}) async-start(), calls=%async_computation.5 | async-start | bytes 1032192 | tf_op jit(solution)/shard_map/reduce_scatter | solution.py:157
  46.8 0.8 copy-start.10
  46.8 0.7 copy-start.17
  47.2 3.2 copy-start.4
  53.6 3.5 copy-start.11
  53.6 3.5 copy-start.15
  56.8 2.5 copy-start.8
  56.8 2.5 copy-start.16
  59.3 4.1 copy-start.6
  63.3 1.6 copy-start.1
  64.7 87.8 %all-reduce.12.cloned.1.call-start = ((), (), s32[]{:S(2)}) async-start(), calls=%async_computation.7 | async-start | bytes 1179648 | tf_op jit(solution)/shard_map/psum | solution.py:207
  65.2 6.8 copy-start.13
  65.3 6.8 copy-start.14
  65.7 10.7 %copy-start.7 = (f32[384,192]{0,1:T(8,128)S(1)}, f32[384,192]{0,1:T(8,128)}, u32[]{:S(2)}) copy-start(f32[384,192]{0,1:T(8,128)} %param.23) | copy-start | bytes 884740
  72.1 4.3 copy-start.18
  77.1 1.1 copy-start.9
  78.2 83.8 %reduce-scatter.5.cloned.1.call-start = ((), (), s32[]{:S(2)}) async-start(), calls=%async_computation.6 | async-start | bytes 1032192 | tf_op jit(solution)/shard_map/reduce_scatter | solution.py:158
  167.0 685.5 %copy-start.2 = (bf16[6,12,12,96]{3,2,1,0:T(8,128)(2,1)}, bf16[6,12,12,96]{3,2,1,0:T(8,128)(2,1)S(1)}, u32[]{:S(2)}) copy-start(bf16[6,12,12,96]{3,2,1,0:T(8,128)(2,1)S(1)} %reshape.336) | copy-start | bytes 497668
  859.5 6.7 copy-start.3
  859.5 6.7 copy-start.5
  860.5 47.1 %all-to-all-start.2 = ((bf16[8,6,3,12,96]{4,1,3,2,0:T(8,128)(2,1)}), bf16[8,6,3,12,96]{4,1,3,2,0:T(8,128)(2,1)S(1)}, u32[]{:S(2)}, u32[]{:S(2)}) async-start(bf16[8,6,3,12,96]{4,1,3,2,0:T(8,128)(2,1)} %copy.226), calls=%async_computation.4 | async-start | bytes 1179648 | tf_op jit(solution)/shard_map/all_to_all | solution.py:192
Sparse Core Ops, SparseCore 0:
  64.8 7.2 reduce-scatter.2
  78.3 74.0 all-reduce.11
  154.8 7.1 reduce-scatter.4
where the time goes:
time: 920 us; the launch traced here: 919 us
  matrix products  700 us (76%)
  waiting for transfers between devices  102 us (11%)
  blocking collectives  49.6 us (5%)
  local copies, waits for them, and re-layouts  19.3 us (2%)
  starting transfers between devices  16.8 us (2%)
  other arithmetic  16.5 us (2%)
  between operations  14.5 us (2%)
    conv_general_dilated x3, matrix products, depthwise(): lax.conv_general_dilated(field, weights[:, :, None, :], (1, 1), 'VALID',...  691 us
    psum x1, waiting for transfers between devices, local(): lax.psum((part_in, part_out, part_kernel), 'tiles')  71.7 us
    psum x1, blocking collectives, local(): lax.psum((part_in, part_out, part_kernel), 'tiles')  38.1 us
  transfers between devices with their start and end apart: 6, of which 5 were waited for; matrix products, arithmetic and copies ran while one was open for 1% of the time, Pallas kernels for 0%

commit v1 on v0

v1 whole, which is shorter than its diff:
```python
import math

import jax
import jax.numpy as jnp
from jax import lax
from jax.sharding import PartitionSpec as P

eps_norm = 1e-06
root_half = 0.7071067811865476
inv_root_tau = 0.3989422804014327


def edge_strip(block_data, kind_code):
    if kind_code == 0:
        return block_data[:, -3:]
    if kind_code == 1:
        return block_data[:, :3]
    if kind_code == 2:
        return jnp.swapaxes(block_data[:, :, -3:], 1, 2)
    return jnp.swapaxes(block_data[:, :, :3], 1, 2)


def all_strips(block_data):
    return jnp.stack([edge_strip(block_data, kind_code) for kind_code in range(4)], axis=1)


def assemble(inner, strips):
    top_band = jnp.concatenate(
        [strips[:, 4][:, :, -3:], strips[:, 0], strips[:, 5][:, :, :3]], axis=2
    )
    low_band = jnp.concatenate(
        [strips[:, 6][:, :, -3:], strips[:, 1], strips[:, 7][:, :, :3]], axis=2
    )
    mid_band = jnp.concatenate(
        [jnp.swapaxes(strips[:, 2], 1, 2), inner, jnp.swapaxes(strips[:, 3], 1, 2)], axis=2
    )
    return jnp.concatenate([top_band, mid_band, low_band], axis=1)


def depthwise(field, weights):
    return lax.conv_general_dilated(
        field,
        weights[:, :, None, :],
        (1, 1),
        "VALID",
        dimension_numbers=("NHWC", "HWIO", "NHWC"),
        feature_group_count=field.shape[3],
        precision=lax.Precision.HIGHEST,
    )


served_kind = (1, 0, 3, 2, 1, 1, 0, 0)
opposite = (1, 0, 3, 2, 7, 6, 5, 4)


def slots_of(neighbour, tile_dev, owners, capacity):
    links = neighbour.reshape(-1)
    count = links.shape[0]
    target = links // tile_dev
    offset = jnp.mod(target - lax.axis_index("tiles"), owners)
    order = jnp.arange(count, dtype=jnp.int32)
    same = offset[:, None] == offset[None, :]
    rank = jnp.sum((same & (order[None, :] < order[:, None])).astype(jnp.int32), axis=1)
    receive = target * capacity + rank
    facing = jnp.tile(jnp.array(opposite, jnp.int32), tile_dev)
    mirror = links % tile_dev * 8 + facing
    mirror_hot = mirror[:, None] == order[None, :]
    send = target * capacity + jnp.sum(jnp.where(mirror_hot, rank[None, :], 0), axis=1)
    slot = jnp.arange(owners * capacity, dtype=jnp.int32)
    fill = slot[:, None] == send[None, :]
    kinds = jnp.tile(jnp.array(served_kind, jnp.int32), tile_dev)
    which = order // 8 * 4 + kinds
    source = jnp.sum(jnp.where(fill, which[None, :], 0), axis=1)
    return receive, source


def exchange_tiles(box):
    return lax.all_to_all(box, "tiles", split_axis=0, concat_axis=0, tiled=True)


def swap_sub(piece):
    return lax.ppermute(piece, "sub", [(0, 1), (1, 0)])


def halo(block_data, receive, source, keep_side, owners, capacity):
    tile_dev, tile_side, unused, local_ch = block_data.shape
    strips = all_strips(block_data).reshape(tile_dev * 4, 3 * tile_side, local_ch)
    outbox = strips[source].reshape(owners, capacity * 3 * tile_side, local_ch)
    inbox = exchange_tiles(outbox).reshape(owners * capacity, 3, tile_side, local_ch)
    mine = inbox[receive].reshape(tile_dev, 8, 3, tile_side, local_ch)
    return assemble(block_data, jnp.where(keep_side, mine, jnp.zeros_like(mine)))


def local(
    tile_data,
    cotangent,
    neighbour,
    tissue,
    kernel,
    conv_bias,
    layer_norm_gain,
    layer_norm_bias,
    w_in,
    b_in,
    w_out,
    b_out,
    layer_scale,
):
    tile_dev, tile_side, unused, local_ch = tile_data.shape
    every_channel = w_in.shape[0]
    half_hidden = w_in.shape[1]
    owners = lax.axis_size("tiles")
    capacity = max(2, 8 * tile_dev // owners)
    half = tile_dev // 2
    scale = 1.0 / math.sqrt(owners * tile_dev * tile_side * tile_side)
    core = lax.axis_index("sub")
    first = core == 0

    def join(own, other, axis):
        return jnp.where(
            first,
            jnp.concatenate([own, other], axis=axis),
            jnp.concatenate([other, own], axis=axis),
        )

    def split(block):
        own = lax.dynamic_slice_in_dim(block, core * half, half, 0)
        other = lax.dynamic_slice_in_dim(block, (1 - core) * half, half, 0)
        return own.reshape(-1, block.shape[-1]), other.reshape(-1, block.shape[-1])

    receive, source = slots_of(neighbour, tile_dev, owners, capacity)
    keep_side = (tissue > 0)[:, :, None, None, None]
    grown = halo(tile_data, receive, source, keep_side, owners, capacity)

    w_in16 = w_in.astype(jnp.bfloat16)
    w_out16 = w_out.astype(jnp.bfloat16)
    w_in_all = jnp.concatenate([w_in16, swap_sub(w_in16)], axis=1)
    w_out_all = jnp.concatenate([w_out16, swap_sub(w_out16)], axis=0)
    b_in_all = jnp.concatenate([b_in, swap_sub(b_in)])
    vectors = jnp.stack([layer_norm_gain, layer_norm_bias, b_out, layer_scale])
    vectors = join(vectors, swap_sub(vectors), 1)
    gain, shift, b_out_all, branch_scale = vectors
    pair_own, pair_other = split(jnp.concatenate([tile_data, cotangent], axis=3))
    pair_other = swap_sub(pair_other)
    inner_rows = join(pair_own[:, :local_ch], pair_other[:, :local_ch], 1)
    cot_rows = join(pair_own[:, local_ch:], pair_other[:, local_ch:], 1)
    g_branch = (branch_scale * cot_rows.astype(jnp.float32)).astype(jnp.bfloat16)

    grown32 = grown.astype(jnp.float32)
    spatial = depthwise(grown32, kernel) + conv_bias
    spatial_own, spatial_other = split(spatial)
    flat = join(spatial_own, swap_sub(spatial_other), 1)
    centre_pixel = flat - jnp.mean(flat, axis=1, keepdims=True)
    spread_var = jnp.mean(centre_pixel * centre_pixel, axis=1, keepdims=True)
    inverse_deviation = lax.rsqrt(spread_var + eps_norm)
    standardized_input = centre_pixel * inverse_deviation
    normed = (standardized_input * gain + shift).astype(jnp.bfloat16)
    pre = jnp.dot(normed, w_in_all, preferred_element_type=jnp.float32) + b_in_all
    cdf = 0.5 * (1.0 + lax.erf(pre * root_half))
    act = (pre * cdf).astype(jnp.bfloat16)
    branch = jnp.dot(act, w_out_all, preferred_element_type=jnp.float32) + b_out_all
    block_rows = (inner_rows.astype(jnp.float32) + branch_scale * branch).astype(jnp.bfloat16)
    g_act = jnp.dot(g_branch, w_out_all.T, preferred_element_type=jnp.float32)
    slope = cdf + pre * jnp.exp(-0.5 * pre * pre) * inv_root_tau
    g_pre = (g_act * slope).astype(jnp.bfloat16)
    part_out = jnp.dot(act.T, g_branch, preferred_element_type=jnp.float32)
    part_in = jnp.dot(normed.T, g_pre, preferred_element_type=jnp.float32)
    g_normed = jnp.dot(g_pre, w_in_all.T, preferred_element_type=jnp.float32)
    standardized_gradient = g_normed * gain
    g_rows = (
        inverse_deviation
        * (
            standardized_gradient
            - jnp.mean(standardized_gradient, axis=1, keepdims=True)
            - standardized_input
            * jnp.mean(standardized_gradient * standardized_input, axis=1, keepdims=True)
        )
    ).astype(jnp.bfloat16)

    def back(rows):
        low, high = rows[:, :local_ch], rows[:, local_ch:]
        return jnp.where(first, low, high), jnp.where(first, high, low)

    g_own, g_other = back(g_rows)
    block_own, block_other = back(block_rows)
    g_other, block_other = swap_sub(g_other), swap_sub(block_other)
    tile_shape = (half,) + tile_data.shape[1:]
    g_conv = join(g_own.reshape(tile_shape), g_other.reshape(tile_shape), 0)
    block_out = join(block_own.reshape(tile_shape), block_other.reshape(tile_shape), 0)

    other_in = swap_sub(part_in[:, half_hidden:].astype(jnp.bfloat16))
    other_out = swap_sub(part_out[half_hidden:].astype(jnp.bfloat16))
    sum_in = part_in[:, :half_hidden] + other_in.astype(jnp.float32)
    sum_out = part_out[:half_hidden] + other_out.astype(jnp.float32)
    size = every_channel * half_hidden
    parts = jnp.concatenate([sum_in.reshape(owners, -1), sum_out.reshape(owners, -1)], axis=1)
    shares = exchange_tiles(parts.astype(jnp.bfloat16))
    share = jnp.sum(shares.astype(jnp.float32), axis=0).astype(jnp.bfloat16)

    g_grown = halo(g_conv, receive, source, keep_side, owners, capacity).astype(jnp.float32)
    unused, pull_back = jax.vjp(lambda weights: depthwise(grown32, weights), kernel)
    part_kernel = pull_back(g_conv.astype(jnp.float32))[0]
    message = jnp.concatenate([share, part_kernel.astype(jnp.bfloat16).reshape(-1)])
    everyone = exchange_tiles(jnp.broadcast_to(message[None], (owners,) + message.shape))
    each = size // owners
    grad_in = everyone[:, :each].reshape(w_in.shape).astype(jnp.float32) * scale
    grad_out = everyone[:, each : 2 * each].reshape(w_out.shape).astype(jnp.float32) * scale
    grad_kernel = jnp.sum(everyone[:, 2 * each :].astype(jnp.float32), axis=0) * scale
    tile_grad = cotangent.astype(jnp.float32) + depthwise(g_grown, kernel[::-1, ::-1])
    return (
        block_out,
        tile_grad.astype(jnp.bfloat16),
        grad_in,
        grad_out,
        grad_kernel.reshape(kernel.shape),
    )


def solution(mesh):
    placed = (
        P(("slides", "tiles"), None, None, "sub"),
        P(("slides", "tiles"), None, None, "sub"),
        P(("slides", "tiles"), None),
        P(("slides", "tiles"), None),
        P(None, None, "sub"),
        P("sub"),
        P("sub"),
        P("sub"),
        P(None, "sub"),
        P("sub"),
        P("sub", None),
        P("sub"),
        P("sub"),
    )
    return jax.shard_map(
        local,
        mesh=mesh,
        in_specs=placed,
        out_specs=(
            P(("slides", "tiles"), None, None, "sub"),
            P(("slides", "tiles"), None, None, "sub"),
            P("slides", "sub"),
            P(("slides", "sub"), None),
            P("slides", None, "sub"),
        ),
        check_vma=False,
    )
```

time: 920 us -> 99.5 us (0.11)
  matrix products: 700 us -> 15.4 us
  waiting for transfers between devices: 102 us -> 20.8 us
  blocking collectives: 49.6 us -> 0 us
  between operations: 14.5 us -> 1.62 us
    conv_general_dilated x3, matrix products: 691 us -> 8.54 us  [depthwise(): lax.conv_general_dilated(field, weights[:, :, None, :], (1, 1), 'VALID',...]
    psum x1 -> x0, waiting for transfers between devices: 71.7 us -> none  [local(): lax.psum((part_in, part_out, part_kernel), 'tiles')]
    psum x4 -> x0, blocking collectives: 45.5 us -> none  [the longest x1 38.1 us: local(): lax.psum((part_in, part_out, part_kernel), 'tiles')]
    reduce_scatter x2 -> x0, waiting for transfers between devices: 12.5 us -> none  [the longest x1 6.36 us: local(): lax.psum_scatter(branch_part, 'sub', scatter_dimension=1, tiled=True)]
    all_to_all x3 -> x4, starting transfers between devices: 16.5 us -> 19.3 us  [exchange_tiles(): return lax.all_to_all(box, 'tiles', split_axis=0, concat_axis=0, tiled=True)]
    all_to_all x3 -> x4, waiting for transfers between devices: 18.1 us -> 19.6 us  [exchange_tiles(): return lax.all_to_all(box, 'tiles', split_axis=0, concat_axis=0, tiled=True)]
  transfers between devices with their start and end apart: 6 -> 14, of which waited for: 5 -> 5; matrix products, arithmetic and copies ran while one was open for 1% -> 41% of each run, Pallas kernels for 0% -> 0%
where the time goes in v1:
time: 99.5 us; the launch traced here: 98.5 us
  local copies, waits for them, and re-layouts  26.3 us (26%)
  starting transfers between devices  21.6 us (22%)
  waiting for transfers between devices  20.8 us (21%)
  matrix products  15.4 us (15%)
  other arithmetic  12.9 us (13%)
  between operations  1.62 us (2%)
    all_to_all x4, waiting for transfers between devices, exchange_tiles(): return lax.all_to_all(box, 'tiles', split_axis=0, concat_axis=0, tiled=True)  19.6 us
    all_to_all x4, starting transfers between devices, exchange_tiles(): return lax.all_to_all(box, 'tiles', split_axis=0, concat_axis=0, tiled=True)  19.3 us
    conv_general_dilated x3, matrix products, depthwise(): lax.conv_general_dilated(field, weights[:, :, None, :], (1, 1), 'VALID',...  8.54 us
    unnamed x55, local copies, waits for them, and re-layouts  8.15 us
    broadcast_in_dim x1, other arithmetic, local(): jnp.broadcast_to(message[None], (owners,) + message.shape)  2.85 us
    ppermute x10, starting transfers between devices, swap_sub(): return lax.ppermute(piece, 'sub', [(0, 1), (1, 0)])  2.29 us
    reshape x4, local copies, waits for them, and re-layouts, halo(): outbox = strips[source].reshape(owners, capacity * 3 * tile_side, local_ch)  2.22 us
  transfers between devices with their start and end apart: 14, of which 5 were waited for; matrix products, arithmetic and copies ran while one was open for 41% of the time, Pallas kernels for 0%

profile of v1, /device:TPU:0, one launch (start us, length us, event | category | flops | bytes accessed | tf_op | source)
XLA Modules:
  0.0 98.5 jit_solution(12616652958334142872)
XLA Ops:
  0.6 0.7 broadcast_remainder_fusion
  1.3 0.7 compare_and_fusion
  2.0 0.9 fusion.51
  3.0 1.0 %slice_bitcast_fusion.19 = (bf16[6,1,3,12,96]{4,2,3,0,1:T(4,128)(2,1)S(1)}, bf16[6,1,3,12,96]{4,2,3,0,1:T(4,128)(2,1)S(1)}) fusion(bf16[6,12,12,96]{3,2,1,0:T(8,128)(2,1)} %param.15), kind=kLoop, calls=%fused_computation.102 | loop fusion | bytes 165888 | tf_op jit(solution)/shard_map/stack | solution.py:24
  4.3 0.7 tile.20
  5.0 0.7 tile.8
  6.4 0.3 pad_maximum_fusion
  6.8 0.7 gather_fusion
  7.8 1.0 copy.242
  8.7 7.3 %all-to-all-start = ((bf16[8,216,96]{1,2,0:T(8,128)(2,1)}), bf16[8,216,96]{1,2,0:T(8,128)(2,1)S(1)}, u32[]{:S(2)}, u32[]{:S(2)}) async-start(bf16[8,216,96]{1,2,0:T(8,128)(2,1)} %copy.242), calls=%async_computation | async-start | bytes 786432 | tf_op jit(solution)/shard_map/all_to_all | solution.py:78
  16.1 0.7 convert_element_type.81
  16.8 0.5 collective-permute-start.3
  17.9 0.5 collective-permute-start
  18.4 0.7 convert_element_type.83
  19.9 0.7 copy.292
  20.6 0.6 rev.3
  21.2 0.7 copy.293
  22.1 0.6 fusion.54
  22.7 5.0 %all-to-all-done = bf16[8,216,96]{1,2,0:T(8,128)(2,1)S(1)} async-done(((bf16[8,216,96]{1,2,0:T(8,128)(2,1)}), bf16[8,216,96]{1,2,0:T(8,128)(2,1)S(1)}, u32[]{:S(2)}, u32[]{:S(2)}) %all-to-all-start) | async-done | bytes 331808 | tf_op jit(solution)/shard_map/all_to_all | solution.py:78
  28.1 0.7 gather_fusion.1
  28.7 0.3 copy_select_fusion.1
  29.4 0.4 copy-done.7
  29.8 2.8 %convolution_add_fusion.2 = f32[6,12,12,96]{3,0,2,1:T(8,128)S(1)} fusion(bf16[6,18,18,96]{3,0,2,1:T(8,128)(2,1)S(1)} %maximum_maximum_fusion, f32[96]{0:T(128)S(1)} %copy-done.20, f32[7,7,1,96]{3,1,0,2:T(8,128)S(1)} %bitcast.108), kind=kOutput, calls=%fused_computation.15 | convolution fusion | flops 48854016 | bytes 724224 | tf_op jit(solution)/shard_map/conv_general_dilated | solution.py:41
  33.3 1.2 %collective-permute-done.2 = f32[432,96]{0,1:T(8,128)S(1)} collective-permute-done((f32[432,96]{0,1:T(8,128)S(1)}, f32[432,96]{0,1:T(8,128)S(1)}, u32[]{:S(2)}, u32[]{:S(2)}) %collective-permute-start.2) | collective-permute-done | bytes 165920 | tf_op jit(solution)/shard_map/ppermute | solution.py:82
  34.7 1.6 %multiply_convert_fusion = (bf16[432,768]{1,0:T(8,128)(2,1)S(1)}, f32[432,768]{1,0:T(8,128)S(1)}) fusion(f32[768]{0:T(1024)S(1)} %pad_maximum_fusion.10, bf16[192,384]{1,0:T(8,128)(2,1)} %collective-permute-done.3, bf16[192,384]{1,0:T(8,128)(2,1)} %convert_element_type.81, f32[192]{0:T(256)S(1)} %bitcast.125, f32[192]{0:T(256)S(1)} %bitcast.122, ...), kind=kOutput, calls=%fused_computation.12 | convolution fusion | flops 130646016 | bytes 2625409 | tf_op jit(solution)/shard_map/dot_general | solution.py:158
  36.3 1.7 %fusion = bf16[432,768]{1,0:T(8,128)(2,1)S(1)} fusion(f32[432,768]{1,0:T(8,128)S(1)} %get-tuple-element.87, bf16[384,192]{0,1:T(8,128)(2,1)} %collective-permute-done.5, bf16[384,192]{0,1:T(8,128)(2,1)} %convert_element_type.83, bf16[432,96]{0,1:T(8,128)(2,1)S(1)} %get-tuple-element.75, bf16[432,96]{0,1:T(8,128)(2,1)S(1)} %copy-done.5, ...), kind=kOutput, calls=%fused_computation.7 | convolution fusion | flops 132304896 | bytes 2452225 | tf_op jit(solution)/shard_map/dot_general | solution.py:163
  38.1 0.4 fusion.47
  38.7 0.4 fusion.46
  39.1 0.7 slice.280
  39.8 0.3 collective-permute-start.9
  40.1 1.4 %fusion.49 = (f32[432]{0:T(512)S(1)}, f32[432]{0:T(512)S(1)}, f32[432,192]{0,1:T(8,128)S(1)}) fusion(f32[432]{0:T(512)S(1)} %add_rsqrt_fusion, f32[432]{0:T(512)S(1)} %broadcast_multiply_fusion.3, f32[432,96]{0,1:T(8,128)S(1)} %copy.253, f32[432,96]{0,1:T(8,128)S(1)} %collective-permute-done.2, pred[]{:T(512)S(6)} %eq.49, f32[192]{0:T(256)S(1)} %bitcast.124, ...), kind=kOutput, calls=%fused_computation.160 | convolution fusion | flops 128737440 | bytes 1629697 | tf_op jit(solution)/shard_map/dot_general | solution.py:168
  41.9 0.5 copy-done.4
  42.4 1.4 %add_convert_fusion = bf16[432,192]{0,1:T(8,128)(2,1)S(1)} fusion(bf16[432,96]{0,1:T(8,128)(2,1)S(1)} %get-tuple-element.76, bf16[432,96]{0,1:T(8,128)(2,1)S(1)} %copy-done.4, f32[192]{0:T(256)S(1)} %bitcast.121, bf16[432,768]{1,0:T(8,128)(2,1)S(1)} %get-tuple-element.86, f32[192]{0:T(256)S(1)} %bitcast.120, pred[]{:T(512)S(6)} %eq.49, ...), kind=kOutput, calls=%fused_computation.50 | convolution fusion | flops 129153024 | bytes 1291777 | tf_op jit(solution)/shard_map/dot_general | solution.py:161
  43.7 0.7 broadcast_select_fusion.3
  45.5 0.3 maximum_select_fusion.2
  45.9 0.9 fusion.28
  46.9 0.9 fusion.27
  48.2 0.5 broadcast.339
  48.8 0.8 reduce.4
  49.6 0.9 reshape.377
  50.5 3.6 %all-to-all-start.2 = ((bf16[8,2,9216]{2,1,0:T(2,128)(2,1)}), bf16[8,2,9216]{2,1,0:T(2,128)(2,1)S(1)}, u32[]{:S(2)}, u32[]{:S(2)}) async-start(bf16[8,2,9216]{2,1,0:T(2,128)(2,1)} %reshape.377), calls=%async_computation.2 | async-start | bytes 589824 | tf_op jit(solution)/shard_map/all_to_all | solution.py:78
  54.5 0.7 gather_fusion.2
  55.4 1.0 copy.273
  56.3 7.9 %all-to-all-done.2 = bf16[8,2,9216]{2,1,0:T(2,128)(2,1)S(1)} async-done(((bf16[8,2,9216]{2,1,0:T(2,128)(2,1)}), bf16[8,2,9216]{2,1,0:T(2,128)(2,1)S(1)}, u32[]{:S(2)}, u32[]{:S(2)}) %all-to-all-start.2) | async-done | bytes 294944 | tf_op jit(solution)/shard_map/all_to_all | solution.py:78
  64.2 3.6 %all-to-all-start.1 = ((bf16[8,216,96]{1,2,0:T(8,128)(2,1)}), bf16[8,216,96]{1,2,0:T(8,128)(2,1)S(1)}, u32[]{:S(2)}, u32[]{:S(2)}) async-start(bf16[8,216,96]{1,2,0:T(8,128)(2,1)} %copy.273), calls=%async_computation.1 | async-start | bytes 786432 | tf_op jit(solution)/shard_map/all_to_all | solution.py:78
  67.9 2.9 %fusion.7 = bf16[7,7,96]{2,1,0:T(8,128)(2,1)S(1)} fusion(bf16[6,18,18,96]{3,0,2,1:T(8,128)(2,1)S(1)} %maximum_maximum_fusion, bf16[6,12,12,96]{3,0,2,1:T(8,128)(2,1)S(1)} %maximum_select_fusion.2), kind=kOutput, calls=%fused_computation.21 | convolution fusion | flops 8133216 | bytes 548544 | tf_op jit(solution)/shard_map/transpose(jvp())/conv_general_dilated | solution.py:41
  70.8 1.0 %copy.256 = bf16[432,96]{1,0:T(8,128)(2,1)S(1)} copy(bf16[432,96]{0,1:T(8,128)(2,1)} %collective-permute-done.6) | data formatting | bytes 165888 | tf_op jit(solution)/shard_map/ppermute | solution.py:82
  72.0 0.4 maximum_select_fusion.1
  72.4 0.8 copy.282
  73.4 0.7 reduce_sum.101
  74.1 0.4 broadcast_in_dim.68
  74.5 2.8 %reduce.5 = bf16[8,23136]{1,0:T(8,128)(2,1)S(1)} reduce(bf16[8,1,23136]{2,1,0:T(2,128)(2,1)S(1)} %broadcast_in_dim.68, bf16[]{:T(256)} %broadcast.339), dimensions={1}, to_apply=%broadcast_in_dim.68.reduce_sub_computation | reduce | bytes 740354 | tf_op jit(solution)/shard_map/broadcast_in_dim | solution.py:204
  77.3 1.1 %reshape.379 = bf16[8,2,11568]{2,1,0:T(2,128)(2,1)} reshape(bf16[8,23136]{1,0:T(8,128)(2,1)S(1)} %reduce.5) | data formatting | bytes 740352
  78.5 1.2 %all-to-all-done.1 = bf16[8,216,96]{1,2,0:T(8,128)(2,1)S(1)} async-done(((bf16[8,216,96]{1,2,0:T(8,128)(2,1)}), bf16[8,216,96]{1,2,0:T(8,128)(2,1)S(1)}, u32[]{:S(2)}, u32[]{:S(2)}) %all-to-all-start.1) | async-done | bytes 331808 | tf_op jit(solution)/shard_map/all_to_all | solution.py:78
  79.7 4.8 %all-to-all-start.3 = ((bf16[8,2,11568]{2,1,0:T(2,128)(2,1)}), bf16[8,2,11568]{2,1,0:T(2,128)(2,1)S(1)}, u32[]{:S(2)}, u32[]{:S(2)}) async-start(bf16[8,2,11568]{2,1,0:T(2,128)(2,1)} %reshape.379), calls=%async_computation.3 | async-start | bytes 745472 | tf_op jit(solution)/shard_map/all_to_all | solution.py:78
  84.9 0.7 gather_fusion.3
  85.5 0.3 copy_select_fusion
  86.3 2.9 %fusion.5 = bf16[6,12,12,96]{3,0,2,1:T(8,128)(2,1)S(1)} fusion(bf16[6,3,3,96]{3,0,2,1:T(8,128)(2,1)S(1)} %slice.233, bf16[6,3,12,96]{3,0,2,1:T(8,128)(2,1)S(1)} %get-tuple-element.43, bf16[6,3,3,96]{3,0,2,1:T(8,128)(2,1)S(1)} %slice.230, bf16[6,12,12,96]{3,0,2,1:T(8,128)(2,1)S(1)} %maximum_select_fusion.2, bf16[6,3,3,96]{3,0,2,1:T(8,128)(2,1)S(1)} %slice.226, ...), kind=kOutput, calls=%fused_computation.16 | convolution fusion | flops 52379136 | bytes 723840 | tf_op jit(solution)/shard_map/conv_general_dilated | solution.py:41
  89.2 0.8 copy.283
  89.9 5.4 %all-to-all-done.3 = bf16[8,2,11568]{2,1,0:T(2,128)(2,1)S(1)} async-done(((bf16[8,2,11568]{2,1,0:T(2,128)(2,1)}), bf16[8,2,11568]{2,1,0:T(2,128)(2,1)S(1)}, u32[]{:S(2)}, u32[]{:S(2)}) %all-to-all-start.3) | async-done | bytes 370208 | tf_op jit(solution)/shard_map/all_to_all | solution.py:78
  95.4 0.5 reshape.380
  96.2 0.9 copy.284
  97.0 0.8 mul.204
  97.8 0.7 mul.209
  (150 shorter events, 8.5 us)
Async XLA Ops:
  7.5 8.5 %copy-start.11 = (f32[96]{0:T(128)S(1)}, f32[96]{0:T(128)}, u32[]{:S(2)}) copy-start(f32[96]{0:T(128)} %param.27) | copy-start | bytes 1156
  7.5 8.5 %copy-start.12 = (f32[96]{0:T(128)S(1)}, f32[96]{0:T(128)}, u32[]{:S(2)}) copy-start(f32[96]{0:T(128)} %param.26) | copy-start | bytes 1156
  7.5 8.5 %copy-start.13 = (f32[96]{0:T(128)S(1)}, f32[96]{0:T(128)}, u32[]{:S(2)}) copy-start(f32[96]{0:T(128)} %param.22) | copy-start | bytes 1156
  7.6 8.5 %copy-start.14 = (f32[96]{0:T(128)S(1)}, f32[96]{0:T(128)}, u32[]{:S(2)}) copy-start(f32[96]{0:T(128)} %param.21) | copy-start | bytes 1156
  7.6 8.6 %copy-start.1 = (f32[192,384]{1,0:T(8,128)S(1)}, f32[192,384]{1,0:T(8,128)}, u32[]{:S(2)}) copy-start(f32[192,384]{1,0:T(8,128)} %param.23) | copy-start | bytes 884740
  7.6 9.7 %copy-start.10 = (f32[384]{0:T(512)S(1)}, f32[384]{0:T(512)}, u32[]{:S(2)}) copy-start(f32[384]{0:T(512)} %param.24) | copy-start | bytes 4612
  7.6 9.8 %copy-start = (bf16[6,12,12,96]{3,2,1,0:T(8,128)(2,1)S(1)}, bf16[6,12,12,96]{3,2,1,0:T(8,128)(2,1)}, u32[]{:S(2)}) copy-start(bf16[6,12,12,96]{3,2,1,0:T(8,128)(2,1)} %param.15) | copy-start | bytes 497668
  7.6 9.8 %copy-start.3 = (bf16[6,12,12,96]{3,2,1,0:T(8,128)(2,1)S(1)}, bf16[6,12,12,96]{3,2,1,0:T(8,128)(2,1)}, u32[]{:S(2)}) copy-start(bf16[6,12,12,96]{3,2,1,0:T(8,128)(2,1)} %param.16) | copy-start | bytes 497668
  8.7 18.9 %all-to-all-start = ((bf16[8,216,96]{1,2,0:T(8,128)(2,1)}), bf16[8,216,96]{1,2,0:T(8,128)(2,1)S(1)}, u32[]{:S(2)}, u32[]{:S(2)}) async-start(bf16[8,216,96]{1,2,0:T(8,128)(2,1)} %copy.242), calls=%async_computation | async-start | bytes 786432 | tf_op jit(solution)/shard_map/all_to_all | solution.py:78
  16.0 2.4 %copy-start.2 = (f32[384,192]{0,1:T(8,128)S(1)}, f32[384,192]{0,1:T(8,128)}, u32[]{:S(2)}) copy-start(f32[384,192]{0,1:T(8,128)} %param.25) | copy-start | bytes 884740
  16.0 5.9 %collective-permute-start.1 = (f32[4,96]{1,0:T(4,128)S(1)}, f32[4,96]{1,0:T(4,128)S(1)}, u32[]{:S(2)}, u32[]{:S(2)}) collective-permute-start(f32[4,96]{1,0:T(4,128)S(1)} %pad_maximum_fusion.11), channel_id=1, source_target_pairs={{0,1},{1,0},{2,3},{3,2},{4,5},{5,4},{6,7},{7,6},{8,9},{9,8},{10,11... | collective-permute-start | bytes 4616 | tf_op jit(solution)/shard_map/ppermute | solution.py:82
  16.8 2.5 %copy-start.9 = (s32[6,8]{1,0:T(8,128)S(1)}, s32[6,8]{1,0:T(8,128)}, u32[]{:S(2)}) copy-start(s32[6,8]{1,0:T(8,128)} %param.18) | copy-start | bytes 580
  16.8 17.8 %collective-permute-start.3 = (bf16[192,384]{1,0:T(8,128)(2,1)}, bf16[192,384]{1,0:T(8,128)(2,1)}, u32[]{:S(2)}, u32[]{:S(2)}) collective-permute-start(bf16[192,384]{1,0:T(8,128)(2,1)} %convert_element_type.81), channel_id=1, source_target_pairs={{0,1},{1,0},{2,3},{3,2},{4,5},{5,4},{6,7},{7,6},{8,9},{9,8},{10,11... | collective-permute-start | bytes 442376 | tf_op jit(solution)/shard_map/ppermute | solution.py:82
  17.3 4.7 %collective-permute-start.4 = (f32[384]{0:T(512)S(1)}, f32[384]{0:T(512)S(1)}, u32[]{:S(2)}, u32[]{:S(2)}) collective-permute-start(f32[384]{0:T(512)S(1)} %copy-done.10), channel_id=1, source_target_pairs={{0,1},{1,0},{2,3},{3,2},{4,5},{5,4},{6,7},{7,6},{8,9},{9,8},{10,11... | collective-permute-start | bytes 4616 | tf_op jit(solution)/shard_map/ppermute | solution.py:82
  17.8 2.8 %copy-start.6 = (f32[7,7,96]{2,1,0:T(8,128)S(1)}, f32[7,7,96]{2,1,0:T(8,128)}, u32[]{:S(2)}) copy-start(f32[7,7,96]{2,1,0:T(8,128)} %param.19) | copy-start | bytes 56452
  17.9 15.1 %collective-permute-start = (bf16[432,192]{0,1:T(8,128)(2,1)S(1)}, bf16[432,192]{0,1:T(8,128)(2,1)S(1)}, u32[]{:S(2)}, u32[]{:S(2)}) collective-permute-start(bf16[432,192]{0,1:T(8,128)(2,1)S(1)} %copy.236), channel_id=1, source_target_pairs={{0,1},{1,0},{2,3},{3,2},{4,5},{5,4},{6,7},{7,6},{8,9},{9,8},{10,11... | collective-permute-start | bytes 497672 | tf_op jit(solution)/shard_map/ppermute | solution.py:82
  19.1 17.2 %collective-permute-start.5 = (bf16[384,192]{0,1:T(8,128)(2,1)}, bf16[384,192]{0,1:T(8,128)(2,1)}, u32[]{:S(2)}, u32[]{:S(2)}) collective-permute-start(bf16[384,192]{0,1:T(8,128)(2,1)} %convert_element_type.83), channel_id=1, source_target_pairs={{0,1},{1,0},{2,3},{3,2},{4,5},{5,4},{6,7},{7,6},{8,9},{9,8},{10,11... | collective-permute-start | bytes 442376 | tf_op jit(solution)/shard_map/ppermute | solution.py:82
  22.7 13.6 %copy-start.15 = (f32[1,192]{1,0:T(1,128)}, f32[1,192]{1,0:T(1,128)S(1)}, u32[]{:S(2)}) copy-start(f32[1,192]{1,0:T(1,128)S(1)} %get-tuple-element.79) | copy-start | bytes 2308
  29.0 0.8 copy-start.7
  29.1 0.7 copy-start.20
  32.9 1.7 %copy-start.18 = (f32[1,192]{1,0:T(1,128)S(1)}, f32[1,192]{1,0:T(1,128)}, u32[]{:S(2)}) copy-start(f32[1,192]{1,0:T(1,128)} %get-tuple-element.82) | copy-start | bytes 2308
  32.9 1.7 %copy-start.19 = (f32[1,192]{1,0:T(1,128)S(1)}, f32[1,192]{1,0:T(1,128)}, u32[]{:S(2)}) copy-start(f32[1,192]{1,0:T(1,128)} %get-tuple-element.81) | copy-start | bytes 2308
  33.0 1.5 %collective-permute-start.2 = (f32[432,96]{0,1:T(8,128)S(1)}, f32[432,96]{0,1:T(8,128)S(1)}, u32[]{:S(2)}, u32[]{:S(2)}) collective-permute-start(f32[432,96]{0,1:T(8,128)S(1)} %copy.252), channel_id=1, source_target_pairs={{0,1},{1,0},{2,3},{3,2},{4,5},{5,4},{6,7},{7,6},{8,9},{9,8},{10,11... | collective-permute-start | bytes 497672 | tf_op jit(solution)/shard_map/ppermute | solution.py:82
  34.6 1.7 %copy-start.5 = (bf16[432,96]{0,1:T(8,128)(2,1)S(1)}, bf16[432,96]{0,1:T(8,128)(2,1)}, u32[]{:S(2)}) copy-start(bf16[432,96]{0,1:T(8,128)(2,1)} %copy.292) | copy-start | bytes 248836
  38.1 0.7 copy-start.16
  38.5 7.4 %collective-permute-start.8 = (bf16[192,384]{1,0:T(8,128)(2,1)S(1)}, bf16[192,384]{1,0:T(8,128)(2,1)}, u32[]{:S(2)}, u32[]{:S(2)}) collective-permute-start(bf16[192,384]{1,0:T(8,128)(2,1)S(1)} %slice.281), channel_id=1, source_target_pairs={{0,1},{1,0},{2,3},{3,2},{4,5},{5,4},{6,7},{7,6},{8,9},{9,8},{10,11... | collective-permute-start | bytes 442376 | tf_op jit(solution)/shard_map/ppermute | solution.py:82
  39.8 7.2 %collective-permute-start.9 = (bf16[384,192]{0,1:T(8,128)(2,1)}, bf16[384,192]{0,1:T(8,128)(2,1)}, u32[]{:S(2)}, u32[]{:S(2)}) collective-permute-start(bf16[384,192]{0,1:T(8,128)(2,1)} %slice.280), channel_id=1, source_target_pairs={{0,1},{1,0},{2,3},{3,2},{4,5},{5,4},{6,7},{7,6},{8,9},{9,8},{10,11... | collective-permute-start | bytes 442376 | tf_op jit(solution)/shard_map/ppermute | solution.py:82
  41.5 0.9 copy-start.4
  41.5 0.9 copy-start.17
  41.7 3.6 %collective-permute-start.7 = (bf16[432,96]{0,1:T(8,128)(2,1)S(1)}, bf16[432,96]{0,1:T(8,128)(2,1)S(1)}, u32[]{:S(2)}, u32[]{:S(2)}) collective-permute-start(bf16[432,96]{0,1:T(8,128)(2,1)S(1)} %get-tuple-element.74), channel_id=1, source_target_pairs={{0,1},{1,0},{2,3},{3,2},{4,5},{5,4},{6,7},{7,6},{8,9},{9,8},{10,11... | collective-permute-start | bytes 248840 | tf_op jit(solution)/shard_map/ppermute | solution.py:82
  44.7 26.1 %collective-permute-start.6 = (bf16[432,96]{0,1:T(8,128)(2,1)}, bf16[432,96]{0,1:T(8,128)(2,1)}, u32[]{:S(2)}, u32[]{:S(2)}) collective-permute-start(bf16[432,96]{0,1:T(8,128)(2,1)} %get-tuple-element.78), channel_id=1, source_target_pairs={{0,1},{1,0},{2,3},{3,2},{4,5},{5,4},{6,7},{7,6},{8,9},{9,8},{10,11... | collective-permute-start | bytes 248840 | tf_op jit(solution)/shard_map/ppermute | solution.py:82
  50.5 13.7 %all-to-all-start.2 = ((bf16[8,2,9216]{2,1,0:T(2,128)(2,1)}), bf16[8,2,9216]{2,1,0:T(2,128)(2,1)S(1)}, u32[]{:S(2)}, u32[]{:S(2)}) async-start(bf16[8,2,9216]{2,1,0:T(2,128)(2,1)} %reshape.377), calls=%async_computation.2 | async-start | bytes 589824 | tf_op jit(solution)/shard_map/all_to_all | solution.py:78
  64.2 15.5 %all-to-all-start.1 = ((bf16[8,216,96]{1,2,0:T(8,128)(2,1)}), bf16[8,216,96]{1,2,0:T(8,128)(2,1)S(1)}, u32[]{:S(2)}, u32[]{:S(2)}) async-start(bf16[8,216,96]{1,2,0:T(8,128)(2,1)} %copy.273), calls=%async_computation.1 | async-start | bytes 786432 | tf_op jit(solution)/shard_map/all_to_all | solution.py:78
  79.7 15.7 %all-to-all-start.3 = ((bf16[8,2,11568]{2,1,0:T(2,128)(2,1)}), bf16[8,2,11568]{2,1,0:T(2,128)(2,1)S(1)}, u32[]{:S(2)}, u32[]{:S(2)}) async-start(bf16[8,2,11568]{2,1,0:T(2,128)(2,1)} %reshape.379), calls=%async_computation.3 | async-start | bytes 745472 | tf_op jit(solution)/shard_map/all_to_all | solution.py:78
  85.5 0.8 copy-start.8

commit v2 on v1

v2 whole, which is shorter than its diff:
```python
import math

import jax
import jax.numpy as jnp
from jax import lax
from jax.experimental import pallas as pl
from jax.experimental.pallas import tpu as pltpu
from jax.sharding import PartitionSpec as P

eps_norm = 1e-06
root_half = 0.7071067811865476
inv_root_tau = 0.3989422804014327
served_kind = (1, 0, 3, 2, 1, 1, 0, 0)
opposite = (1, 0, 3, 2, 7, 6, 5, 4)
LANES = 128
F32 = jnp.float32
BF16 = jnp.bfloat16


def round_up(value, step):
    return -(-value // step) * step


def call(body, outs, operands, scalars=0, scratch=(), flops=0):
    spaces = [pltpu.SMEM] * scalars + [pltpu.VMEM] * (len(operands) - scalars)
    return pl.pallas_call(
        body,
        out_shape=outs,
        in_specs=[pl.BlockSpec(memory_space=space) for space in spaces],
        scratch_shapes=list(scratch),
        compiler_params=pltpu.CompilerParams(vmem_limit_bytes=48 << 20),
        cost_estimate=pl.CostEstimate(
            flops=flops,
            transcendentals=0,
            bytes_accessed=sum(o.size * o.dtype.itemsize for o in operands),
        ),
    )(*operands)


def shaped(shape, dtype):
    return jax.ShapeDtypeStruct(shape, dtype)


class Sizes:
    def __init__(self, tile_shape, hidden, owners):
        self.tiles, self.side, _, self.ch = tile_shape
        self.hidden = hidden
        self.owners = owners
        self.capacity = max(2, 8 * self.tiles // owners)
        self.pixels = self.side * self.side
        self.rows = self.pixels * self.tiles
        self.half = self.rows // 2
        self.extra = LANES - self.ch
        self.groups = self.ch // self.extra
        self.strip = 3 * self.side * self.ch // LANES
        self.tail = 3 * self.side - self.strip
        self.wide = self.side + 6
        self.box1 = round_up(self.capacity * self.strip, 16)
        self.weight_rows = 2 * (2 * self.ch) * hidden // LANES
        self.share = self.weight_rows // owners
        self.halo_at = round_up(self.share, 16)
        self.box2 = round_up(self.halo_at + self.capacity * self.strip, 16)
        self.taps_at = round_up(self.share, 16)
        self.box3 = round_up(self.taps_at + 49, 16)


def rank_links(z, neighbour, counts, ranks):
    @pl.loop(0, z.owners)
    def _(owner):
        counts[owner] = 0

    for tile in range(z.tiles):
        for side in range(8):
            target = neighbour[tile, side] // z.tiles
            rank = counts[target]
            counts[target] = rank + 1
            ranks[tile * 8 + side] = jnp.minimum(rank, z.capacity - 1)


def pack_strips(z, load_row, load_col, neighbour, ranks, strips, outbox, box, offset):
    direct = z.strip - 2 * z.side
    for tile in range(z.tiles):
        for kind in range(4):
            base = (tile * 4 + kind) * 32
            for line in range(3):
                place = z.side - 3 + line if kind in (0, 2) else line
                value = load_row(tile, place) if kind < 2 else load_col(tile, place)
                start = base + line * z.side
                if line < 2:
                    strips[start : start + z.side, 0 : z.ch] = value
                    continue
                strips[start : start + direct, 0 : z.ch] = value[0:direct]
                for group in range(z.groups):
                    low = base + group * z.tail
                    strips[low : low + z.tail, z.ch : LANES] = value[
                        direct:, group * z.extra : (group + 1) * z.extra
                    ]
    for tile in range(z.tiles):
        for side in range(8):
            link = neighbour[tile, side]
            target = link // z.tiles
            rank = ranks[(link - target * z.tiles) * 8 + opposite[side]]
            base = (tile * 4 + served_kind[side]) * 32
            outbox[pl.ds(target * box + offset + rank * z.strip, z.strip), :] = strips[
                base : base + z.strip, :
            ]


def assemble(z, inbox, box, offset, neighbour, tissue, ranks, flat, grown):
    pitch = z.wide * 8
    for tile in range(z.tiles):
        for side in range(8):
            target = neighbour[tile, side] // z.tiles
            rank = ranks[tile * 8 + side]
            value = inbox[pl.ds(target * box + offset + rank * z.strip, z.strip), :]
            value = jnp.where(tissue[tile, side] > 0, value, 0.0)
            base = (tile * 8 + side) * 40
            flat[base : base + z.strip, :] = value[:, 0 : z.ch]
            low = base + z.strip
            for group in range(z.groups):
                flat[low : low + z.tail, group * z.extra : (group + 1) * z.extra] = value[
                    group * z.tail : (group + 1) * z.tail, z.ch : LANES
                ]
    far = z.side + 3
    for tile in range(z.tiles):
        for side in range(8):
            base = (tile * 8 + side) * 40
            for line in range(3):
                start = base + line * z.side
                if side in (0, 1):
                    row = line if side == 0 else far + line
                    spot = pl.ds((row * z.wide + 3) * 8 + tile, z.side, stride=8)
                    grown[spot, :] = flat[start : start + z.side, :]
                elif side in (2, 3):
                    col = line if side == 2 else far + line
                    spot = pl.ds((3 * z.wide + col) * 8 + tile, z.side, stride=pitch)
                    grown[spot, :] = flat[start : start + z.side, :]
                else:
                    row = line if side in (4, 5) else far + line
                    col = 0 if side in (4, 6) else far
                    start += z.side - 3 if side in (4, 6) else 0
                    spot = pl.ds((row * z.wide + col) * 8 + tile, 3, stride=8)
                    grown[spot, :] = flat[start : start + 3, :]


def inner_spot(z, tile, row):
    return pl.ds(((row + 3) * z.wide + 3) * 8 + tile, z.side, stride=8)


def conv_row(z, grown, taps, row, start, flipped):
    line = z.wide * 8
    total = start
    for a in range(7):
        band = grown[pl.ds(pl.multiple_of((row + a) * line, 8), line), :]
        for b in range(7):
            tap = 48 - (a * 7 + b) if flipped else a * 7 + b
            total = total + band[b * 8 : (b + z.side) * 8] * taps[tap : tap + 1, :]
    return total


def tiny(z):
    return [pltpu.SMEM((z.owners,), jnp.int32), pltpu.SMEM((8 * z.tiles,), jnp.int32)]


def field(z):
    return pltpu.VMEM((z.wide * z.wide * 8, z.ch), F32)


def first_strips(z, neighbour, tile_data):
    def body(neighbour, tile_data, out, counts, ranks, plain, strips, box):
        rank_links(z, neighbour, counts, ranks)
        for tile in range(z.tiles):
            for row in range(z.side):
                at = (tile * z.side + row) * z.side
                plain[at : at + z.side, :] = tile_data[tile, row].astype(F32)

        def load_row(tile, row):
            return plain[pl.ds((tile * z.side + row) * z.side, z.side), :]

        def load_col(tile, col):
            return plain[pl.ds(tile * z.pixels + col, z.side, stride=z.side), :]

        pack_strips(z, load_row, load_col, neighbour, ranks, strips, box, z.box1, 0)
        out[...] = box[...].astype(BF16)

    rows = z.owners * z.box1
    return call(
        body,
        shaped((rows, LANES), BF16),
        [neighbour, tile_data],
        1,
        tiny(z)
        + [
            pltpu.VMEM((z.rows, z.ch), F32),
            pltpu.VMEM((z.tiles * 4 * 32, LANES), F32),
            pltpu.VMEM((rows, LANES), F32),
        ],
    )


def pixel_rows(z, tile_data, cotangent):
    def body(tile_data, cotangent, keep, send, work):
        core = lax.axis_index("sub")
        for which, block in enumerate((tile_data, cotangent)):
            for tile in range(z.tiles):
                for row in range(z.side):
                    spot = pl.ds(row * z.side * z.tiles + tile, z.side, stride=z.tiles)
                    work[spot, :] = block[tile, row].astype(F32)
            at = which * z.half
            own = pl.multiple_of(core * z.half, 16)
            far = pl.multiple_of((1 - core) * z.half, 16)
            keep[at : at + z.half, :] = work[pl.ds(own, z.half), :].astype(BF16)
            send[at : at + z.half, :] = work[pl.ds(far, z.half), :].astype(BF16)

    out = shaped((2 * z.half, z.ch), BF16)
    return call(
        body, (out, out), [tile_data, cotangent], 0, [pltpu.VMEM((z.rows, z.ch), F32)]
    )


def first_conv(z, neighbour, tissue, inbox, tile_data, taps, conv_bias):
    def body(neighbour, tissue, inbox, tile_data, taps, bias, own, far, counts, ranks, box, flat, grown):
        core = lax.axis_index("sub")
        rank_links(z, neighbour, counts, ranks)
        box[...] = inbox[...].astype(F32)
        assemble(z, box, z.box1, 0, neighbour, tissue, ranks, flat, grown)
        for tile in range(z.tiles):
            for row in range(z.side):
                grown[inner_spot(z, tile, row), :] = tile_data[tile, row].astype(F32)
        start = jnp.broadcast_to(bias[...], (z.side * 8, z.ch))
        half_side = z.side // 2

        def fill(out, first_row):
            @pl.loop(0, half_side)
            def _(step):
                total = conv_row(z, grown, taps, first_row + step, start, False)
                for col in range(z.side):
                    at = step * (z.side * z.tiles) + col * z.tiles
                    out[pl.ds(at, z.tiles), :] = total[col * 8 : col * 8 + z.tiles]

        fill(far, (1 - core) * half_side)
        fill(own, core * half_side)

    out = shaped((z.half, z.ch), F32)
    return call(
        body,
        (out, out),
        [neighbour, tissue, inbox, tile_data, taps, conv_bias],
        2,
        tiny(z)
        + [
            pltpu.VMEM((z.owners * z.box1, LANES), F32),
            pltpu.VMEM((z.tiles * 8 * 40, z.ch), F32),
            field(z),
        ],
    )


def block_pass(z, spatial, rows, w_in, w_out, vectors):
    hid = z.hidden
    wide = 2 * z.ch

    def body(sp_own, sp_far, row_own, row_far, wi_own, wi_far, wo_own, wo_far, v_own, v_far,
             g_own, block_own, keep, send, normed_s, branch_s, pre_s, gact_s, act_s, gpre_s,
             xhat_s, inv_s):
        first = lax.axis_index("sub") == 0

        def join(own, far):
            return jnp.where(
                first,
                jnp.concatenate([own, far], axis=1),
                jnp.concatenate([far, own], axis=1),
            )

        def vector(index):
            at = index * z.ch
            return join(v_own[:, at : at + z.ch], v_far[:, at : at + z.ch])

        gain, shift, b_out, layer_scale = [vector(index) for index in range(4)]
        flat = join(sp_own[...], sp_far[...])
        centre = flat - jnp.sum(flat, axis=1, keepdims=True) * (1.0 / wide)
        var = jnp.sum(centre * centre, axis=1, keepdims=True) * (1.0 / wide)
        inverse = lax.rsqrt(var + eps_norm)
        xhat = centre * inverse
        xhat_s[...] = xhat
        inv_s[...] = inverse
        normed_s[...] = (xhat * gain + shift).astype(BF16)
        cot = join(row_own[z.half :, :].astype(F32), row_far[z.half :, :].astype(F32))
        branch_s[...] = (layer_scale * cot).astype(BF16)
        normed = normed_s[...]
        g_branch = branch_s[...]
        across = (((1,), (1,)), ((), ()))
        down = (((0,), (0,)), ((), ()))
        for side, (wi, wo, vec) in enumerate(((wi_own, wo_own, v_own), (wi_far, wo_far, v_far))):
            at = side * hid
            b_in = vec[:, 4 * z.ch : 4 * z.ch + hid]
            pre_s[:, at : at + hid] = jnp.dot(normed, wi[...], preferred_element_type=F32) + b_in
            gact_s[:, at : at + hid] = lax.dot_general(
                g_branch, wo[...], across, preferred_element_type=F32
            )

        @pl.loop(0, z.half // 16)
        def _(step):
            spot = pl.ds(pl.multiple_of(step * 16, 16), 16)
            pre = pre_s[spot, :]
            cdf = 0.5 * (1.0 + lax.erf(pre * root_half))
            act_s[spot, :] = (pre * cdf).astype(BF16)
            slope = cdf + pre * jnp.exp(-0.5 * pre * pre) * inv_root_tau
            gpre_s[spot, :] = (gact_s[spot, :] * slope).astype(BF16)

        g_normed = lax.dot_general(
            gpre_s[:, 0:hid], wi_own[...], across, preferred_element_type=F32
        ) + lax.dot_general(gpre_s[:, hid:], wi_far[...], across, preferred_element_type=F32)
        xhat = xhat_s[...]
        leading = g_normed * gain
        mean_h = jnp.sum(leading, axis=1, keepdims=True) * (1.0 / wide)
        mean_hx = jnp.sum(leading * xhat, axis=1, keepdims=True) * (1.0 / wide)
        g_rows = inv_s[...] * (leading - mean_h - xhat * mean_hx)
        branch = (
            jnp.dot(act_s[:, 0:hid], wo_own[...], preferred_element_type=F32)
            + jnp.dot(act_s[:, hid:], wo_far[...], preferred_element_type=F32)
            + b_out
        )
        inner = join(row_own[0 : z.half, :].astype(F32), row_far[0 : z.half, :].astype(F32))
        block = inner + layer_scale * branch

        def part(value, mine):
            low, high = value[:, 0 : z.ch], value[:, z.ch :]
            return jnp.where(first == mine, low, high).astype(BF16)

        g_own[...] = part(g_rows, True)
        block_own[...] = part(block, True)
        send[0 : z.half, 0 : z.ch] = part(g_rows, False)
        send[z.half : 2 * z.half, 0 : z.ch] = part(block, False)
        for side in range(2):
            at = side * hid
            part_in = lax.dot_general(
                normed, gpre_s[:, at : at + hid], down, preferred_element_type=F32
            )
            part_out = lax.dot_general(
                act_s[:, at : at + hid], g_branch, down, preferred_element_type=F32
            )
            ref, base = (keep, 0) if side == 0 else (send, 2 * z.half)
            for group in range(hid // LANES):
                low = base + group * wide
                ref[low : low + wide, :] = part_in[
                    :, group * LANES : (group + 1) * LANES
                ].astype(ref.dtype)
            low = base + hid // LANES * wide
            ref[low : low + hid, :] = part_out[:, 0:LANES].astype(ref.dtype)
            low += hid
            ref[low : low + hid // 2, :] = jnp.concatenate(
                [part_out[0 : hid // 2, LANES:], part_out[hid // 2 :, LANES:]], axis=1
            ).astype(ref.dtype)

    rows_out = shaped((z.half, z.ch), BF16)
    return call(
        body,
        (
            rows_out,
            rows_out,
            shaped((z.weight_rows, LANES), F32),
            shaped((2 * z.half + z.weight_rows, LANES), BF16),
        ),
        [*spatial, *rows, *w_in, *w_out, *vectors],
        0,
        [
            pltpu.VMEM((z.half, wide), BF16),
            pltpu.VMEM((z.half, wide), BF16),
            pltpu.VMEM((z.half, 2 * hid), F32),
            pltpu.VMEM((z.half, 2 * hid), F32),
            pltpu.VMEM((z.half, 2 * hid), BF16),
            pltpu.VMEM((z.half, 2 * hid), BF16),
            pltpu.VMEM((z.half, wide), F32),
            pltpu.VMEM((z.half, 1), F32),
        ],
        flops=12 * z.half * wide * 2 * hid,
    )


def both_halves(z, work, own, far):
    core = lax.axis_index("sub")
    work[pl.ds(pl.multiple_of(core * z.half, 16), z.half), :] = own.astype(F32)
    work[pl.ds(pl.multiple_of((1 - core) * z.half, 16), z.half), :] = far.astype(F32)


def second_strips(z, neighbour, g_own, keep, received):
    def body(neighbour, g_own, keep, received, out, counts, ranks, plain, strips, box):
        rank_links(z, neighbour, counts, ranks)
        both_halves(z, plain, g_own[...], received[0 : z.half, 0 : z.ch])
        for owner in range(z.owners):
            at = owner * z.share
            low = 2 * z.half + at
            box[owner * z.box2 : owner * z.box2 + z.share, :] = keep[
                at : at + z.share, :
            ] + received[low : low + z.share, :].astype(F32)

        def load_row(tile, row):
            return plain[pl.ds(row * z.side * z.tiles + tile, z.side, stride=z.tiles), :]

        def load_col(tile, col):
            return plain[pl.ds(col * z.tiles + tile, z.side, stride=z.side * z.tiles), :]

        pack_strips(z, load_row, load_col, neighbour, ranks, strips, box, z.box2, z.halo_at)
        out[...] = box[...].astype(BF16)

    rows = z.owners * z.box2
    return call(
        body,
        shaped((rows, LANES), BF16),
        [neighbour, g_own, keep, received],
        1,
        tiny(z)
        + [
            pltpu.VMEM((z.rows, z.ch), F32),
            pltpu.VMEM((z.tiles * 4 * 32, LANES), F32),
            pltpu.VMEM((rows, LANES), F32),
        ],
    )


def filter_gradient(z, neighbour, tissue, inbox, tile_data, g_own, block_own, received):
    def body(neighbour, tissue, inbox, tile_data, g_own, block_own, received, taps, block_out,
             counts, ranks, box, flat, grown, plain, g_field, sums):
        rank_links(z, neighbour, counts, ranks)
        box[...] = inbox[...].astype(F32)
        assemble(z, box, z.box1, 0, neighbour, tissue, ranks, flat, grown)
        for tile in range(z.tiles):
            for row in range(z.side):
                grown[inner_spot(z, tile, row), :] = tile_data[tile, row].astype(F32)
        empty = jnp.zeros((z.wide * z.wide, z.ch), F32)
        for tile in range(z.tiles, 8):
            grown[pl.ds(tile, z.wide * z.wide, stride=8), :] = empty
        both_halves(z, plain, block_own[...], received[z.half : 2 * z.half, 0 : z.ch])
        for tile in range(z.tiles):
            for row in range(z.side):
                spot = pl.ds(row * z.side * z.tiles + tile, z.side, stride=z.tiles)
                block_out[tile, row] = plain[spot, :].astype(BF16)
        both_halves(z, plain, g_own[...], received[0 : z.half, 0 : z.ch])
        g_field[...] = jnp.zeros_like(g_field)
        for tile in range(z.tiles):
            g_field[pl.ds(tile, z.pixels, stride=8), :] = plain[
                pl.ds(tile, z.pixels, stride=z.tiles), :
            ]
        sums[...] = jnp.zeros_like(sums)
        line = z.wide * 8

        @pl.loop(0, z.side)
        def _(row):
            g_row = g_field[pl.ds(pl.multiple_of(row * z.side * 8, 8), z.side * 8), :]
            for a in range(7):
                band = grown[pl.ds(pl.multiple_of((row + a) * line, 8), line), :]
                for b in range(7):
                    product = band[b * 8 : (b + z.side) * 8] * g_row
                    total = product[0:8]
                    for col in range(1, z.side):
                        total = total + product[col * 8 : (col + 1) * 8]
                    at = (a * 7 + b) * 8
                    sums[at : at + 8, :] += total

        taps[...] = jnp.sum(sums[...].reshape(49, 8, z.ch), axis=1)

    return call(
        body,
        (shaped((49, z.ch), F32), shaped((z.tiles, z.side, z.side, z.ch), BF16)),
        [neighbour, tissue, inbox, tile_data, g_own, block_own, received],
        2,
        tiny(z)
        + [
            pltpu.VMEM((z.owners * z.box1, LANES), F32),
            pltpu.VMEM((z.tiles * 8 * 40, z.ch), F32),
            field(z),
            pltpu.VMEM((z.rows, z.ch), F32),
            pltpu.VMEM((z.pixels * 8, z.ch), F32),
            pltpu.VMEM((49 * 8, z.ch), F32),
        ],
    )


def sum_shares(z, inbox, taps):
    def body(inbox, taps, out):
        total = inbox[0 : z.share, :].astype(F32)
        for owner in range(1, z.owners):
            at = owner * z.box2
            total = total + inbox[at : at + z.share, :].astype(F32)
        share = total.astype(BF16)
        taps16 = taps[...].astype(BF16)
        for owner in range(z.owners):
            at = owner * z.box3
            out[at : at + z.share, :] = share
            at += z.taps_at
            out[at : at + 49, 0 : z.ch] = taps16

    return call(body, shaped((z.owners * z.box3, LANES), BF16), [inbox, taps])


def second_conv(z, neighbour, tissue, inbox, g_own, received, cotangent, taps):
    def body(neighbour, tissue, inbox, g_own, received, cotangent, taps, out,
             counts, ranks, box, flat, grown, plain, totals):
        rank_links(z, neighbour, counts, ranks)
        box[...] = inbox[...].astype(F32)
        assemble(z, box, z.box2, z.halo_at, neighbour, tissue, ranks, flat, grown)
        both_halves(z, plain, g_own[...], received[0 : z.half, 0 : z.ch])
        for tile in range(z.tiles):
            for row in range(z.side):
                spot = pl.ds(row * z.side * z.tiles + tile, z.side, stride=z.tiles)
                grown[inner_spot(z, tile, row), :] = plain[spot, :]
        start = jnp.zeros((z.side * 8, z.ch), F32)

        @pl.loop(0, z.side)
        def _(row):
            total = conv_row(z, grown, taps, row, start, True)
            totals[pl.ds(pl.multiple_of(row * z.side * 8, 8), z.side * 8), :] = total

        for tile in range(z.tiles):
            for row in range(z.side):
                spot = pl.ds(row * z.side * 8 + tile, z.side, stride=8)
                out[tile, row] = (totals[spot, :] + cotangent[tile, row].astype(F32)).astype(BF16)

    return call(
        body,
        shaped((z.tiles, z.side, z.side, z.ch), BF16),
        [neighbour, tissue, inbox, g_own, received, cotangent, taps],
        2,
        tiny(z)
        + [
            pltpu.VMEM((z.owners * z.box2, LANES), F32),
            pltpu.VMEM((z.tiles * 8 * 40, z.ch), F32),
            field(z),
            pltpu.VMEM((z.rows, z.ch), F32),
            pltpu.VMEM((z.pixels * 8, z.ch), F32),
        ],
    )


def finish(z, inbox, scale):
    hid = z.hidden
    wide = 2 * z.ch

    def body(inbox, grad_in, grad_out, grad_taps, work):
        total = jnp.zeros((49, z.ch), F32)
        for owner in range(z.owners):
            at = owner * z.box3
            work[owner * z.share : (owner + 1) * z.share, :] = (
                inbox[at : at + z.share, :].astype(F32) * scale
            )
            at += z.taps_at
            total = total + inbox[at : at + 49, 0 : z.ch].astype(F32)
        grad_taps[...] = total * scale
        for group in range(hid // LANES):
            low = group * wide
            grad_in[:, group * LANES : (group + 1) * LANES] = work[low : low + wide, :]
        low = hid // LANES * wide
        grad_out[:, 0:LANES] = work[low : low + hid, :]
        low += hid
        mid = hid // 2
        grad_out[0:mid, LANES:] = work[low : low + mid, 0 : wide - LANES]
        grad_out[mid:, LANES:] = work[low : low + mid, wide - LANES :]

    return call(
        body,
        (shaped((wide, hid), F32), shaped((hid, wide), F32), shaped((49, z.ch), F32)),
        [inbox],
        0,
        [pltpu.VMEM((z.weight_rows, LANES), F32)],
    )


def exchange_tiles(z, box):
    boxes = box.reshape(z.owners, -1, LANES)
    return lax.all_to_all(boxes, "tiles", split_axis=0, concat_axis=0, tiled=True).reshape(box.shape)


def swap_sub(piece):
    return lax.ppermute(piece, "sub", [(0, 1), (1, 0)])


def local(
    tile_data,
    cotangent,
    neighbour,
    tissue,
    kernel,
    conv_bias,
    layer_norm_gain,
    layer_norm_bias,
    w_in,
    b_in,
    w_out,
    b_out,
    layer_scale,
):
    z = Sizes(tile_data.shape, w_in.shape[1], lax.axis_size("tiles"))
    scale = 1.0 / math.sqrt(z.owners * z.rows)
    taps = kernel.reshape(49, z.ch)

    outbox = first_strips(z, neighbour, tile_data)
    inbox = exchange_tiles(z, outbox)

    w_in16 = w_in.astype(BF16)
    w_out16 = w_out.astype(BF16)
    vectors = jnp.concatenate([layer_norm_gain, layer_norm_bias, b_out, layer_scale, b_in])
    vectors = vectors.reshape(1, -1)
    rows_keep, rows_send = pixel_rows(z, tile_data, cotangent)

    sp_own, sp_far = first_conv(
        z, neighbour, tissue, inbox, tile_data, taps, conv_bias.reshape(1, z.ch)
    )
    g_own, block_own, keep, send = block_pass(
        z,
        (sp_own, swap_sub(sp_far)),
        (rows_keep, swap_sub(rows_send)),
        (w_in16, swap_sub(w_in16)),
        (w_out16, swap_sub(w_out16)),
        (vectors, swap_sub(vectors)),
    )
    received = swap_sub(send)
    inbox2 = exchange_tiles(z, second_strips(z, neighbour, g_own, keep, received))
    grad_taps, block_out = filter_gradient(
        z, neighbour, tissue, inbox, tile_data, g_own, block_own, received
    )
    inbox3 = exchange_tiles(z, sum_shares(z, inbox2, grad_taps))
    tile_grad = second_conv(z, neighbour, tissue, inbox2, g_own, received, cotangent, taps)
    grad_in, grad_out, grad_taps = finish(z, inbox3, scale)
    return block_out, tile_grad, grad_in, grad_out, grad_taps.reshape(kernel.shape)


def solution(mesh):
    placed = (
        P(("slides", "tiles"), None, None, "sub"),
        P(("slides", "tiles"), None, None, "sub"),
        P(("slides", "tiles"), None),
        P(("slides", "tiles"), None),
        P(None, None, "sub"),
        P("sub"),
        P("sub"),
        P("sub"),
        P(None, "sub"),
        P("sub"),
        P("sub", None),
        P("sub"),
        P("sub"),
    )
    return jax.shard_map(
        local,
        mesh=mesh,
        in_specs=placed,
        out_specs=(
            P(("slides", "tiles"), None, None, "sub"),
            P(("slides", "tiles"), None, None, "sub"),
            P("slides", "sub"),
            P(("slides", "sub"), None),
            P("slides", None, "sub"),
        ),
        check_vma=False,
    )
```

time: 99.5 us -> 79.8 us (0.80)
  Pallas kernels: 0 us -> 23.6 us
  local copies, waits for them, and re-layouts: 26.3 us -> 4.74 us
  matrix products: 15.4 us -> 0 us
  waiting for transfers between devices: 20.8 us -> 33.8 us
  other arithmetic: 12.9 us -> 0.02 us
  starting transfers between devices: 21.6 us -> 16.3 us
    pallas_call x0 -> x9, Pallas kernels: none -> 23.6 us  [call(): pl.pallas_call(body, out_shape=outs, in_specs=[pl.BlockSpec(memory_space=...]
    all_to_all x4 -> x3, waiting for transfers between devices: 19.6 us -> 31.4 us  [exchange_tiles(): lax.all_to_all(boxes, 'tiles', split_axis=0, concat_axis=0, tiled=True)]
    conv_general_dilated x3 -> x0, matrix products: 8.54 us -> none  [depthwise(): lax.conv_general_dilated(field, weights[:, :, None, :], (1, 1), 'VALID',...]
    dot_general x6 -> x0, matrix products: 6.82 us -> none  [the longest x1 1.74 us: local(): g_act = jnp.dot(g_branch, w_out_all.T, preferred_element_type=jnp.float32)]
    all_to_all x4 -> x3, starting transfers between devices: 19.3 us -> 14.6 us  [exchange_tiles(): lax.all_to_all(boxes, 'tiles', split_axis=0, concat_axis=0, tiled=True)]
    unnamed x55 -> x32, local copies, waits for them, and re-layouts: 8.15 us -> 4.04 us
    another operation x11 -> x0, local copies, waits for them, and re-layouts: 3.59 us -> none  [the longest x5 1.38 us: all_strips(): jnp.stack([edge_strip(block_data, kind_code) for kind_code in range(4)],...]
    reshape x23 -> x3, local copies, waits for them, and re-layouts: 3.77 us -> 0.62 us  [the longest x1 0.61 us: local(): grad_taps.reshape(kernel.shape)]
  transfers between devices with their start and end apart: 14 -> 9, of which waited for: 5 -> 5; matrix products, arithmetic and copies ran while one was open for 41% -> 0% of each run, Pallas kernels for 0% -> 17%
where the time goes in v2:
time: 79.8 us; the launch traced here: 79.2 us
  waiting for transfers between devices  33.8 us (42%)
  Pallas kernels  23.6 us (30%)
  starting transfers between devices  16.3 us (20%)
  local copies, waits for them, and re-layouts  4.74 us (6%)
  between operations  0.84 us (1%)
    all_to_all x3, waiting for transfers between devices, exchange_tiles(): lax.all_to_all(boxes, 'tiles', split_axis=0, concat_axis=0, tiled=True)  31.4 us
    pallas_call x9, Pallas kernels, call(): pl.pallas_call(body, out_shape=outs, in_specs=[pl.BlockSpec(memory_space=...  23.6 us
    all_to_all x3, starting transfers between devices, exchange_tiles(): lax.all_to_all(boxes, 'tiles', split_axis=0, concat_axis=0, tiled=True)  14.6 us
    unnamed x32, local copies, waits for them, and re-layouts  4.04 us
    ppermute x6, waiting for transfers between devices, swap_sub(): return lax.ppermute(piece, 'sub', [(0, 1), (1, 0)])  2.4 us
    ppermute x6, starting transfers between devices, swap_sub(): return lax.ppermute(piece, 'sub', [(0, 1), (1, 0)])  1.67 us
  transfers between devices with their start and end apart: 9, of which 5 were waited for; matrix products, arithmetic and copies ran while one was open for 0% of the time, Pallas kernels for 17%

profile of v2, /device:TPU:0, one launch (start us, length us, event | category | flops | bytes accessed | tf_op | source)
XLA Modules:
  0.0 79.2 jit_solution(9133190580746989509)
XLA Ops:
  0.6 0.0 copy-start
  0.6 1.0 %copy-done = bf16[6,12,12,96]{3,2,1,0:T(8,128)(2,1)S(1)} copy-done((bf16[6,12,12,96]{3,2,1,0:T(8,128)(2,1)S(1)}, bf16[6,12,12,96]{3,2,1,0:T(8,128)(2,1)}, u32[]{:S(2)}) %copy-start) | copy-done | bytes 165912
  1.6 0.0 copy-start.3
  1.6 0.7 copy-done.3
  2.3 2.2 %shard_map.164 = bf16[1408,128]{1,0:T(8,128)(2,1)} custom-call(s32[6,8]{1,0:T(8,128)S(1)} %copy-done.3, bf16[6,12,12,96]{3,2,1,0:T(8,128)(2,1)S(1)} %copy-done), custom_call_target="tpu_custom_call" | custom-call | bytes 166080 | tf_op jit(solution)/shard_map/pallas_call | solution.py:26
  4.4 0.0 copy-start.1
  4.4 0.0 copy-start.2
  4.4 7.4 %all-to-all-start = ((bf16[8,176,128]{2,1,0:T(8,128)(2,1)}), bf16[8,176,128]{2,1,0:T(8,128)(2,1)S(1)}, u32[]{:S(2)}, u32[]{:S(2)}) async-start(bf16[8,176,128]{2,1,0:T(8,128)(2,1)} %bitcast), calls=%async_computation | async-start | bytes 720896 | tf_op jit(solution)/shard_map/all_to_all | solution.py:571
  11.8 0.0 copy-done.1
  11.8 0.0 copy-done.2
  11.8 0.0 copy-start.9
  11.8 0.2 shard_map.166
  12.0 0.1 collective-permute-start.1
  12.1 0.5 copy-done.9
  12.6 0.0 copy-start.4
  12.6 0.0 copy-start.5
  12.6 10.2 %all-to-all-done = bf16[8,176,128]{2,1,0:T(8,128)(2,1)S(1)} async-done(((bf16[8,176,128]{2,1,0:T(8,128)(2,1)}), bf16[8,176,128]{2,1,0:T(8,128)(2,1)S(1)}, u32[]{:S(2)}, u32[]{:S(2)}) %all-to-all-start) | async-done | bytes 360480 | tf_op jit(solution)/shard_map/all_to_all | solution.py:571
  22.8 0.0 copy-start.6
  22.8 0.0 copy-done.4
  22.8 0.0 copy-done.5
  22.8 0.6 copy-done.6
  23.5 0.0 copy-start.7
  23.5 4.1 %shard_map.165 = (f32[432,96]{1,0:T(8,128)S(1)}, f32[432,96]{1,0:T(8,128)S(1)}) custom-call(s32[6,8]{1,0:T(8,128)S(1)} %copy-done.4, s32[6,8]{1,0:T(8,128)S(1)} %copy-done.5, bf16[1408,128]{1,0:T(8,128)(2,1)S(1)} %bitcast.9, bf16[6,12,12,96]{3,2,1,0:T(8,128)(2,1)S(1)} %copy-done.1, f32[49,96]{1,0:T(8,128)S(1)} %reshape.42.taps, f32[1,96]{1,0:T(1,128)S(1)} %bitcast.12), custom_call_target="tpu_custom_call" | custom-call | bytes 545920 | tf_op jit(solution)/shard_map/pallas_call | solution.py:26
  27.6 0.0 copy-start.8
  27.6 0.1 collective-permute-start
  27.7 0.0 copy-done.7
  27.7 0.0 copy-start.10
  27.7 0.0 copy-start.11
  27.7 0.0 copy-start.12
  27.7 0.0 copy-start.13
  27.7 0.0 copy-start.14
  27.8 0.5 collective-permute-start.2
  28.3 0.2 copy-done.8
  28.5 0.1 copy.18.wo_own
  28.7 0.1 collective-permute-start.3
  28.7 0.0 copy-done.10
  28.8 0.0 copy-done.11
  28.8 0.0 copy-done.12
  28.8 0.0 copy-done.13
  28.8 0.0 copy-done.14
  28.8 0.1 concatenate.3
  28.9 0.5 collective-permute-start.4
  29.4 0.8 %collective-permute-done.4.v_far = f32[1,768]{1,0:T(1,128)S(1)} collective-permute-done((f32[1,768]{1,0:T(1,128)S(1)}, f32[1,768]{1,0:T(1,128)S(1)}, u32[]{:S(2)}, u32[]{:S(2)}) %collective-permute-start.4) | collective-permute-done | bytes 3104 | tf_op jit(solution)/shard_map/ppermute | solution.py:575
  30.2 0.0 collective-permute-done.2.wi_far
  30.2 0.0 collective-permute-done.3.wo_far
  30.2 0.0 collective-permute-done.1.row_far
  30.2 0.0 collective-permute-done.sp_far
  30.2 3.9 %shard_map.167 = (bf16[432,96]{1,0:T(8,128)(2,1)S(1)}, bf16[432,96]{1,0:T(8,128)(2,1)S(1)}, f32[1152,128]{1,0:T(8,128)S(1)}, bf16[2016,128]{1,0:T(8,128)(2,1)S(1)}) custom-call(f32[432,96]{1,0:T(8,128)S(1)} %get-tuple-element.18.sp_own, f32[432,96]{1,0:T(8,128)S(1)} %collective-permute-done.sp_far, bf16[864,96]{1,0:T(8,128)(2,1)S(1)} %get-tuple-element.20.row_own, ...), custom_call_target="tpu_custom_call" | custom-call | flops 764411904 | bytes 1259520 | tf_op jit(solution)/shard_map/pallas_call | solution.py:26
  34.2 0.4 collective-permute-start.5
  34.6 1.6 %collective-permute-done.5.received = bf16[2016,128]{1,0:T(8,128)(2,1)S(1)} collective-permute-done((bf16[2016,128]{1,0:T(8,128)(2,1)S(1)}, bf16[2016,128]{1,0:T(8,128)(2,1)S(1)}, u32[]{:S(2)}, u32[]{:S(2)}) %collective-permute-start.5) | collective-permute-done | bytes 516128 | tf_op jit(solution)/shard_map/ppermute | solution.py:575
  36.1 2.3 %shard_map.169 = bf16[2560,128]{1,0:T(8,128)(2,1)} custom-call(s32[6,8]{1,0:T(8,128)S(1)} %copy-done.4, bf16[432,96]{1,0:T(8,128)(2,1)S(1)} %get-tuple-element.22.g_own, f32[1152,128]{1,0:T(8,128)S(1)} %get-tuple-element.26.keep, bf16[2016,128]{1,0:T(8,128)(2,1)S(1)} %collective-permute-done.5.received), custom_call_target="tpu_custom_call" | custom-call | bytes 1189056 | tf_op jit(solution)/shard_map/pallas_call | solution.py:26
  38.4 3.6 %all-to-all-start.1 = ((bf16[8,320,128]{2,1,0:T(8,128)(2,1)}), bf16[8,320,128]{2,1,0:T(8,128)(2,1)S(1)}, u32[]{:S(2)}, u32[]{:S(2)}) async-start(bf16[8,320,128]{2,1,0:T(8,128)(2,1)} %bitcast.3), calls=%async_computation.1 | async-start | bytes 1310720 | tf_op jit(solution)/shard_map/all_to_all | solution.py:571
  42.0 4.4 %shard_map.168 = (f32[49,96]{1,0:T(8,128)S(1)}, bf16[6,12,12,96]{3,2,1,0:T(8,128)(2,1)}) custom-call(s32[6,8]{1,0:T(8,128)S(1)} %copy-done.4, s32[6,8]{1,0:T(8,128)S(1)} %copy-done.5, bf16[1408,128]{1,0:T(8,128)(2,1)S(1)} %bitcast.10, bf16[6,12,12,96]{3,2,1,0:T(8,128)(2,1)S(1)} %copy-done.1, bf16[432,96]{1,0:T(8,128)(2,1)S(1)} %get-tuple-element.22.g_own, ...), custom_call_target="tpu_custom_call" | custom-call | bytes 1208704 | tf_op jit(solution)/shard_map/pallas_call | solution.py:26
  46.4 13.6 %all-to-all-done.1 = bf16[8,320,128]{2,1,0:T(8,128)(2,1)S(1)} async-done(((bf16[8,320,128]{2,1,0:T(8,128)(2,1)}), bf16[8,320,128]{2,1,0:T(8,128)(2,1)S(1)}, u32[]{:S(2)}, u32[]{:S(2)}) %all-to-all-start.1) | async-done | bytes 655392 | tf_op jit(solution)/shard_map/all_to_all | solution.py:571
  60.0 0.8 %shard_map.171 = bf16[1664,128]{1,0:T(8,128)(2,1)} custom-call(bf16[2560,128]{1,0:T(8,128)(2,1)S(1)} %bitcast.7, f32[49,96]{1,0:T(8,128)S(1)} %get-tuple-element.27.taps), custom_call_target="tpu_custom_call" | custom-call | bytes 674176 | tf_op jit(solution)/shard_map/pallas_call | solution.py:26
  60.8 3.6 %all-to-all-start.2 = ((bf16[8,208,128]{2,1,0:T(8,128)(2,1)}), bf16[8,208,128]{2,1,0:T(8,128)(2,1)S(1)}, u32[]{:S(2)}, u32[]{:S(2)}) async-start(bf16[8,208,128]{2,1,0:T(8,128)(2,1)} %bitcast.5), calls=%async_computation.2 | async-start | bytes 851968 | tf_op jit(solution)/shard_map/all_to_all | solution.py:571
  64.4 5.0 %shard_map.170 = bf16[6,12,12,96]{3,2,1,0:T(8,128)(2,1)} custom-call(s32[6,8]{1,0:T(8,128)S(1)} %copy-done.4, s32[6,8]{1,0:T(8,128)S(1)} %copy-done.5, bf16[2560,128]{1,0:T(8,128)(2,1)S(1)} %bitcast.8, bf16[432,96]{1,0:T(8,128)(2,1)S(1)} %get-tuple-element.22.g_own, bf16[2016,128]{1,0:T(8,128)(2,1)S(1)} %collective-permute-done.5.received, ...), custom_call_target="tpu_custom_call" | custom-call | bytes 1439488 | tf_op jit(solution)/shard_map/pallas_call | solution.py:26
  69.5 7.6 %all-to-all-done.2 = bf16[8,208,128]{2,1,0:T(8,128)(2,1)S(1)} async-done(((bf16[8,208,128]{2,1,0:T(8,128)(2,1)}), bf16[8,208,128]{2,1,0:T(8,128)(2,1)S(1)}, u32[]{:S(2)}, u32[]{:S(2)}) %all-to-all-start.2) | async-done | bytes 426016 | tf_op jit(solution)/shard_map/all_to_all | solution.py:571
  77.0 0.8 shard_map.172
  77.8 0.6 reshape.49
  78.4 0.9 %copy.19 = f32[384,192]{0,1:T(8,128)} copy(f32[384,192]{1,0:T(8,128)S(1)} %get-tuple-element.34) | data formatting | bytes 589824
  (3 shorter events, 0.0 us)
Async XLA Ops:
  0.6 1.0 %copy-start = (bf16[6,12,12,96]{3,2,1,0:T(8,128)(2,1)S(1)}, bf16[6,12,12,96]{3,2,1,0:T(8,128)(2,1)}, u32[]{:S(2)}) copy-start(bf16[6,12,12,96]{3,2,1,0:T(8,128)(2,1)} %tile_data.7) | copy-start | bytes 497668
  1.6 0.7 copy-start.3
  4.4 7.4 %copy-start.1 = (bf16[6,12,12,96]{3,2,1,0:T(8,128)(2,1)S(1)}, bf16[6,12,12,96]{3,2,1,0:T(8,128)(2,1)}, u32[]{:S(2)}) copy-start(bf16[6,12,12,96]{3,2,1,0:T(8,128)(2,1)} %tile_data.7) | copy-start | bytes 497668
  4.4 7.4 %copy-start.2 = (bf16[6,12,12,96]{3,2,1,0:T(8,128)(2,1)S(1)}, bf16[6,12,12,96]{3,2,1,0:T(8,128)(2,1)}, u32[]{:S(2)}) copy-start(bf16[6,12,12,96]{3,2,1,0:T(8,128)(2,1)} %cotangent.3) | copy-start | bytes 497668
  4.4 18.4 %all-to-all-start = ((bf16[8,176,128]{2,1,0:T(8,128)(2,1)}), bf16[8,176,128]{2,1,0:T(8,128)(2,1)S(1)}, u32[]{:S(2)}, u32[]{:S(2)}) async-start(bf16[8,176,128]{2,1,0:T(8,128)(2,1)} %bitcast), calls=%async_computation | async-start | bytes 720896 | tf_op jit(solution)/shard_map/all_to_all | solution.py:571
  11.8 0.8 copy-start.9
  12.0 18.2 %collective-permute-start.1 = (bf16[864,96]{1,0:T(8,128)(2,1)S(1)}, bf16[864,96]{1,0:T(8,128)(2,1)S(1)}, u32[]{:S(2)}, u32[]{:S(2)}) collective-permute-start(bf16[864,96]{1,0:T(8,128)(2,1)S(1)} %get-tuple-element.21), channel_id=1, source_target_pairs={{0,1},{1,0},{2,3},{3,2},{4,5},{5,4},{6,7},{7,6},{8,9},{9,8},{10,11... | collective-permute-start | bytes 497672 | tf_op jit(solution)/shard_map/ppermute | solution.py:575
  12.6 10.2 %copy-start.4 = (s32[6,8]{1,0:T(8,128)S(1)}, s32[6,8]{1,0:T(8,128)}, u32[]{:S(2)}) copy-start(s32[6,8]{1,0:T(8,128)} %neighbour.9) | copy-start | bytes 580
  12.6 10.2 %copy-start.5 = (s32[6,8]{1,0:T(8,128)S(1)}, s32[6,8]{1,0:T(8,128)}, u32[]{:S(2)}) copy-start(s32[6,8]{1,0:T(8,128)} %tissue.5) | copy-start | bytes 580
  22.8 0.7 copy-start.6
  23.5 4.2 %copy-start.7 = (f32[192,384]{1,0:T(8,128)S(1)}, f32[192,384]{1,0:T(8,128)}, u32[]{:S(2)}) copy-start(f32[192,384]{1,0:T(8,128)} %param.21) | copy-start | bytes 884740
  27.6 1.0 %copy-start.8 = (f32[384,192]{0,1:T(8,128)S(1)}, f32[384,192]{0,1:T(8,128)}, u32[]{:S(2)}) copy-start(f32[384,192]{0,1:T(8,128)} %param.23) | copy-start | bytes 884740
  27.6 2.7 %collective-permute-start = (f32[432,96]{1,0:T(8,128)S(1)}, f32[432,96]{1,0:T(8,128)S(1)}, u32[]{:S(2)}, u32[]{:S(2)}) collective-permute-start(f32[432,96]{1,0:T(8,128)S(1)} %get-tuple-element.19), channel_id=1, source_target_pairs={{0,1},{1,0},{2,3},{3,2},{4,5},{5,4},{6,7},{7,6},{8,9},{9,8},{10,11... | collective-permute-start | bytes 497672 | tf_op jit(solution)/shard_map/ppermute | solution.py:575
  27.7 1.1 %copy-start.10 = (f32[384]{0:T(512)S(1)}, f32[384]{0:T(512)}, u32[]{:S(2)}) copy-start(f32[384]{0:T(512)} %param.22) | copy-start | bytes 4612
  27.7 1.1 %copy-start.11 = (f32[96]{0:T(128)S(1)}, f32[96]{0:T(128)}, u32[]{:S(2)}) copy-start(f32[96]{0:T(128)} %param.19) | copy-start | bytes 1156
  27.7 1.1 %copy-start.12 = (f32[96]{0:T(128)S(1)}, f32[96]{0:T(128)}, u32[]{:S(2)}) copy-start(f32[96]{0:T(128)} %param.20) | copy-start | bytes 1156
  27.7 1.0 %copy-start.13 = (f32[96]{0:T(128)S(1)}, f32[96]{0:T(128)}, u32[]{:S(2)}) copy-start(f32[96]{0:T(128)} %param.24) | copy-start | bytes 1156
  27.7 1.0 %copy-start.14 = (f32[96]{0:T(128)S(1)}, f32[96]{0:T(128)}, u32[]{:S(2)}) copy-start(f32[96]{0:T(128)} %param.25) | copy-start | bytes 1156
  27.8 2.5 %collective-permute-start.2 = (bf16[192,384]{1,0:T(8,128)(2,1)S(1)}, bf16[192,384]{1,0:T(8,128)(2,1)S(1)}, u32[]{:S(2)}, u32[]{:S(2)}) collective-permute-start(bf16[192,384]{1,0:T(8,128)(2,1)S(1)} %convert_element_type.6.wi_own), channel_id=1, source_target_pairs={{0,1},{1,0},{2,3},{3,2},{4,5},{5,4},{6,7},{7,6},{8,9},{9,8},{10,11... | collective-permute-start | bytes 442376 | tf_op jit(solution)/shard_map/ppermute | solution.py:575
  28.7 1.6 %collective-permute-start.3 = (bf16[384,192]{1,0:T(8,128)(2,1)S(1)}, bf16[384,192]{1,0:T(8,128)(2,1)S(1)}, u32[]{:S(2)}, u32[]{:S(2)}) collective-permute-start(bf16[384,192]{1,0:T(8,128)(2,1)S(1)} %copy.18.wo_own), channel_id=1, source_target_pairs={{0,1},{1,0},{2,3},{3,2},{4,5},{5,4},{6,7},{7,6},{8,9},{9,8},{10,11... | collective-permute-start | bytes 442376 | tf_op jit(solution)/shard_map/ppermute | solution.py:575
  28.9 1.3 %collective-permute-start.4 = (f32[1,768]{1,0:T(1,128)S(1)}, f32[1,768]{1,0:T(1,128)S(1)}, u32[]{:S(2)}, u32[]{:S(2)}) collective-permute-start(f32[1,768]{1,0:T(1,128)S(1)} %reshape.44.v_own), channel_id=1, source_target_pairs={{0,1},{1,0},{2,3},{3,2},{4,5},{5,4},{6,7},{7,6},{8,9},{9,8},{10,11... | collective-permute-start | bytes 9224 | tf_op jit(solution)/shard_map/ppermute | solution.py:575
  34.2 2.0 %collective-permute-start.5 = (bf16[2016,128]{1,0:T(8,128)(2,1)S(1)}, bf16[2016,128]{1,0:T(8,128)(2,1)S(1)}, u32[]{:S(2)}, u32[]{:S(2)}) collective-permute-start(bf16[2016,128]{1,0:T(8,128)(2,1)S(1)} %get-tuple-element.24), channel_id=1, source_target_pairs={{0,1},{1,0},{2,3},{3,2},{4,5},{5,4},{6,7},{7,6},{8,9},{9,8},{10,11... | collective-permute-start | bytes 1548296 | tf_op jit(solution)/shard_map/ppermute | solution.py:575
  38.4 21.6 %all-to-all-start.1 = ((bf16[8,320,128]{2,1,0:T(8,128)(2,1)}), bf16[8,320,128]{2,1,0:T(8,128)(2,1)S(1)}, u32[]{:S(2)}, u32[]{:S(2)}) async-start(bf16[8,320,128]{2,1,0:T(8,128)(2,1)} %bitcast.3), calls=%async_computation.1 | async-start | bytes 1310720 | tf_op jit(solution)/shard_map/all_to_all | solution.py:571
  60.8 16.2 %all-to-all-start.2 = ((bf16[8,208,128]{2,1,0:T(8,128)(2,1)}), bf16[8,208,128]{2,1,0:T(8,128)(2,1)S(1)}, u32[]{:S(2)}, u32[]{:S(2)}) async-start(bf16[8,208,128]{2,1,0:T(8,128)(2,1)} %bitcast.5), calls=%async_computation.2 | async-start | bytes 851968 | tf_op jit(solution)/shard_map/all_to_all | solution.py:571

commit v3 on v2

v3 whole, which is shorter than its diff:
```python
import math

import jax
import jax.numpy as jnp
from jax import lax
from jax.experimental import pallas as pl
from jax.experimental.pallas import tpu as pltpu
from jax.sharding import PartitionSpec as P

eps_norm = 1e-06
root_half = 0.7071067811865476
inv_root_tau = 0.3989422804014327
served_kind = (1, 0, 3, 2, 1, 1, 0, 0)
opposite = (1, 0, 3, 2, 7, 6, 5, 4)
LANES = 128
FIRST_VMEM = 60
F32 = jnp.float32
BF16 = jnp.bfloat16


def round_up(value, step):
    return -(-value // step) * step


def call(body, outs, operands, scalars=0, scratch=(), flops=0, vmem=16, after=(), **specs):
    spaces = specs.pop("spaces", None)
    if spaces is None:
        spaces = [pltpu.SMEM] * scalars + [pltpu.VMEM] * (len(operands) - scalars)
    count = len(operands)
    stop = count + len(after)

    def run(*refs):
        body(*refs[:count], *refs[stop:])

    return pl.pallas_call(
        run,
        out_shape=outs,
        in_specs=[pl.BlockSpec(memory_space=space) for space in [*spaces, *[pl.ANY] * len(after)]],
        scratch_shapes=list(scratch),
        compiler_params=pltpu.CompilerParams(vmem_limit_bytes=vmem << 20),
        cost_estimate=pl.CostEstimate(
            flops=flops,
            transcendentals=0,
            bytes_accessed=sum(o.size * o.dtype.itemsize for o in operands),
        ),
        **specs,
    )(*operands, *after)


def shaped(shape, dtype):
    return jax.ShapeDtypeStruct(shape, dtype)


class Sizes:
    def __init__(self, tile_shape, hidden, owners):
        self.tiles, self.side, _, self.ch = tile_shape
        self.hidden = hidden
        self.owners = owners
        self.capacity = max(2, 8 * self.tiles // owners)
        self.links = 8 * self.tiles
        self.pixels = self.side * self.side
        self.rows = self.pixels * self.tiles
        self.half = self.rows // 2
        self.extra = LANES - self.ch
        self.groups = self.ch // self.extra
        self.strip = 3 * self.side * self.ch // LANES
        self.tail = 3 * self.side - self.strip
        self.far = self.side + 3
        self.wide = self.side + 6
        self.box1 = round_up(self.capacity * self.strip, 8)
        self.weight_rows = 2 * (2 * self.ch) * hidden // LANES
        self.share = self.weight_rows // owners
        self.halo_at = round_up(self.share, 8)
        self.box2 = round_up(self.halo_at + self.capacity * self.strip, 8)
        self.box3 = round_up(self.share, 8)

    def owner_of(self, link):
        factor = -(-65536 // self.tiles)
        assert self.owners * self.tiles * (factor * self.tiles - 65536) < 65536
        return (link * factor) >> 16


def rank_links(z, neighbour, counts, slots):
    @pl.loop(0, z.owners)
    def _(owner):
        counts[owner] = 0

    for link in range(z.links):
        owner = z.owner_of(neighbour[link // 8, link % 8])
        rank = counts[owner]
        counts[owner] = rank + 1
        slots[link] = owner
        slots[z.links + link] = jnp.minimum(rank, z.capacity - 1)
    for link in range(z.links):
        slot = neighbour[link // 8, link % 8] - slots[link] * z.tiles
        slots[2 * z.links + link] = slots[z.links + slot * 8 + opposite[link % 8]]


def pack_strips(z, load_row, load_col, slots, strips, outbox, box, offset):
    direct = z.strip - 2 * z.side
    for tile in range(z.tiles):
        for kind in range(4):
            base = (tile * 4 + kind) * 32
            for line in range(3):
                place = z.side - 3 + line if kind in (0, 2) else line
                value = load_row(tile, place) if kind < 2 else load_col(tile, place)
                start = base + line * z.side
                if line < 2:
                    strips[start : start + z.side, 0 : z.ch] = value
                    continue
                strips[start : start + direct, 0 : z.ch] = value[0:direct]
                for group in range(z.groups):
                    low = base + group * z.tail
                    strips[low : low + z.tail, z.ch : LANES] = value[
                        direct:, group * z.extra : (group + 1) * z.extra
                    ]
    for link in range(z.links):
        base = (link // 8 * 4 + served_kind[link % 8]) * 32
        low = slots[link] * box + offset + slots[2 * z.links + link] * z.strip
        outbox[pl.ds(low, z.strip), :] = strips[base : base + z.strip, :]


def assemble(z, inbox, box, offset, slots, tissue, flat, grown):
    pitch = z.wide * 8
    for link in range(z.links):
        low = slots[link] * box + offset + slots[z.links + link] * z.strip
        value = inbox[pl.ds(low, z.strip), :]
        value = jnp.where(tissue[link // 8, link % 8] > 0, value, 0.0)
        base = link * 40
        flat[base : base + z.strip, :] = value[:, 0 : z.ch]
        low = base + z.strip
        for group in range(z.groups):
            flat[low : low + z.tail, group * z.extra : (group + 1) * z.extra] = value[
                group * z.tail : (group + 1) * z.tail, z.ch : LANES
            ]
    far = z.far
    for tile in range(z.tiles):
        for side in range(8):
            base = (tile * 8 + side) * 40
            for line in range(3):
                start = base + line * z.side
                if side in (0, 1):
                    row = line if side == 0 else far + line
                    spot = pl.ds((row * z.wide + 3) * 8 + tile, z.side, stride=8)
                    grown[spot, :] = flat[start : start + z.side, :]
                elif side in (2, 3):
                    col = line if side == 2 else far + line
                    spot = pl.ds((3 * z.wide + col) * 8 + tile, z.side, stride=pitch)
                    grown[spot, :] = flat[start : start + z.side, :]
                else:
                    row = line if side in (4, 5) else far + line
                    col = 0 if side in (4, 6) else far
                    start += z.side - 3 if side in (4, 6) else 0
                    spot = pl.ds((row * z.wide + col) * 8 + tile, 3, stride=8)
                    grown[spot, :] = flat[start : start + 3, :]


def inner_spot(z, tile, row):
    return pl.ds(((row + 3) * z.wide + 3) * 8 + tile, z.side, stride=8)


def fill_inner(z, grown, tile_data):
    for tile in range(z.tiles):
        for row in range(z.side):
            grown[inner_spot(z, tile, row), :] = tile_data[tile, row].astype(F32)


def conv_row(z, grown, taps, row, start, flipped):
    line = z.wide * 8
    total = start
    for a in range(7):
        band = grown[pl.ds(pl.multiple_of((row + a) * line, 8), line), :]
        for b in range(7):
            tap = taps[6 - a, 6 - b : 7 - b, :] if flipped else taps[a, b : b + 1, :]
            total = total + band[b * 8 : (b + z.side) * 8] * tap
    return total


def rim_row(z, grown, taps, row, start):
    total = start
    inner = []
    for a in range(7):
        at = (row + a) * z.wide * 8
        if 3 <= row + a < z.far:
            inner.append((a, at))
            continue
        for b in range(7):
            low = at + b * 8
            total = total + grown[low : low + z.side * 8, :] * taps[a, b : b + 1, :]
    pieces = [total[col * 8 : (col + 1) * 8] for col in range(z.side)]
    for a, at in inner:
        for col in range(z.side):
            for b in range(7):
                if col + b < 3 or col + b >= z.far:
                    low = at + (col + b) * 8
                    pieces[col] = pieces[col] + grown[low : low + 8, :] * taps[a, b : b + 1, :]
    return pieces


def field(z):
    return pltpu.VMEM((z.wide * z.wide * 8, z.ch), F32)


def boxes(z, box):
    return pltpu.VMEM((z.owners * box, LANES), F32)


def flat_strips(z):
    return pltpu.VMEM((z.links * 40, z.ch), F32)


def packed_strips(z):
    return pltpu.VMEM((z.tiles * 4 * 32, LANES), F32)


def pixel_major(z):
    return pltpu.VMEM((z.rows, z.ch), F32)


def first_strips(z, neighbour, tile_data):
    def body(neighbour_hbm, tile_hbm, out, slots, neighbour, tile_data, sems, counts, plain, strips, box):
        fetch_links = pltpu.make_async_copy(neighbour_hbm, neighbour, sems.at[0])
        fetch_tiles = pltpu.make_async_copy(tile_hbm, tile_data, sems.at[1])
        fetch_links.start()
        fetch_tiles.start()
        fetch_links.wait()
        rank_links(z, neighbour, counts, slots)
        fetch_tiles.wait()
        for tile in range(z.tiles):
            for row in range(z.side):
                at = (tile * z.side + row) * z.side
                plain[at : at + z.side, :] = tile_data[tile, row].astype(F32)

        def load_row(tile, row):
            return plain[pl.ds((tile * z.side + row) * z.side, z.side), :]

        def load_col(tile, col):
            return plain[pl.ds(tile * z.pixels + col, z.side, stride=z.side), :]

        pack_strips(z, load_row, load_col, slots, strips, box, z.box1, 0)
        out[...] = box[...].astype(BF16)

    rows = z.owners * z.box1
    return call(
        body,
        (shaped((rows, LANES), BF16), shaped((3 * z.links,), jnp.int32)),
        [neighbour, tile_data],
        spaces=[pl.ANY, pl.ANY],
        vmem=FIRST_VMEM,
        out_specs=(
            pl.BlockSpec(memory_space=pltpu.VMEM),
            pl.BlockSpec(memory_space=pltpu.SMEM),
        ),
        scratch=[
            pltpu.SMEM(neighbour.shape, jnp.int32),
            pltpu.VMEM(tile_data.shape, BF16),
            pltpu.SemaphoreType.DMA((2,)),
            pltpu.SMEM((z.owners,), jnp.int32),
            pixel_major(z),
            packed_strips(z),
            boxes(z, z.box1),
        ],
    )


def local_part(z, tile_data, cotangent, taps, conv_bias):
    def body(tile_data, cotangent, taps, bias, keep, send, out, work, grown):
        core = lax.axis_index("sub")
        for which, block in enumerate((tile_data, cotangent)):
            for tile in range(z.tiles):
                for row in range(z.side):
                    spot = pl.ds(row * z.side * z.tiles + tile, z.side, stride=z.tiles)
                    work[spot, :] = block[tile, row].astype(F32)
            at = which * z.half
            own = pl.multiple_of(core * z.half, 16)
            far = pl.multiple_of((1 - core) * z.half, 16)
            keep[at : at + z.half, :] = work[pl.ds(own, z.half), :].astype(BF16)
            send[at : at + z.half, :] = work[pl.ds(far, z.half), :].astype(BF16)
        grown[...] = jnp.zeros_like(grown)
        fill_inner(z, grown, tile_data)
        start = jnp.broadcast_to(bias[...], (z.side * 8, z.ch))

        @pl.loop(0, z.side)
        def _(row):
            total = conv_row(z, grown, taps, row, start, False)
            out[pl.ds(pl.multiple_of(row * z.side * 8, 8), z.side * 8), :] = total

    rows = shaped((2 * z.half, z.ch), BF16)
    return call(
        body,
        (rows, rows, shaped((z.pixels * 8, z.ch), F32)),
        [tile_data, cotangent, taps, conv_bias],
        scratch=[pixel_major(z), field(z)],
        flops=2 * 49 * z.rows * z.ch,
    )


def rim_conv(z, slots, tissue, inbox, inner, taps, after):
    def body(slots, tissue, inbox, inner, taps, own, far, box, flat, grown, whole):
        core = lax.axis_index("sub")
        box[...] = inbox[...].astype(F32)
        assemble(z, box, z.box1, 0, slots, tissue, flat, grown)
        for row in range(z.side):
            start = inner[row * z.side * 8 : (row + 1) * z.side * 8, :]
            for col, piece in enumerate(rim_row(z, grown, taps, row, start)):
                at = (row * z.side + col) * z.tiles
                whole[at : at + z.tiles, :] = piece[0 : z.tiles]
        own[...] = whole[pl.ds(pl.multiple_of(core * z.half, 8), z.half), :]
        far[...] = whole[pl.ds(pl.multiple_of((1 - core) * z.half, 8), z.half), :]

    out = shaped((z.half, z.ch), F32)
    return call(
        body,
        (out, out),
        [slots, tissue, inbox, inner, taps],
        2,
        [boxes(z, z.box1), flat_strips(z), field(z), pixel_major(z)],
        after=after,
    )


ACROSS = (((1,), (1,)), ((), ()))
DOWN = (((0,), (0,)), ((), ()))


def join(first, own, far):
    return jnp.where(
        first, jnp.concatenate([own, far], axis=1), jnp.concatenate([far, own], axis=1)
    )


def both_vectors(z, first, v_own, v_far, index):
    at = index * z.ch
    return join(first, v_own[:, at : at + z.ch], v_far[:, at : at + z.ch])


def block_pass(z, spatial, rows, w_in, w_out, vectors):
    hid = z.hidden
    wide = 2 * z.ch

    def body(sp_own, sp_far, row_own, row_far, wi_own, wi_far, wo_own, wo_far, v_own,
             v_far, g_own, block_own, block_far, keep, send, normed_s, branch_s, pre_s, gact_s, act_s, gpre_s, xhat_s, inv_s):
        first = lax.axis_index("sub") == 0
        gain, shift, b_out, layer_scale = [
            both_vectors(z, first, v_own, v_far, index) for index in range(4)
        ]
        flat = join(first, sp_own[...], sp_far[...])
        centre = flat - jnp.sum(flat, axis=1, keepdims=True) * (1.0 / wide)
        var = jnp.sum(centre * centre, axis=1, keepdims=True) * (1.0 / wide)
        inverse = lax.rsqrt(var + eps_norm)
        xhat = centre * inverse
        xhat_s[...] = xhat
        inv_s[...] = inverse
        normed_s[...] = (xhat * gain + shift).astype(BF16)
        normed = normed_s[...]
        cot = join(first, row_own[z.half :, :].astype(F32), row_far[z.half :, :].astype(F32))
        branch_s[...] = (layer_scale * cot).astype(BF16)
        g_branch = branch_s[...]
        for side, (wi, wo, vec) in enumerate(((wi_own, wo_own, v_own), (wi_far, wo_far, v_far))):
            at = side * hid
            b_in = vec[:, 4 * z.ch : 4 * z.ch + hid]
            pre_s[:, at : at + hid] = jnp.dot(normed, wi[...], preferred_element_type=F32) + b_in
            gact_s[:, at : at + hid] = jnp.dot(g_branch, wo[...], preferred_element_type=F32)

        @pl.loop(0, z.half // 16)
        def _(step):
            spot = pl.ds(pl.multiple_of(step * 16, 16), 16)
            pre = pre_s[spot, :]
            cdf = 0.5 * (1.0 + lax.erf(pre * root_half))
            act_s[spot, :] = (pre * cdf).astype(BF16)
            slope = cdf + pre * jnp.exp(-0.5 * pre * pre) * inv_root_tau
            gpre_s[spot, :] = (gact_s[spot, :] * slope).astype(BF16)

        g_normed = lax.dot_general(
            gpre_s[:, 0:hid], wi_own[...], ACROSS, preferred_element_type=F32
        ) + lax.dot_general(gpre_s[:, hid:], wi_far[...], ACROSS, preferred_element_type=F32)
        xhat = xhat_s[...]
        leading = g_normed * gain
        mean_h = jnp.sum(leading, axis=1, keepdims=True) * (1.0 / wide)
        mean_hx = jnp.sum(leading * xhat, axis=1, keepdims=True) * (1.0 / wide)
        g_rows = inv_s[...] * (leading - mean_h - xhat * mean_hx)
        branch = (
            lax.dot_general(act_s[:, 0:hid], wo_own[...], ACROSS, preferred_element_type=F32)
            + lax.dot_general(act_s[:, hid:], wo_far[...], ACROSS, preferred_element_type=F32)
            + b_out
        )
        inner = join(
            first, row_own[0 : z.half, :].astype(F32), row_far[0 : z.half, :].astype(F32)
        )
        block = inner + layer_scale * branch

        def part(value, mine):
            low, high = value[:, 0 : z.ch], value[:, z.ch :]
            return jnp.where(first == mine, low, high).astype(BF16)

        g_own[...] = part(g_rows, True)
        block_own[...] = part(block, True)
        send[0 : z.half, 0 : z.ch] = part(g_rows, False)
        block_far[...] = part(block, False)
        for side in range(2):
            at = side * hid
            ref, low = (keep, 0) if side == 0 else (send, z.half)
            for left, right in ((normed, gpre_s), (g_branch, act_s)):
                grad = lax.dot_general(
                    left, right[:, at : at + hid], DOWN, preferred_element_type=F32
                )
                for group in range(hid // LANES):
                    lanes = slice(group * LANES, (group + 1) * LANES)
                    ref[low : low + wide, :] = grad[:, lanes].astype(ref.dtype)
                    low += wide

    rows_out = shaped((z.half, z.ch), BF16)
    return call(
        body,
        (
            rows_out,
            rows_out,
            rows_out,
            shaped((z.weight_rows, LANES), F32),
            shaped((z.half + z.weight_rows, LANES), BF16),
        ),
        [*spatial, *rows, *w_in, *w_out, *vectors],
        0,
        [
            pltpu.VMEM((z.half, wide), BF16),
            pltpu.VMEM((z.half, wide), BF16),
            pltpu.VMEM((z.half, 2 * hid), F32),
            pltpu.VMEM((z.half, 2 * hid), F32),
            pltpu.VMEM((z.half, 2 * hid), BF16),
            pltpu.VMEM((z.half, 2 * hid), BF16),
            pltpu.VMEM((z.half, wide), F32),
            pltpu.VMEM((z.half, 1), F32),
        ],
        flops=12 * z.half * wide * 2 * hid,
    )


def both_halves(z, work, own, far):
    core = lax.axis_index("sub")
    work[pl.ds(pl.multiple_of(core * z.half, 16), z.half), :] = own.astype(F32)
    work[pl.ds(pl.multiple_of((1 - core) * z.half, 16), z.half), :] = far.astype(F32)


def second_strips(z, slots, g_own, keep, received):
    def body(slots, g_own, keep, received, out, plain, strips, box):
        both_halves(z, plain, g_own[...], received[0 : z.half, 0 : z.ch])
        for owner in range(z.owners):
            at = owner * z.share
            low = z.half + at
            box[owner * z.box2 : owner * z.box2 + z.share, :] = keep[
                at : at + z.share, :
            ] + received[low : low + z.share, :].astype(F32)

        def load_row(tile, row):
            return plain[pl.ds(row * z.side * z.tiles + tile, z.side, stride=z.tiles), :]

        def load_col(tile, col):
            return plain[pl.ds(col * z.tiles + tile, z.side, stride=z.side * z.tiles), :]

        pack_strips(z, load_row, load_col, slots, strips, box, z.box2, z.halo_at)
        out[...] = box[...].astype(BF16)

    return call(
        body,
        shaped((z.owners * z.box2, LANES), BF16),
        [slots, g_own, keep, received],
        1,
        [pixel_major(z), packed_strips(z), boxes(z, z.box2)],
    )


def filter_gradient(z, slots, tissue, inbox, tile_data, g_own, received, scale):
    def body(slots, tissue, inbox, tile_data, g_own, received, taps, box, flat, grown, plain,
             g_field, sums):
        box[...] = inbox[...].astype(F32)
        assemble(z, box, z.box1, 0, slots, tissue, flat, grown)
        fill_inner(z, grown, tile_data)
        empty = jnp.zeros((z.wide * z.wide, z.ch), F32)
        for tile in range(z.tiles, 8):
            grown[pl.ds(tile, z.wide * z.wide, stride=8), :] = empty
        both_halves(z, plain, g_own[...], received[0 : z.half, 0 : z.ch])
        g_field[...] = jnp.zeros_like(g_field)
        for tile in range(z.tiles):
            g_field[pl.ds(tile, z.pixels, stride=8), :] = plain[
                pl.ds(tile, z.pixels, stride=z.tiles), :
            ]
        sums[...] = jnp.zeros_like(sums)
        line = z.wide * 8

        @pl.loop(0, z.side)
        def _(row):
            g_row = g_field[pl.ds(pl.multiple_of(row * z.side * 8, 8), z.side * 8), :]
            for a in range(7):
                band = grown[pl.ds(pl.multiple_of((row + a) * line, 8), line), :]
                for b in range(7):
                    product = band[b * 8 : (b + z.side) * 8] * g_row
                    total = product[0:8]
                    for col in range(1, z.side):
                        total = total + product[col * 8 : (col + 1) * 8]
                    at = (a * 7 + b) * 8
                    sums[at : at + 8, :] += total

        for a in range(7):
            rows = sums[a * 56 : (a + 1) * 56, :].reshape(7, 8, z.ch)
            taps[a] = jnp.sum(rows, axis=1) * scale

    return call(
        body,
        shaped((7, 7, z.ch), F32),
        [slots, tissue, inbox, tile_data, g_own, received],
        2,
        [
            boxes(z, z.box1),
            flat_strips(z),
            field(z),
            pixel_major(z),
            pltpu.VMEM((z.pixels * 8, z.ch), F32),
            pltpu.VMEM((49 * 8, z.ch), F32),
        ],
        flops=2 * 49 * z.rows * z.ch,
    )


def sum_shares(z, inbox, after):
    def body(inbox, out):
        total = inbox[0 : z.share, :].astype(F32)
        for owner in range(1, z.owners):
            at = owner * z.box2
            total = total + inbox[at : at + z.share, :].astype(F32)
        share = total.astype(BF16)
        for owner in range(z.owners):
            at = owner * z.box3
            out[at : at + z.share, :] = share

    return call(body, shaped((z.owners * z.box3, LANES), BF16), [inbox], after=after)


def second_conv(z, slots, tissue, inbox, g_own, received, block, cotangent, taps):
    def body(slots, tissue, inbox, g_own, received, block_own, block_far, cotangent, taps, out,
             block_out, box, flat, grown, plain, totals):
        box[...] = inbox[...].astype(F32)
        assemble(z, box, z.box2, z.halo_at, slots, tissue, flat, grown)
        both_halves(z, plain, g_own[...], received[0 : z.half, 0 : z.ch])
        for tile in range(z.tiles):
            for row in range(z.side):
                spot = pl.ds(row * z.side * z.tiles + tile, z.side, stride=z.tiles)
                grown[inner_spot(z, tile, row), :] = plain[spot, :]
        start = jnp.zeros((z.side * 8, z.ch), F32)

        @pl.loop(0, z.side)
        def _(row):
            total = conv_row(z, grown, taps, row, start, True)
            totals[pl.ds(pl.multiple_of(row * z.side * 8, 8), z.side * 8), :] = total

        for tile in range(z.tiles):
            for row in range(z.side):
                spot = pl.ds(row * z.side * 8 + tile, z.side, stride=8)
                out[tile, row] = (totals[spot, :] + cotangent[tile, row].astype(F32)).astype(BF16)

        both_halves(z, plain, block_own[...], block_far[...])
        for tile in range(z.tiles):
            for row in range(z.side):
                spot = pl.ds(row * z.side * z.tiles + tile, z.side, stride=z.tiles)
                block_out[tile, row] = plain[spot, :].astype(BF16)

    out = shaped((z.tiles, z.side, z.side, z.ch), BF16)
    return call(
        body,
        (out, out),
        [slots, tissue, inbox, g_own, received, *block, cotangent, taps],
        2,
        [
            boxes(z, z.box2),
            flat_strips(z),
            field(z),
            pixel_major(z),
            pltpu.VMEM((z.pixels * 8, z.ch), F32),
        ],
        flops=2 * 49 * z.rows * z.ch,
    )


def finish(z, inbox, taps, scale):
    hid = z.hidden
    wide = 2 * z.ch
    groups = hid // LANES

    def body(inbox, taps_own, taps_far, grad_in, grad_out, grad_taps):
        grad_taps[...] = taps_own[...] + taps_far[...]
        for owner in range(z.owners):
            row = owner * z.share
            stop = row + z.share
            while row < stop:
                group, place = divmod(row, wide)
                count = min(stop - row, wide - place)
                at = owner * z.box3 + row - owner * z.share
                out = grad_in if group < groups else grad_out
                low = group % groups * LANES
                out[place : place + count, low : low + LANES] = (
                    inbox[at : at + count, :].astype(F32) * scale
                )
                row += count

    out = shaped((wide, hid), F32)
    return call(body, (out, out, shaped((7, 7, z.ch), F32)), [inbox, *taps])


def exchange_tiles(z, box):
    boxes = box.reshape(z.owners, -1, LANES)
    return lax.all_to_all(boxes, "tiles", split_axis=0, concat_axis=0, tiled=True).reshape(box.shape)


def swap_sub(piece):
    return lax.ppermute(piece, "sub", [(0, 1), (1, 0)])


def sum_tiles(z, part):
    step = 1
    while True:
        pairs = [(owner, owner ^ step) for owner in range(z.owners)]
        other = lax.ppermute(part, "tiles", pairs)
        step *= 2
        if step == z.owners:
            return part, other
        part = part + other


def local(
    tile_data,
    cotangent,
    neighbour,
    tissue,
    kernel,
    conv_bias,
    layer_norm_gain,
    layer_norm_bias,
    w_in,
    b_in,
    w_out,
    b_out,
    layer_scale,
):
    z = Sizes(tile_data.shape, w_in.shape[1], lax.axis_size("tiles"))
    scale = 1.0 / math.sqrt(z.owners * z.rows)

    outbox, slots = first_strips(z, neighbour, tile_data)
    inbox = exchange_tiles(z, outbox)

    w_in16 = w_in.astype(BF16)
    w_out16 = w_out.T.astype(BF16)
    vectors = jnp.concatenate([layer_norm_gain, layer_norm_bias, b_out, layer_scale, b_in])
    vectors = vectors.reshape(1, -1)
    rows_keep, rows_send, inner = local_part(
        z, tile_data, cotangent, kernel, conv_bias.reshape(1, z.ch)
    )
    w_in_both = (w_in16, swap_sub(w_in16))
    w_out_both = (w_out16, swap_sub(w_out16))
    v_both = (vectors, swap_sub(vectors))
    rows_both = (rows_keep, swap_sub(rows_send))
    ready = (rows_both[1], w_in_both[1], w_out_both[1], v_both[1])
    sp_own, sp_far = rim_conv(z, slots, tissue, inbox, inner, kernel, ready)
    g_own, block_own, block_far, keep, send = block_pass(
        z, (sp_own, swap_sub(sp_far)), rows_both, w_in_both, w_out_both, v_both
    )
    received = swap_sub(send)
    inbox2 = exchange_tiles(z, second_strips(z, slots, g_own, keep, received))
    taps = filter_gradient(z, slots, tissue, inbox, tile_data, g_own, received, scale)
    taps_own, taps_far = sum_tiles(z, taps)
    inbox3 = exchange_tiles(z, sum_shares(z, inbox2, (taps_own,)))
    tile_grad, block_out = second_conv(
        z, slots, tissue, inbox2, g_own, received, (block_own, swap_sub(block_far)), cotangent, kernel
    )
    grad_in, grad_out, grad_kernel = finish(z, inbox3, (taps_own, taps_far), scale)
    return block_out, tile_grad, grad_in, grad_out.T, grad_kernel


def solution(mesh):
    placed = (
        P(("slides", "tiles"), None, None, "sub"),
        P(("slides", "tiles"), None, None, "sub"),
        P(("slides", "tiles"), None),
        P(("slides", "tiles"), None),
        P(None, None, "sub"),
        P("sub"),
        P("sub"),
        P("sub"),
        P(None, "sub"),
        P("sub"),
        P("sub", None),
        P("sub"),
        P("sub"),
    )
    return jax.shard_map(
        local,
        mesh=mesh,
        in_specs=placed,
        out_specs=(
            P(("slides", "tiles"), None, None, "sub"),
            P(("slides", "tiles"), None, None, "sub"),
            P("slides", "sub"),
            P(("slides", "sub"), None),
            P("slides", None, "sub"),
        ),
        check_vma=False,
    )
```

time: 79.8 us -> 70.5 us (0.88)
  waiting for transfers between devices: 33.8 us -> 22.2 us
  starting transfers between devices: 16.3 us -> 22.1 us
  local copies, waits for them, and re-layouts: 4.74 us -> 1.67 us
    all_to_all x3, waiting for transfers between devices: 31.4 us -> 9.29 us  [exchange_tiles(): lax.all_to_all(boxes, 'tiles', split_axis=0, concat_axis=0, tiled=True)]
    ppermute x0 -> x3, waiting for transfers between devices: none -> 9.05 us  [sum_tiles(): other = lax.ppermute(part, 'tiles', pairs)]
    ppermute x0 -> x3, starting transfers between devices: none -> 6.04 us  [sum_tiles(): other = lax.ppermute(part, 'tiles', pairs)]
    unnamed x32 -> x26, local copies, waits for them, and re-layouts: 4.04 us -> 1.59 us
    ppermute x6 -> x7, waiting for transfers between devices: 2.4 us -> 3.91 us  [swap_sub(): return lax.ppermute(piece, 'sub', [(0, 1), (1, 0)])]
    ppermute x6 -> x7, starting transfers between devices: 1.67 us -> 1.49 us  [swap_sub(): return lax.ppermute(piece, 'sub', [(0, 1), (1, 0)])]
  transfers between devices with their start and end apart: 9 -> 13, of which waited for: 5 -> 8; matrix products, arithmetic and copies ran while one was open for 0% -> 0% of each run, Pallas kernels for 17% -> 16%
where the time goes in v3:
time: 70.5 us; the launch traced here: 70 us
  Pallas kernels  23.1 us (33%)
  waiting for transfers between devices  22.2 us (31%)
  starting transfers between devices  22.1 us (31%)
  local copies, waits for them, and re-layouts  1.67 us (2%)
  between operations  0.86 us (1%)
    pallas_call x9, Pallas kernels, call(): pl.pallas_call(run, out_shape=outs, in_specs=[pl.BlockSpec(memory_space=s...  23.1 us
    all_to_all x3, starting transfers between devices, exchange_tiles(): lax.all_to_all(boxes, 'tiles', split_axis=0, concat_axis=0, tiled=True)  14.6 us
    all_to_all x3, waiting for transfers between devices, exchange_tiles(): lax.all_to_all(boxes, 'tiles', split_axis=0, concat_axis=0, tiled=True)  9.29 us
    ppermute x3, waiting for transfers between devices, sum_tiles(): other = lax.ppermute(part, 'tiles', pairs)  9.05 us
    ppermute x3, starting transfers between devices, sum_tiles(): other = lax.ppermute(part, 'tiles', pairs)  6.04 us
    ppermute x7, waiting for transfers between devices, swap_sub(): return lax.ppermute(piece, 'sub', [(0, 1), (1, 0)])  3.91 us
    unnamed x26, local copies, waits for them, and re-layouts  1.59 us
    ppermute x7, starting transfers between devices, swap_sub(): return lax.ppermute(piece, 'sub', [(0, 1), (1, 0)])  1.49 us
  transfers between devices with their start and end apart: 13, of which 8 were waited for; matrix products, arithmetic and copies ran while one was open for 0% of the time, Pallas kernels for 16%

profile of v3, /device:TPU:0, one launch (start us, length us, event | category | flops | bytes accessed | tf_op | source)
XLA Modules:
  0.0 70.0 jit_solution(16439184139682321029)
XLA Ops:
  0.6 2.2 %shard_map.164 = (bf16[1344,128]{1,0:T(8,128)(2,1)}, s32[144]{0:T(256)}) custom-call(s32[6,8]{1,0:T(8,128)} %refs_0_.2, bf16[6,12,12,96]{3,2,1,0:T(8,128)(2,1)} %refs_3_.1), custom_call_target="tpu_custom_call" | custom-call | bytes 166080 | tf_op jit(solution)/shard_map/pallas_call | solution.py:35
  2.9 0.0 copy-start
  2.9 0.0 copy-start.1
  2.9 0.0 copy-start.2
  2.9 7.4 %all-to-all-start = ((bf16[8,168,128]{2,1,0:T(8,128)(2,1)}), bf16[8,168,128]{2,1,0:T(8,128)(2,1)S(1)}, u32[]{:S(2)}, u32[]{:S(2)}) async-start(bf16[8,168,128]{2,1,0:T(8,128)(2,1)} %bitcast.16), calls=%async_computation | async-start | bytes 688128 | tf_op jit(solution)/shard_map/all_to_all | solution.py:610
  10.3 0.0 copy-start.5
  10.3 0.0 copy-done
  10.3 0.0 copy-done.1
  10.3 0.0 copy-done.2
  10.4 0.6 copy-done.5
  11.0 0.0 copy-start.6
  11.0 3.0 %shard_map.165 = (bf16[864,96]{1,0:T(8,128)(2,1)S(1)}, bf16[864,96]{1,0:T(8,128)(2,1)S(1)}, f32[1152,96]{1,0:T(8,128)S(1)}) custom-call(bf16[6,12,12,96]{3,2,1,0:T(8,128)(2,1)S(1)} %copy-done, bf16[6,12,12,96]{3,2,1,0:T(8,128)(2,1)S(1)} %copy-done.1, f32[7,7,96]{2,1,0:T(8,128)S(1)} %copy-done.2, f32[1,96]{1,0:T(1,128)S(1)} %bitcast.15), custom_call_target="tpu_custom_call" | custom-call | flops 8128512 | bytes 350976 | tf_op jit(solution)/shard_map/pallas_call | solution.py:35
  14.0 0.0 copy-start.7
  14.0 0.1 collective-permute-start
  14.1 0.0 copy-done.6
  14.1 0.0 copy-start.8
  14.2 0.0 copy-start.9
  14.2 0.0 copy-start.10
  14.2 0.0 copy-start.11
  14.2 0.0 copy-start.12
  14.2 0.5 collective-permute-start.2
  14.8 0.2 copy-done.7
  15.0 0.1 collective-permute-start.1
  15.1 0.0 copy-done.8
  15.1 0.0 copy-done.9
  15.1 0.0 copy-done.10
  15.1 0.0 copy-done.11
  15.1 0.0 copy-done.12
  15.1 0.1 concatenate.3
  15.2 0.0 copy-start.3
  15.2 0.5 collective-permute-start.3
  15.8 0.8 %collective-permute-done.3.refs_8_.refs_9_ = f32[1,768]{1,0:T(1,128)S(1)} collective-permute-done((f32[1,768]{1,0:T(1,128)S(1)}, f32[1,768]{1,0:T(1,128)S(1)}, u32[]{:S(2)}, u32[]{:S(2)}) %collective-permute-start.3) | collective-permute-done | bytes 3104 | tf_op jit(solution)/shard_map/ppermute | solution.py:614
  16.6 0.0 collective-permute-done.2.refs_7_
  16.6 0.0 collective-permute-done.1.refs_6_.refs_5_
  16.6 0.0 collective-permute-done.refs_5_.refs_3_
  16.6 4.4 %all-to-all-done = bf16[8,168,128]{2,1,0:T(8,128)(2,1)S(1)} async-done(((bf16[8,168,128]{2,1,0:T(8,128)(2,1)}), bf16[8,168,128]{2,1,0:T(8,128)(2,1)S(1)}, u32[]{:S(2)}, u32[]{:S(2)}) %all-to-all-start) | async-done | bytes 344096 | tf_op jit(solution)/shard_map/all_to_all | solution.py:610
  21.0 0.0 copy-start.4
  21.0 0.0 copy-done.3
  21.0 0.7 copy-done.4
  21.7 1.7 %shard_map.166 = (f32[432,96]{1,0:T(8,128)S(1)}, f32[432,96]{1,0:T(8,128)S(1)}) custom-call(s32[144]{0:T(256)S(1)} %copy-done.4, s32[6,8]{1,0:T(8,128)S(1)} %copy-done.3, bf16[1344,128]{1,0:T(8,128)(2,1)S(1)} %bitcast.12, f32[1152,96]{1,0:T(8,128)S(1)} %get-tuple-element.24.refs_3_, f32[7,7,96]{2,1,0:T(8,128)S(1)} %copy-done.2, ...), custom_call_target="tpu_custom_call" | custom-call | bytes 806016 | tf_op jit(solution)/shard_map/pallas_call | solution.py:35
  23.3 0.1 collective-permute-start.4
  23.4 1.5 %collective-permute-done.4.refs_1_ = f32[432,96]{1,0:T(8,128)S(1)} collective-permute-done((f32[432,96]{1,0:T(8,128)S(1)}, f32[432,96]{1,0:T(8,128)S(1)}, u32[]{:S(2)}, u32[]{:S(2)}) %collective-permute-start.4) | collective-permute-done | bytes 165920 | tf_op jit(solution)/shard_map/ppermute | solution.py:614
  24.9 4.3 %shard_map.167 = (bf16[432,96]{1,0:T(8,128)(2,1)S(1)}, bf16[432,96]{1,0:T(8,128)(2,1)S(1)}, bf16[432,96]{1,0:T(8,128)(2,1)S(1)}, f32[1152,128]{1,0:T(8,128)S(1)}, bf16[1584,128]{1,0:T(8,128)(2,1)S(1)}) custom-call(f32[432,96]{1,0:T(8,128)S(1)} %get-tuple-element.26.refs_0_, f32[432,96]{1,0:T(8,128)S(1)} %collective-permute-done.4.refs_1_, ...), custom_call_target="tpu_custom_call" | custom-call | flops 764411904 | bytes 1259520 | tf_op jit(solution)/shard_map/pallas_call | solution.py:35
  29.2 0.2 collective-permute-start.5
  29.4 1.6 %collective-permute-done.5.refs_3_.refs_4_.refs_5_ = bf16[1584,128]{1,0:T(8,128)(2,1)S(1)} collective-permute-done((bf16[1584,128]{1,0:T(8,128)(2,1)S(1)}, bf16[1584,128]{1,0:T(8,128)(2,1)S(1)}, u32[]{:S(2)}, u32[]{:S(2)}) %collective-permute-start.5) | collective-permute-done | bytes 405536 | tf_op jit(solution)/shard_map/ppermute | solution.py:614
  31.0 1.8 %shard_map.168 = bf16[2496,128]{1,0:T(8,128)(2,1)} custom-call(s32[144]{0:T(256)S(1)} %copy-done.4, bf16[432,96]{1,0:T(8,128)(2,1)S(1)} %get-tuple-element.29.refs_1_.refs_3_.refs_4_, f32[1152,128]{1,0:T(8,128)S(1)} %get-tuple-element.30.refs_2_, bf16[1584,128]{1,0:T(8,128)(2,1)S(1)} %collective-permute-done.5.refs_3_.refs_4_.refs_5_), custom_call_target="tpu_custom_call" | custom-call | bytes 1078848 | tf_op jit(solution)/shard_map/pallas_call | solution.py:35
  32.8 3.6 %all-to-all-start.1 = ((bf16[8,312,128]{2,1,0:T(8,128)(2,1)}), bf16[8,312,128]{2,1,0:T(8,128)(2,1)S(1)}, u32[]{:S(2)}, u32[]{:S(2)}) async-start(bf16[8,312,128]{2,1,0:T(8,128)(2,1)} %bitcast.4), calls=%async_computation.1 | async-start | bytes 1277952 | tf_op jit(solution)/shard_map/all_to_all | solution.py:610
  36.4 3.5 %shard_map.170 = f32[7,7,96]{2,1,0:T(8,128)S(1)} custom-call(s32[144]{0:T(256)S(1)} %copy-done.4, s32[6,8]{1,0:T(8,128)S(1)} %copy-done.3, bf16[1344,128]{1,0:T(8,128)(2,1)S(1)} %bitcast.13, bf16[6,12,12,96]{3,2,1,0:T(8,128)(2,1)S(1)} %copy-done, bf16[432,96]{1,0:T(8,128)(2,1)S(1)} %get-tuple-element.29.refs_1_.refs_3_.refs_4_, ...), custom_call_target="tpu_custom_call" | custom-call | flops 8128512 | bytes 999168 | tf_op jit(solution)/shard_map/pallas_call | solution.py:35
  39.9 2.1 %collective-permute-start.7 = (f32[7,7,96]{2,1,0:T(8,128)S(1)}, f32[7,7,96]{2,1,0:T(8,128)S(1)}, u32[]{:S(2)}, u32[]{:S(2)}) collective-permute-start(f32[7,7,96]{2,1,0:T(8,128)S(1)} %shard_map.170), channel_id=1, source_target_pairs={{0,2},{2,0},{4,6},{6,4},{8,10},{10,8},{12,14},{14,12},{1,3},{3,1},... | collective-permute-start | bytes 56456 | tf_op jit(solution)/shard_map/ppermute | solution.py:621
  42.0 2.8 %collective-permute-done.7 = f32[7,7,96]{2,1,0:T(8,128)S(1)} collective-permute-done((f32[7,7,96]{2,1,0:T(8,128)S(1)}, f32[7,7,96]{2,1,0:T(8,128)S(1)}, u32[]{:S(2)}, u32[]{:S(2)}) %collective-permute-start.7) | collective-permute-done | bytes 18848 | tf_op jit(solution)/shard_map/ppermute | solution.py:621
  44.8 1.0 %collective-permute-start.8 = (f32[7,7,96]{2,1,0:T(8,128)S(1)}, f32[7,7,96]{2,1,0:T(8,128)S(1)}, u32[]{:S(2)}, u32[]{:S(2)}) collective-permute-start(f32[7,7,96]{2,1,0:T(8,128)S(1)} %add.6), channel_id=1, source_target_pairs={{0,4},{2,6},{4,0},{6,2},{8,12},{10,14},{12,8},{14,10},{1,5},{3,7},... | collective-permute-start | bytes 56456 | tf_op jit(solution)/shard_map/ppermute | solution.py:621
  45.9 3.0 %collective-permute-done.8 = f32[7,7,96]{2,1,0:T(8,128)S(1)} collective-permute-done((f32[7,7,96]{2,1,0:T(8,128)S(1)}, f32[7,7,96]{2,1,0:T(8,128)S(1)}, u32[]{:S(2)}, u32[]{:S(2)}) %collective-permute-start.8) | collective-permute-done | bytes 18848 | tf_op jit(solution)/shard_map/ppermute | solution.py:621
  48.9 4.9 %all-to-all-done.1 = bf16[8,312,128]{2,1,0:T(8,128)(2,1)S(1)} async-done(((bf16[8,312,128]{2,1,0:T(8,128)(2,1)}), bf16[8,312,128]{2,1,0:T(8,128)(2,1)S(1)}, u32[]{:S(2)}, u32[]{:S(2)}) %all-to-all-start.1) | async-done | bytes 639008 | tf_op jit(solution)/shard_map/all_to_all | solution.py:610
  53.8 0.8 %shard_map.171 = bf16[1152,128]{1,0:T(8,128)(2,1)} custom-call(bf16[2496,128]{1,0:T(8,128)(2,1)S(1)} %bitcast.10, f32[7,7,96]{2,1,0:T(8,128)S(1)} %add.7.refs_1_), custom_call_target="tpu_custom_call" | custom-call | bytes 638976 | tf_op jit(solution)/shard_map/pallas_call | solution.py:35
  54.6 3.6 %all-to-all-start.2 = ((bf16[8,144,128]{2,1,0:T(8,128)(2,1)}), bf16[8,144,128]{2,1,0:T(8,128)(2,1)S(1)}, u32[]{:S(2)}, u32[]{:S(2)}) async-start(bf16[8,144,128]{2,1,0:T(8,128)(2,1)} %bitcast.6), calls=%async_computation.2 | async-start | bytes 589824 | tf_op jit(solution)/shard_map/all_to_all | solution.py:610
  58.2 0.0 collective-permute-start.6
  58.2 2.9 %collective-permute-start.9 = (f32[7,7,96]{2,1,0:T(8,128)S(1)}, f32[7,7,96]{2,1,0:T(8,128)S(1)}, u32[]{:S(2)}, u32[]{:S(2)}) collective-permute-start(f32[7,7,96]{2,1,0:T(8,128)S(1)} %add.7.refs_1_), channel_id=1, source_target_pairs={{0,8},{2,10},{4,12},{6,14},{8,0},{10,2},{12,4},{14,6},{1,9},{3,11}... | collective-permute-start | bytes 56456 | tf_op jit(solution)/shard_map/ppermute | solution.py:621
  61.1 0.0 collective-permute-done.6.refs_6_
  61.1 4.9 %shard_map.169 = (bf16[6,12,12,96]{3,2,1,0:T(8,128)(2,1)}, bf16[6,12,12,96]{3,2,1,0:T(8,128)(2,1)}) custom-call(s32[144]{0:T(256)S(1)} %copy-done.4, s32[6,8]{1,0:T(8,128)S(1)} %copy-done.3, bf16[2496,128]{1,0:T(8,128)(2,1)S(1)} %bitcast.11, bf16[432,96]{1,0:T(8,128)(2,1)S(1)} %get-tuple-element.29.refs_1_.refs_3_.refs_4_, ...), custom_call_target="tpu_custom_call" | custom-call | flops 8128512 | bytes 1478784 | tf_op jit(solution)/shard_map/pallas_call | solution.py:35
  66.0 3.2 %collective-permute-done.9.refs_2_ = f32[7,7,96]{2,1,0:T(8,128)S(1)} collective-permute-done((f32[7,7,96]{2,1,0:T(8,128)S(1)}, f32[7,7,96]{2,1,0:T(8,128)S(1)}, u32[]{:S(2)}, u32[]{:S(2)}) %collective-permute-start.9) | collective-permute-done | bytes 18848 | tf_op jit(solution)/shard_map/ppermute | solution.py:621
  69.2 0.0 all-to-all-done.2
  69.2 0.9 %shard_map.172 = (f32[192,384]{1,0:T(8,128)}, f32[192,384]{1,0:T(8,128)}, f32[7,7,96]{2,1,0:T(8,128)}) custom-call(bf16[1152,128]{1,0:T(8,128)(2,1)S(1)} %bitcast.14, f32[7,7,96]{2,1,0:T(8,128)S(1)} %add.7.refs_1_, f32[7,7,96]{2,1,0:T(8,128)S(1)} %collective-permute-done.9.refs_2_), custom_call_target="tpu_custom_call" | custom-call | bytes 332544 | tf_op jit(solution)/shard_map/pallas_call | solution.py:35
  (5 shorter events, 0.1 us)
Async XLA Ops:
  2.9 7.4 %copy-start = (bf16[6,12,12,96]{3,2,1,0:T(8,128)(2,1)S(1)}, bf16[6,12,12,96]{3,2,1,0:T(8,128)(2,1)}, u32[]{:S(2)}) copy-start(bf16[6,12,12,96]{3,2,1,0:T(8,128)(2,1)} %refs_3_.1) | copy-start | bytes 497668
  2.9 7.4 %copy-start.1 = (bf16[6,12,12,96]{3,2,1,0:T(8,128)(2,1)S(1)}, bf16[6,12,12,96]{3,2,1,0:T(8,128)(2,1)}, u32[]{:S(2)}) copy-start(bf16[6,12,12,96]{3,2,1,0:T(8,128)(2,1)} %refs_7_.1) | copy-start | bytes 497668
  2.9 7.4 %copy-start.2 = (f32[7,7,96]{2,1,0:T(8,128)S(1)}, f32[7,7,96]{2,1,0:T(8,128)}, u32[]{:S(2)}) copy-start(f32[7,7,96]{2,1,0:T(8,128)} %refs_8_.1) | copy-start | bytes 56452
  2.9 18.1 %all-to-all-start = ((bf16[8,168,128]{2,1,0:T(8,128)(2,1)}), bf16[8,168,128]{2,1,0:T(8,128)(2,1)S(1)}, u32[]{:S(2)}, u32[]{:S(2)}) async-start(bf16[8,168,128]{2,1,0:T(8,128)(2,1)} %bitcast.16), calls=%async_computation | async-start | bytes 688128 | tf_op jit(solution)/shard_map/all_to_all | solution.py:610
  10.3 0.7 copy-start.5
  11.0 3.1 %copy-start.6 = (f32[384,192]{0,1:T(8,128)S(1)}, f32[384,192]{0,1:T(8,128)}, u32[]{:S(2)}) copy-start(f32[384,192]{0,1:T(8,128)} %param.23) | copy-start | bytes 884740
  14.0 1.0 %copy-start.7 = (f32[192,384]{1,0:T(8,128)S(1)}, f32[192,384]{1,0:T(8,128)}, u32[]{:S(2)}) copy-start(f32[192,384]{1,0:T(8,128)} %param.21) | copy-start | bytes 884740
  14.0 2.6 %collective-permute-start = (bf16[864,96]{1,0:T(8,128)(2,1)S(1)}, bf16[864,96]{1,0:T(8,128)(2,1)S(1)}, u32[]{:S(2)}, u32[]{:S(2)}) collective-permute-start(bf16[864,96]{1,0:T(8,128)(2,1)S(1)} %get-tuple-element.25), channel_id=1, source_target_pairs={{0,1},{1,0},{2,3},{3,2},{4,5},{5,4},{6,7},{7,6},{8,9},{9,8},{10,11... | collective-permute-start | bytes 497672 | tf_op jit(solution)/shard_map/ppermute | solution.py:614
  14.1 0.9 %copy-start.8 = (f32[384]{0:T(512)S(1)}, f32[384]{0:T(512)}, u32[]{:S(2)}) copy-start(f32[384]{0:T(512)} %param.22) | copy-start | bytes 4612
  14.2 0.9 %copy-start.9 = (f32[96]{0:T(128)S(1)}, f32[96]{0:T(128)}, u32[]{:S(2)}) copy-start(f32[96]{0:T(128)} %param.19) | copy-start | bytes 1156
  14.2 0.9 %copy-start.10 = (f32[96]{0:T(128)S(1)}, f32[96]{0:T(128)}, u32[]{:S(2)}) copy-start(f32[96]{0:T(128)} %param.20) | copy-start | bytes 1156
  14.2 0.9 %copy-start.11 = (f32[96]{0:T(128)S(1)}, f32[96]{0:T(128)}, u32[]{:S(2)}) copy-start(f32[96]{0:T(128)} %param.24) | copy-start | bytes 1156
  14.2 0.9 %copy-start.12 = (f32[96]{0:T(128)S(1)}, f32[96]{0:T(128)}, u32[]{:S(2)}) copy-start(f32[96]{0:T(128)} %param.25) | copy-start | bytes 1156
  14.2 2.4 %collective-permute-start.2 = (bf16[192,384]{1,0:T(8,128)(2,1)S(1)}, bf16[192,384]{1,0:T(8,128)(2,1)S(1)}, u32[]{:S(2)}, u32[]{:S(2)}) collective-permute-start(bf16[192,384]{1,0:T(8,128)(2,1)S(1)} %convert_bitcast_fusion.refs_6_), channel_id=1, source_target_pairs={{0,1},{1,0},{2,3},{3,2},{4,5},{5,4},{6,7},{7,6},{8,9},{9,8},{10,11... | collective-permute-start | bytes 442376 | tf_op jit(solution)/shard_map/ppermute | solution.py:614
  15.0 1.6 %collective-permute-start.1 = (bf16[192,384]{1,0:T(8,128)(2,1)S(1)}, bf16[192,384]{1,0:T(8,128)(2,1)S(1)}, u32[]{:S(2)}, u32[]{:S(2)}) collective-permute-start(bf16[192,384]{1,0:T(8,128)(2,1)S(1)} %convert_element_type.8.refs_4_), channel_id=1, source_target_pairs={{0,1},{1,0},{2,3},{3,2},{4,5},{5,4},{6,7},{7,6},{8,9},{9,8},{10,11... | collective-permute-start | bytes 442376 | tf_op jit(solution)/shard_map/ppermute | solution.py:614
  15.2 5.8 %copy-start.3 = (s32[6,8]{1,0:T(8,128)S(1)}, s32[6,8]{1,0:T(8,128)}, u32[]{:S(2)}) copy-start(s32[6,8]{1,0:T(8,128)} %refs_1_.9) | copy-start | bytes 580
  15.2 1.4 %collective-permute-start.3 = (f32[1,768]{1,0:T(1,128)S(1)}, f32[1,768]{1,0:T(1,128)S(1)}, u32[]{:S(2)}, u32[]{:S(2)}) collective-permute-start(f32[1,768]{1,0:T(1,128)S(1)} %reshape.37.refs_8_), channel_id=1, source_target_pairs={{0,1},{1,0},{2,3},{3,2},{4,5},{5,4},{6,7},{7,6},{8,9},{9,8},{10,11... | collective-permute-start | bytes 9224 | tf_op jit(solution)/shard_map/ppermute | solution.py:614
  21.0 0.7 copy-start.4
  23.3 1.5 %collective-permute-start.4 = (f32[432,96]{1,0:T(8,128)S(1)}, f32[432,96]{1,0:T(8,128)S(1)}, u32[]{:S(2)}, u32[]{:S(2)}) collective-permute-start(f32[432,96]{1,0:T(8,128)S(1)} %get-tuple-element.27), channel_id=1, source_target_pairs={{0,1},{1,0},{2,3},{3,2},{4,5},{5,4},{6,7},{7,6},{8,9},{9,8},{10,11... | collective-permute-start | bytes 497672 | tf_op jit(solution)/shard_map/ppermute | solution.py:614
  29.2 1.8 %collective-permute-start.5 = (bf16[1584,128]{1,0:T(8,128)(2,1)S(1)}, bf16[1584,128]{1,0:T(8,128)(2,1)S(1)}, u32[]{:S(2)}, u32[]{:S(2)}) collective-permute-start(bf16[1584,128]{1,0:T(8,128)(2,1)S(1)} %get-tuple-element.31), channel_id=1, source_target_pairs={{0,1},{1,0},{2,3},{3,2},{4,5},{5,4},{6,7},{7,6},{8,9},{9,8},{10,11... | collective-permute-start | bytes 1216520 | tf_op jit(solution)/shard_map/ppermute | solution.py:614
  32.8 21.0 %all-to-all-start.1 = ((bf16[8,312,128]{2,1,0:T(8,128)(2,1)}), bf16[8,312,128]{2,1,0:T(8,128)(2,1)S(1)}, u32[]{:S(2)}, u32[]{:S(2)}) async-start(bf16[8,312,128]{2,1,0:T(8,128)(2,1)} %bitcast.4), calls=%async_computation.1 | async-start | bytes 1277952 | tf_op jit(solution)/shard_map/all_to_all | solution.py:610
  39.9 4.9 %collective-permute-start.7 = (f32[7,7,96]{2,1,0:T(8,128)S(1)}, f32[7,7,96]{2,1,0:T(8,128)S(1)}, u32[]{:S(2)}, u32[]{:S(2)}) collective-permute-start(f32[7,7,96]{2,1,0:T(8,128)S(1)} %shard_map.170), channel_id=1, source_target_pairs={{0,2},{2,0},{4,6},{6,4},{8,10},{10,8},{12,14},{14,12},{1,3},{3,1},... | collective-permute-start | bytes 56456 | tf_op jit(solution)/shard_map/ppermute | solution.py:621
  44.8 4.1 %collective-permute-start.8 = (f32[7,7,96]{2,1,0:T(8,128)S(1)}, f32[7,7,96]{2,1,0:T(8,128)S(1)}, u32[]{:S(2)}, u32[]{:S(2)}) collective-permute-start(f32[7,7,96]{2,1,0:T(8,128)S(1)} %add.6), channel_id=1, source_target_pairs={{0,4},{2,6},{4,0},{6,2},{8,12},{10,14},{12,8},{14,10},{1,5},{3,7},... | collective-permute-start | bytes 56456 | tf_op jit(solution)/shard_map/ppermute | solution.py:621
  54.6 14.6 %all-to-all-start.2 = ((bf16[8,144,128]{2,1,0:T(8,128)(2,1)}), bf16[8,144,128]{2,1,0:T(8,128)(2,1)S(1)}, u32[]{:S(2)}, u32[]{:S(2)}) async-start(bf16[8,144,128]{2,1,0:T(8,128)(2,1)} %bitcast.6), calls=%async_computation.2 | async-start | bytes 589824 | tf_op jit(solution)/shard_map/all_to_all | solution.py:610
  58.2 2.9 %collective-permute-start.6 = (bf16[432,96]{1,0:T(8,128)(2,1)S(1)}, bf16[432,96]{1,0:T(8,128)(2,1)S(1)}, u32[]{:S(2)}, u32[]{:S(2)}) collective-permute-start(bf16[432,96]{1,0:T(8,128)(2,1)S(1)} %get-tuple-element.33), channel_id=1, source_target_pairs={{0,1},{1,0},{2,3},{3,2},{4,5},{5,4},{6,7},{7,6},{8,9},{9,8},{10,11... | collective-permute-start | bytes 248840 | tf_op jit(solution)/shard_map/ppermute | solution.py:614
  58.2 11.0 %collective-permute-start.9 = (f32[7,7,96]{2,1,0:T(8,128)S(1)}, f32[7,7,96]{2,1,0:T(8,128)S(1)}, u32[]{:S(2)}, u32[]{:S(2)}) collective-permute-start(f32[7,7,96]{2,1,0:T(8,128)S(1)} %add.7.refs_1_), channel_id=1, source_target_pairs={{0,8},{2,10},{4,12},{6,14},{8,0},{10,2},{12,4},{14,6},{1,9},{3,11}... | collective-permute-start | bytes 56456 | tf_op jit(solution)/shard_map/ppermute | solution.py:621

commit v4 on v3

--- a/solution.py
+++ b/solution.py
@@ -73,6 +73,9 @@
         self.halo_at = round_up(self.share, 8)
         self.box2 = round_up(self.halo_at + self.capacity * self.strip, 8)
         self.box3 = round_up(self.share, 8)
+        self.taps_at = round_up(self.share, 16)
+        self.message = round_up(self.taps_at + 49, 16)
+        self.paired = owners in (4, 8)
 
     def owner_of(self, link):
         factor = -(-65536 // self.tiles)
@@ -176,9 +179,13 @@
     return total
 
 
-def rim_row(z, grown, taps, row, start):
+def rim_row(z, grown, taps, row, start, flipped):
     total = start
     inner = []
+
+    def tap(a, b):
+        return taps[6 - a, 6 - b : 7 - b, :] if flipped else taps[a, b : b + 1, :]
+
     for a in range(7):
         at = (row + a) * z.wide * 8
         if 3 <= row + a < z.far:
@@ -186,14 +193,14 @@
             continue
         for b in range(7):
             low = at + b * 8
-            total = total + grown[low : low + z.side * 8, :] * taps[a, b : b + 1, :]
+            total = total + grown[low : low + z.side * 8, :] * tap(a, b)
     pieces = [total[col * 8 : (col + 1) * 8] for col in range(z.side)]
     for a, at in inner:
         for col in range(z.side):
             for b in range(7):
                 if col + b < 3 or col + b >= z.far:
                     low = at + (col + b) * 8
-                    pieces[col] = pieces[col] + grown[low : low + 8, :] * taps[a, b : b + 1, :]
+                    pieces[col] = pieces[col] + grown[low : low + 8, :] * tap(a, b)
     return pieces
 
 
@@ -263,8 +270,10 @@
     )
 
 
-def local_part(z, tile_data, cotangent, taps, conv_bias):
-    def body(tile_data, cotangent, taps, bias, keep, send, out, work, grown):
+def local_part(z, slots, tile_data, cotangent, taps, conv_bias):
+    def body(slots, tile_data, cotangent, taps, bias, keep, send, out, links, work, grown):
+        for place in range(3 * z.links):
+            links[place] = slots[place]
         core = lax.axis_index("sub")
         for which, block in enumerate((tile_data, cotangent)):
             for tile in range(z.tiles):
@@ -288,9 +297,13 @@
     rows = shaped((2 * z.half, z.ch), BF16)
     return call(
         body,
-        (rows, rows, shaped((z.pixels * 8, z.ch), F32)),
-        [tile_data, cotangent, taps, conv_bias],
+        (rows, rows, shaped((z.pixels * 8, z.ch), F32), shaped(slots.shape, jnp.int32)),
+        [slots, tile_data, cotangent, taps, conv_bias],
+        1,
         scratch=[pixel_major(z), field(z)],
+        out_specs=tuple(
+            pl.BlockSpec(memory_space=space) for space in [pltpu.VMEM] * 3 + [pltpu.SMEM]
+        ),
         flops=2 * 49 * z.rows * z.ch,
     )
 
@@ -302,7 +315,7 @@
         assemble(z, box, z.box1, 0, slots, tissue, flat, grown)
         for row in range(z.side):
             start = inner[row * z.side * 8 : (row + 1) * z.side * 8, :]
-            for col, piece in enumerate(rim_row(z, grown, taps, row, start)):
+            for col, piece in enumerate(rim_row(z, grown, taps, row, start, False)):
                 at = (row * z.side + col) * z.tiles
                 whole[at : at + z.tiles, :] = piece[0 : z.tiles]
         own[...] = whole[pl.ds(pl.multiple_of(core * z.half, 8), z.half), :]
@@ -535,49 +548,132 @@
     return call(body, shaped((z.owners * z.box3, LANES), BF16), [inbox], after=after)
 
 
-def second_conv(z, slots, tissue, inbox, g_own, received, block, cotangent, taps):
-    def body(slots, tissue, inbox, g_own, received, block_own, block_far, cotangent, taps, out,
-             block_out, box, flat, grown, plain, totals):
-        box[...] = inbox[...].astype(F32)
-        assemble(z, box, z.box2, z.halo_at, slots, tissue, flat, grown)
-        both_halves(z, plain, g_own[...], received[0 : z.half, 0 : z.ch])
-        for tile in range(z.tiles):
-            for row in range(z.side):
-                spot = pl.ds(row * z.side * z.tiles + tile, z.side, stride=z.tiles)
-                grown[inner_spot(z, tile, row), :] = plain[spot, :]
-        start = jnp.zeros((z.side * 8, z.ch), F32)
-
-        @pl.loop(0, z.side)
-        def _(row):
-            total = conv_row(z, grown, taps, row, start, True)
-            totals[pl.ds(pl.multiple_of(row * z.side * 8, 8), z.side * 8), :] = total
-
-        for tile in range(z.tiles):
-            for row in range(z.side):
-                spot = pl.ds(row * z.side * 8 + tile, z.side, stride=8)
-                out[tile, row] = (totals[spot, :] + cotangent[tile, row].astype(F32)).astype(BF16)
-
+def second_inner(z, g_own, received, block, cotangent, taps):
+    def body(g_own, received, block_own, block_far, cotangent, taps, out, block_out, plain, grown, cot):
         both_halves(z, plain, block_own[...], block_far[...])
         for tile in range(z.tiles):
             for row in range(z.side):
                 spot = pl.ds(row * z.side * z.tiles + tile, z.side, stride=z.tiles)
                 block_out[tile, row] = plain[spot, :].astype(BF16)
-
-    out = shaped((z.tiles, z.side, z.side, z.ch), BF16)
+        both_halves(z, plain, g_own[...], received[0 : z.half, 0 : z.ch])
+        grown[...] = jnp.zeros_like(grown)
+        for tile in range(z.tiles):
+            for row in range(z.side):
+                spot = pl.ds(row * z.side * z.tiles + tile, z.side, stride=z.tiles)
+                grown[inner_spot(z, tile, row), :] = plain[spot, :]
+                spot = pl.ds(row * z.side * 8 + tile, z.side, stride=8)
+                cot[spot, :] = cotangent[tile, row].astype(F32)
+
+        @pl.loop(0, z.side)
+        def _(row):
+            spot = pl.ds(pl.multiple_of(row * z.side * 8, 8), z.side * 8)
+            out[spot, :] = conv_row(z, grown, taps, row, cot[spot, :], True)
+
     return call(
         body,
-        (out, out),
-        [slots, tissue, inbox, g_own, received, *block, cotangent, taps],
+        (
+            shaped((z.pixels * 8, z.ch), F32),
+            shaped((z.tiles, z.side, z.side, z.ch), BF16),
+        ),
+        [g_own, received, *block, cotangent, taps],
+        0,
+        [pixel_major(z), field(z), pltpu.VMEM((z.pixels * 8, z.ch), F32)],
+        flops=2 * 49 * z.rows * z.ch,
+    )
+
+
+def second_rim(z, slots, tissue, inbox, inner, taps, after):
+    def body(slots, tissue, inbox, inner, taps, out, box, flat, grown, totals):
+        box[...] = inbox[...].astype(F32)
+        assemble(z, box, z.box2, z.halo_at, slots, tissue, flat, grown)
+        for row in range(z.side):
+            start = inner[row * z.side * 8 : (row + 1) * z.side * 8, :]
+            for col, piece in enumerate(rim_row(z, grown, taps, row, start, True)):
+                at = (row * z.side + col) * 8
+                totals[at : at + 8, :] = piece
+            for tile in range(z.tiles):
+                spot = pl.ds(row * z.side * 8 + tile, z.side, stride=8)
+                out[tile, row] = totals[spot, :].astype(BF16)
+
+    return call(
+        body,
+        shaped((z.tiles, z.side, z.side, z.ch), BF16),
+        [slots, tissue, inbox, inner, taps],
         2,
         [
             boxes(z, z.box2),
             flat_strips(z),
             field(z),
-            pixel_major(z),
             pltpu.VMEM((z.pixels * 8, z.ch), F32),
         ],
-        flops=2 * 49 * z.rows * z.ch,
-    )
+        after=after,
+    )
+
+
+def share_message(z, inbox, taps, after):
+    def body(inbox, taps_own, taps_far, out):
+        total = inbox[0 : z.share, :].astype(F32)
+        for owner in range(1, z.owners):
+            at = owner * z.box2
+            total = total + inbox[at : at + z.share, :].astype(F32)
+        out[0 : z.share, :] = total.astype(BF16)
+        rows = [taps_own[a] + taps_far[a] for a in range(7)]
+        low = z.taps_at
+        out[low : low + 49, 0 : z.ch] = jnp.concatenate(rows, axis=0).astype(BF16)
+
+    return call(body, shaped((z.message, LANES), BF16), [inbox, *taps], after=after)
+
+
+def column(z, messages):
+    count = len(messages)
+
+    def body(*refs):
+        messages, (out, taps, work) = refs[:count], refs[count:]
+        line = lax.axis_index("tiles") // 2
+        for step, message in enumerate(messages):
+            place = jnp.bitwise_xor(line, step)
+            at = pl.multiple_of(place * z.share, 16)
+            out[pl.ds(at, z.share), :] = message[0 : z.share, :]
+            at = pl.multiple_of(place * 56, 8)
+            work[pl.ds(at, 49), :] = message[z.taps_at : z.taps_at + 49, 0 : z.ch].astype(F32)
+        for a in range(7):
+            total = work[a * 7 : a * 7 + 7, :]
+            for place in range(1, count):
+                low = place * 56 + a * 7
+                total = total + work[low : low + 7, :]
+            taps[a] = total
+
+    return call(
+        body,
+        (shaped((count * z.share, LANES), BF16), shaped((7, 7, z.ch), F32)),
+        messages,
+        scratch=[pltpu.VMEM((count * 56, z.ch), F32)],
+    )
+
+
+def finish_columns(z, own, far, scale):
+    hid = z.hidden
+    wide = 2 * z.ch
+    groups = hid // LANES
+
+    def body(own, far, grad_in, grad_out):
+        first = lax.axis_index("tiles") % 2 == 0
+        for owner in range(z.owners):
+            row = owner * z.share
+            stop = row + z.share
+            while row < stop:
+                group, place = divmod(row, wide)
+                count = min(stop - row, wide - place)
+                at = owner // 2 * z.share + row - owner * z.share
+                out = grad_in if group < groups else grad_out
+                low = group % groups * LANES
+                mine, other = own[at : at + count, :], far[at : at + count, :]
+                value = jnp.where(first == (owner % 2 == 0), mine.astype(F32), other.astype(F32))
+                out[place : place + count, low : low + LANES] = value * scale
+                row += count
+
+    out = shaped((wide, hid), F32)
+    return call(body, (out, out), [own, far])
 
 
 def finish(z, inbox, taps, scale):
@@ -614,11 +710,15 @@
     return lax.ppermute(piece, "sub", [(0, 1), (1, 0)])
 
 
+def swap_tiles(z, piece, step):
+    pairs = [(owner, owner ^ step) for owner in range(z.owners)]
+    return lax.ppermute(piece, "tiles", pairs)
+
+
 def sum_tiles(z, part):
     step = 1
     while True:
-        pairs = [(owner, owner ^ step) for owner in range(z.owners)]
-        other = lax.ppermute(part, "tiles", pairs)
+        other = swap_tiles(z, part, step)
         step *= 2
         if step == z.owners:
             return part, other
@@ -650,8 +750,8 @@
     w_out16 = w_out.T.astype(BF16)
     vectors = jnp.concatenate([layer_norm_gain, layer_norm_bias, b_out, layer_scale, b_in])
     vectors = vectors.reshape(1, -1)
-    rows_keep, rows_send, inner = local_part(
-        z, tile_data, cotangent, kernel, conv_bias.reshape(1, z.ch)
+    rows_keep, rows_send, inner, slots = local_part(
+        z, slots, tile_data, cotangent, kernel, conv_bias.reshape(1, z.ch)
     )
     w_in_both = (w_in16, swap_sub(w_in16))
     w_out_both = (w_out16, swap_sub(w_out16))
@@ -665,12 +765,23 @@
     received = swap_sub(send)
     inbox2 = exchange_tiles(z, second_strips(z, slots, g_own, keep, received))
     taps = filter_gradient(z, slots, tissue, inbox, tile_data, g_own, received, scale)
-    taps_own, taps_far = sum_tiles(z, taps)
-    inbox3 = exchange_tiles(z, sum_shares(z, inbox2, (taps_own,)))
-    tile_grad, block_out = second_conv(
-        z, slots, tissue, inbox2, g_own, received, (block_own, swap_sub(block_far)), cotangent, kernel
-    )
-    grad_in, grad_out, grad_kernel = finish(z, inbox3, (taps_own, taps_far), scale)
+    inner2, block_out = second_inner(
+        z, g_own, received, (block_own, swap_sub(block_far)), cotangent, kernel
+    )
+    if z.paired:
+        taps_both = (taps, swap_tiles(z, taps, 1))
+        message = share_message(z, inbox2, taps_both, (inner2,))
+        steps = range(2, z.owners, 2)
+        messages = [message] + [swap_tiles(z, message, step) for step in steps]
+        own, grad_kernel = column(z, messages)
+        far = swap_tiles(z, own, 1)
+        tile_grad = second_rim(z, slots, tissue, inbox2, inner2, kernel, (own,))
+        grad_in, grad_out = finish_columns(z, own, far, scale)
+    else:
+        taps_own, taps_far = sum_tiles(z, taps)
+        inbox3 = exchange_tiles(z, sum_shares(z, inbox2, (taps_own, inner2)))
+        tile_grad = second_rim(z, slots, tissue, inbox2, inner2, kernel, ())
+        grad_in, grad_out, grad_kernel = finish(z, inbox3, (taps_own, taps_far), scale)
     return block_out, tile_grad, grad_in, grad_out.T, grad_kernel
 
 

time: 70.5 us -> 67.5 us (0.957)
  waiting for transfers between devices: 22.2 us -> 19.5 us
  Pallas kernels: 23.1 us -> 25.4 us
  starting transfers between devices: 22.1 us -> 20.3 us
    ppermute x3 -> x5, waiting for transfers between devices: 9.05 us -> 4.27 us  [swap_tiles(): return lax.ppermute(piece, 'tiles', pairs)]
    all_to_all x3 -> x2, starting transfers between devices: 14.6 us -> 11 us  [exchange_tiles(): lax.all_to_all(boxes, 'tiles', split_axis=0, concat_axis=0, tiled=True)]
    pallas_call x9 -> x11, Pallas kernels: 23.1 us -> 25.4 us  [call(): pl.pallas_call(run, out_shape=outs, in_specs=[pl.BlockSpec(memory_space=s...]
    all_to_all x3 -> x2, waiting for transfers between devices: 9.29 us -> 11.3 us  [exchange_tiles(): lax.all_to_all(boxes, 'tiles', split_axis=0, concat_axis=0, tiled=True)]
    ppermute x3 -> x5, starting transfers between devices: 6.04 us -> 7.71 us  [swap_tiles(): return lax.ppermute(piece, 'tiles', pairs)]
  transfers between devices with their start and end apart: 13 -> 14, of which waited for: 8 -> 8; matrix products, arithmetic and copies ran while one was open for 0% -> 0% of each run, Pallas kernels for 16% -> 21%
where the time goes in v4:
time: 67.5 us; the launch traced here: 67.1 us
  Pallas kernels  25.4 us (38%)
  starting transfers between devices  20.3 us (30%)
  waiting for transfers between devices  19.5 us (29%)
  local copies, waits for them, and re-layouts  1.01 us (1%)
  between operations  0.87 us (1%)
    pallas_call x11, Pallas kernels, call(): pl.pallas_call(run, out_shape=outs, in_specs=[pl.BlockSpec(memory_space=s...  25.4 us
    all_to_all x2, waiting for transfers between devices, exchange_tiles(): lax.all_to_all(boxes, 'tiles', split_axis=0, concat_axis=0, tiled=True)  11.3 us
    all_to_all x2, starting transfers between devices, exchange_tiles(): lax.all_to_all(boxes, 'tiles', split_axis=0, concat_axis=0, tiled=True)  11 us
    ppermute x5, starting transfers between devices, swap_tiles(): return lax.ppermute(piece, 'tiles', pairs)  7.71 us
    ppermute x5, waiting for transfers between devices, swap_tiles(): return lax.ppermute(piece, 'tiles', pairs)  4.27 us
    ppermute x7, waiting for transfers between devices, swap_sub(): return lax.ppermute(piece, 'sub', [(0, 1), (1, 0)])  3.9 us
    ppermute x7, starting transfers between devices, swap_sub(): return lax.ppermute(piece, 'sub', [(0, 1), (1, 0)])  1.66 us
  transfers between devices with their start and end apart: 14, of which 8 were waited for; matrix products, arithmetic and copies ran while one was open for 0% of the time, Pallas kernels for 21%

profile of v4, /device:TPU:0, one launch (start us, length us, event | category | flops | bytes accessed | tf_op | source)
XLA Modules:
  0.0 67.1 jit_solution(6197994580410129617)
XLA Ops:
  0.6 2.2 %shard_map.164 = (bf16[1344,128]{1,0:T(8,128)(2,1)}, s32[144]{0:T(256)}) custom-call(s32[6,8]{1,0:T(8,128)} %refs_0_.1, bf16[6,12,12,96]{3,2,1,0:T(8,128)(2,1)} %refs_3_.3), custom_call_target="tpu_custom_call" | custom-call | bytes 166080 | tf_op jit(solution)/shard_map/pallas_call | solution.py:35
  2.9 0.0 copy-start
  2.9 0.0 copy-start.1
  2.9 0.0 copy-start.2
  2.9 7.4 %all-to-all-start = ((bf16[8,168,128]{2,1,0:T(8,128)(2,1)}), bf16[8,168,128]{2,1,0:T(8,128)(2,1)S(1)}, u32[]{:S(2)}, u32[]{:S(2)}) async-start(bf16[8,168,128]{2,1,0:T(8,128)(2,1)} %bitcast.13), calls=%async_computation | async-start | bytes 688128 | tf_op jit(solution)/shard_map/all_to_all | solution.py:706
  10.3 0.0 copy-start.4
  10.3 0.0 copy-start.5
  10.3 0.0 copy-done
  10.3 0.0 copy-done.1
  10.4 0.0 copy-done.2
  10.4 0.6 copy-done.4
  11.0 0.0 copy-done.5
  11.0 0.0 copy-start.6
  11.0 4.2 %shard_map.165 = (bf16[864,96]{1,0:T(8,128)(2,1)S(1)}, bf16[864,96]{1,0:T(8,128)(2,1)S(1)}, f32[1152,96]{1,0:T(8,128)S(1)}, s32[144]{0:T(256)S(1)}) custom-call(s32[144]{0:T(256)S(1)} %copy-done.4, bf16[6,12,12,96]{3,2,1,0:T(8,128)(2,1)S(1)} %copy-done, bf16[6,12,12,96]{3,2,1,0:T(8,128)(2,1)S(1)} %copy-done.1, f32[7,7,96]{2,1,0:T(8,128)S(1)} %copy-done.2, ...), custom_call_target="tpu_custom_call" | custom-call | flops 8128512 | bytes 351552 | tf_op jit(solution)/shard_map/pallas_call | solution.py:35
  15.2 0.0 copy-start.7
  15.2 0.1 collective-permute-start
  15.3 0.0 copy-done.6
  15.3 0.0 copy-start.8
  15.3 0.0 copy-start.9
  15.3 0.0 copy-start.10
  15.4 0.0 copy-start.11
  15.4 0.0 copy-start.12
  15.4 0.5 collective-permute-start.2
  15.9 0.2 copy-done.7
  16.2 0.1 collective-permute-start.1
  16.3 0.0 copy-done.8
  16.3 0.0 copy-done.9
  16.3 0.0 copy-done.10
  16.3 0.0 copy-done.11
  16.3 0.0 copy-done.12
  16.3 0.1 concatenate.3
  16.4 0.5 collective-permute-start.3
  16.9 0.8 %collective-permute-done.3.refs_8_.refs_9_ = f32[1,768]{1,0:T(1,128)S(1)} collective-permute-done((f32[1,768]{1,0:T(1,128)S(1)}, f32[1,768]{1,0:T(1,128)S(1)}, u32[]{:S(2)}, u32[]{:S(2)}) %collective-permute-start.3) | collective-permute-done | bytes 3104 | tf_op jit(solution)/shard_map/ppermute | solution.py:710
  17.8 0.0 collective-permute-done.2.refs_7_
  17.8 0.0 collective-permute-done.1.refs_6_.refs_5_
  17.8 0.0 collective-permute-done.refs_5_.refs_3_
  17.8 3.2 %all-to-all-done = bf16[8,168,128]{2,1,0:T(8,128)(2,1)S(1)} async-done(((bf16[8,168,128]{2,1,0:T(8,128)(2,1)}), bf16[8,168,128]{2,1,0:T(8,128)(2,1)S(1)}, u32[]{:S(2)}, u32[]{:S(2)}) %all-to-all-start) | async-done | bytes 344096 | tf_op jit(solution)/shard_map/all_to_all | solution.py:706
  21.0 0.0 copy-done.3
  21.0 1.7 %shard_map.166 = (f32[432,96]{1,0:T(8,128)S(1)}, f32[432,96]{1,0:T(8,128)S(1)}) custom-call(s32[144]{0:T(256)S(1)} %get-tuple-element.25.refs_0_, s32[6,8]{1,0:T(8,128)S(1)} %copy-done.3, bf16[1344,128]{1,0:T(8,128)(2,1)S(1)} %bitcast.10, f32[1152,96]{1,0:T(8,128)S(1)} %get-tuple-element.27.refs_3_, f32[7,7,96]{2,1,0:T(8,128)S(1)} %copy-done.2, ...), custom_call_target="tpu_custom_call" | custom-call | bytes 806016 | tf_op jit(solution)/shard_map/pallas_call | solution.py:35
  22.6 0.1 collective-permute-start.4
  22.7 1.5 %collective-permute-done.4.refs_1_ = f32[432,96]{1,0:T(8,128)S(1)} collective-permute-done((f32[432,96]{1,0:T(8,128)S(1)}, f32[432,96]{1,0:T(8,128)S(1)}, u32[]{:S(2)}, u32[]{:S(2)}) %collective-permute-start.4) | collective-permute-done | bytes 165920 | tf_op jit(solution)/shard_map/ppermute | solution.py:710
  24.2 4.3 %shard_map.167 = (bf16[432,96]{1,0:T(8,128)(2,1)S(1)}, bf16[432,96]{1,0:T(8,128)(2,1)S(1)}, bf16[432,96]{1,0:T(8,128)(2,1)S(1)}, f32[1152,128]{1,0:T(8,128)S(1)}, bf16[1584,128]{1,0:T(8,128)(2,1)S(1)}) custom-call(f32[432,96]{1,0:T(8,128)S(1)} %get-tuple-element.29.refs_0_, f32[432,96]{1,0:T(8,128)S(1)} %collective-permute-done.4.refs_1_, ...), custom_call_target="tpu_custom_call" | custom-call | flops 764411904 | bytes 1259520 | tf_op jit(solution)/shard_map/pallas_call | solution.py:35
  28.5 0.2 collective-permute-start.5
  28.7 1.6 %collective-permute-done.5.refs_1_.refs_3_.refs_5_ = bf16[1584,128]{1,0:T(8,128)(2,1)S(1)} collective-permute-done((bf16[1584,128]{1,0:T(8,128)(2,1)S(1)}, bf16[1584,128]{1,0:T(8,128)(2,1)S(1)}, u32[]{:S(2)}, u32[]{:S(2)}) %collective-permute-start.5) | collective-permute-done | bytes 405536 | tf_op jit(solution)/shard_map/ppermute | solution.py:710
  30.3 1.8 %shard_map.169 = bf16[2496,128]{1,0:T(8,128)(2,1)} custom-call(s32[144]{0:T(256)S(1)} %get-tuple-element.25.refs_0_, bf16[432,96]{1,0:T(8,128)(2,1)S(1)} %get-tuple-element.32.refs_0_.refs_1_.refs_4_, f32[1152,128]{1,0:T(8,128)S(1)} %get-tuple-element.37.refs_2_, bf16[1584,128]{1,0:T(8,128)(2,1)S(1)} %collective-permute-done.5.refs_1_.refs_3_.refs_5_), custom_call_target="tpu_custom_call" | custom-call | bytes 1078848 | tf_op jit(solution)/shard_map/pallas_call | solution.py:35
  32.1 3.6 %all-to-all-start.1 = ((bf16[8,312,128]{2,1,0:T(8,128)(2,1)}), bf16[8,312,128]{2,1,0:T(8,128)(2,1)S(1)}, u32[]{:S(2)}, u32[]{:S(2)}) async-start(bf16[8,312,128]{2,1,0:T(8,128)(2,1)} %bitcast.4), calls=%async_computation.1 | async-start | bytes 1277952 | tf_op jit(solution)/shard_map/all_to_all | solution.py:706
  35.7 0.2 collective-permute-start.6
  35.9 3.5 %shard_map.170.refs_1_ = f32[7,7,96]{2,1,0:T(8,128)S(1)} custom-call(s32[144]{0:T(256)S(1)} %get-tuple-element.25.refs_0_, s32[6,8]{1,0:T(8,128)S(1)} %copy-done.3, bf16[1344,128]{1,0:T(8,128)(2,1)S(1)} %bitcast.11, bf16[6,12,12,96]{3,2,1,0:T(8,128)(2,1)S(1)} %copy-done, bf16[432,96]{1,0:T(8,128)(2,1)S(1)} %get-tuple-element.32.refs_0_.refs_1_.refs_4_, ...), custom_call_target="tpu_custom_call" | custom-call | flops 8128512 | bytes 999168 | tf_op jit(solution)/shard_map/pallas_call | solution.py:35
  39.4 1.9 %collective-permute-start.7 = (f32[7,7,96]{2,1,0:T(8,128)S(1)}, f32[7,7,96]{2,1,0:T(8,128)S(1)}, u32[]{:S(2)}, u32[]{:S(2)}) collective-permute-start(f32[7,7,96]{2,1,0:T(8,128)S(1)} %shard_map.170.refs_1_), channel_id=1, source_target_pairs={{0,2},{2,0},{4,6},{6,4},{8,10},{10,8},{12,14},{14,12},{1,3},{3,1},... | collective-permute-start | bytes 56456 | tf_op jit(solution)/shard_map/ppermute | solution.py:715
  41.3 0.0 collective-permute-done.6.refs_3_
  41.3 3.7 %shard_map.168 = (f32[1152,96]{1,0:T(8,128)S(1)}, bf16[6,12,12,96]{3,2,1,0:T(8,128)(2,1)}) custom-call(bf16[432,96]{1,0:T(8,128)(2,1)S(1)} %get-tuple-element.32.refs_0_.refs_1_.refs_4_, bf16[1584,128]{1,0:T(8,128)(2,1)S(1)} %collective-permute-done.5.refs_1_.refs_3_.refs_5_, bf16[432,96]{1,0:T(8,128)(2,1)S(1)} %get-tuple-element.34.refs_2_, ...), custom_call_target="tpu_custom_call" | custom-call | flops 8128512 | bytes 839040 | tf_op jit(solution)/shard_map/pallas_call | solution.py:35
  45.0 0.0 collective-permute-done.7.refs_2_
  45.0 8.1 %all-to-all-done.1 = bf16[8,312,128]{2,1,0:T(8,128)(2,1)S(1)} async-done(((bf16[8,312,128]{2,1,0:T(8,128)(2,1)}), bf16[8,312,128]{2,1,0:T(8,128)(2,1)S(1)}, u32[]{:S(2)}, u32[]{:S(2)}) %all-to-all-start.1) | async-done | bytes 639008 | tf_op jit(solution)/shard_map/all_to_all | solution.py:706
  53.1 1.3 %collective-permute-start.10 = (bf16[208,128]{1,0:T(8,128)(2,1)S(1)}, bf16[208,128]{1,0:T(8,128)(2,1)S(1)}, u32[]{:S(2)}, u32[]{:S(2)}) collective-permute-start(bf16[208,128]{1,0:T(8,128)(2,1)S(1)} %shard_map.171.refs_0_), channel_id=1, source_target_pairs={{0,12},{2,14},{4,8},{6,10},{8,4},{10,6},{12,0},{14,2},{1,13},{3,15... | collective-permute-start | bytes 159752 | tf_op jit(solution)/shard_map/ppermute | solution.py:715
  54.4 0.9 %collective-permute-start.9 = (bf16[208,128]{1,0:T(8,128)(2,1)S(1)}, bf16[208,128]{1,0:T(8,128)(2,1)S(1)}, u32[]{:S(2)}, u32[]{:S(2)}) collective-permute-start(bf16[208,128]{1,0:T(8,128)(2,1)S(1)} %shard_map.171.refs_0_), channel_id=1, source_target_pairs={{0,8},{2,10},{4,12},{6,14},{8,0},{10,2},{12,4},{14,6},{1,9},{3,11}... | collective-permute-start | bytes 159752 | tf_op jit(solution)/shard_map/ppermute | solution.py:715
  55.3 2.3 %collective-permute-start.8 = (bf16[208,128]{1,0:T(8,128)(2,1)S(1)}, bf16[208,128]{1,0:T(8,128)(2,1)S(1)}, u32[]{:S(2)}, u32[]{:S(2)}) collective-permute-start(bf16[208,128]{1,0:T(8,128)(2,1)S(1)} %shard_map.171.refs_0_), channel_id=1, source_target_pairs={{0,4},{2,6},{4,0},{6,2},{8,12},{10,14},{12,8},{14,10},{1,5},{3,7},... | collective-permute-start | bytes 159752 | tf_op jit(solution)/shard_map/ppermute | solution.py:715
  57.6 1.9 %collective-permute-done.10.refs_3_ = bf16[208,128]{1,0:T(8,128)(2,1)S(1)} collective-permute-done((bf16[208,128]{1,0:T(8,128)(2,1)S(1)}, bf16[208,128]{1,0:T(8,128)(2,1)S(1)}, u32[]{:S(2)}, u32[]{:S(2)}) %collective-permute-start.10) | collective-permute-done | bytes 53280 | tf_op jit(solution)/shard_map/ppermute | solution.py:715
  59.5 1.0 %collective-permute-done.9.refs_2_ = bf16[208,128]{1,0:T(8,128)(2,1)S(1)} collective-permute-done((bf16[208,128]{1,0:T(8,128)(2,1)S(1)}, bf16[208,128]{1,0:T(8,128)(2,1)S(1)}, u32[]{:S(2)}, u32[]{:S(2)}) %collective-permute-start.9) | collective-permute-done | bytes 53280 | tf_op jit(solution)/shard_map/ppermute | solution.py:715
  60.5 0.0 collective-permute-done.8.refs_1_
  60.5 0.6 shard_map.172
  61.1 1.3 %collective-permute-start.11 = (bf16[576,128]{1,0:T(8,128)(2,1)S(1)}, bf16[576,128]{1,0:T(8,128)(2,1)S(1)}, u32[]{:S(2)}, u32[]{:S(2)}) collective-permute-start(bf16[576,128]{1,0:T(8,128)(2,1)S(1)} %get-tuple-element.39.refs_5_.refs_0_), channel_id=1, source_target_pairs={{0,2},{2,0},{4,6},{6,4},{8,10},{10,8},{12,14},{14,12},{1,3},{3,1},... | collective-permute-start | bytes 442376 | tf_op jit(solution)/shard_map/ppermute | solution.py:715
  62.4 2.4 %shard_map.173 = bf16[6,12,12,96]{3,2,1,0:T(8,128)(2,1)} custom-call(s32[144]{0:T(256)S(1)} %get-tuple-element.25.refs_0_, s32[6,8]{1,0:T(8,128)S(1)} %copy-done.3, bf16[2496,128]{1,0:T(8,128)(2,1)S(1)} %bitcast.9, f32[1152,96]{1,0:T(8,128)S(1)} %get-tuple-element.38.refs_3_, f32[7,7,96]{2,1,0:T(8,128)S(1)} %copy-done.2, ...), custom_call_target="tpu_custom_call" | custom-call | bytes 1100928 | tf_op jit(solution)/shard_map/pallas_call | solution.py:35
  64.9 1.4 %collective-permute-done.11.refs_1_ = bf16[576,128]{1,0:T(8,128)(2,1)S(1)} collective-permute-done((bf16[576,128]{1,0:T(8,128)(2,1)S(1)}, bf16[576,128]{1,0:T(8,128)(2,1)S(1)}, u32[]{:S(2)}, u32[]{:S(2)}) %collective-permute-start.11) | collective-permute-done | bytes 147488 | tf_op jit(solution)/shard_map/ppermute | solution.py:715
  66.3 0.9 %shard_map.174 = (f32[192,384]{1,0:T(8,128)}, f32[192,384]{1,0:T(8,128)}) custom-call(bf16[576,128]{1,0:T(8,128)(2,1)S(1)} %get-tuple-element.39.refs_5_.refs_0_, bf16[576,128]{1,0:T(8,128)(2,1)S(1)} %collective-permute-done.11.refs_1_), custom_call_target="tpu_custom_call" | custom-call | bytes 294912 | tf_op jit(solution)/shard_map/pallas_call | solution.py:35
  (5 shorter events, 0.1 us)
Async XLA Ops:
  2.9 7.5 %copy-start = (bf16[6,12,12,96]{3,2,1,0:T(8,128)(2,1)S(1)}, bf16[6,12,12,96]{3,2,1,0:T(8,128)(2,1)}, u32[]{:S(2)}) copy-start(bf16[6,12,12,96]{3,2,1,0:T(8,128)(2,1)} %refs_3_.3) | copy-start | bytes 497668
  2.9 7.5 %copy-start.1 = (bf16[6,12,12,96]{3,2,1,0:T(8,128)(2,1)S(1)}, bf16[6,12,12,96]{3,2,1,0:T(8,128)(2,1)}, u32[]{:S(2)}) copy-start(bf16[6,12,12,96]{3,2,1,0:T(8,128)(2,1)} %refs_4_.4) | copy-start | bytes 497668
  2.9 7.4 %copy-start.2 = (f32[7,7,96]{2,1,0:T(8,128)S(1)}, f32[7,7,96]{2,1,0:T(8,128)}, u32[]{:S(2)}) copy-start(f32[7,7,96]{2,1,0:T(8,128)} %refs_4_.5) | copy-start | bytes 56452
  2.9 18.1 %all-to-all-start = ((bf16[8,168,128]{2,1,0:T(8,128)(2,1)}), bf16[8,168,128]{2,1,0:T(8,128)(2,1)S(1)}, u32[]{:S(2)}, u32[]{:S(2)}) async-start(bf16[8,168,128]{2,1,0:T(8,128)(2,1)} %bitcast.13), calls=%async_computation | async-start | bytes 688128 | tf_op jit(solution)/shard_map/all_to_all | solution.py:706
  10.3 0.7 %copy-start.4 = (s32[144]{0:T(256)S(1)}, s32[144]{0:T(256)}, u32[]{:S(2)}) copy-start(s32[144]{0:T(256)} %get-tuple-element.24.refs_0_) | copy-start | bytes 1732
  10.3 0.7 %copy-start.5 = (f32[96]{0:T(128)S(1)}, f32[96]{0:T(128)}, u32[]{:S(2)}) copy-start(f32[96]{0:T(128)} %param.18) | copy-start | bytes 1156
  11.0 4.3 %copy-start.6 = (f32[384,192]{0,1:T(8,128)S(1)}, f32[384,192]{0,1:T(8,128)}, u32[]{:S(2)}) copy-start(f32[384,192]{0,1:T(8,128)} %param.23) | copy-start | bytes 884740
  15.2 1.0 %copy-start.7 = (f32[192,384]{1,0:T(8,128)S(1)}, f32[192,384]{1,0:T(8,128)}, u32[]{:S(2)}) copy-start(f32[192,384]{1,0:T(8,128)} %param.21) | copy-start | bytes 884740
  15.2 2.6 %collective-permute-start = (bf16[864,96]{1,0:T(8,128)(2,1)S(1)}, bf16[864,96]{1,0:T(8,128)(2,1)S(1)}, u32[]{:S(2)}, u32[]{:S(2)}) collective-permute-start(bf16[864,96]{1,0:T(8,128)(2,1)S(1)} %get-tuple-element.28), channel_id=1, source_target_pairs={{0,1},{1,0},{2,3},{3,2},{4,5},{5,4},{6,7},{7,6},{8,9},{9,8},{10,11... | collective-permute-start | bytes 497672 | tf_op jit(solution)/shard_map/ppermute | solution.py:710
  15.3 0.9 %copy-start.8 = (f32[384]{0:T(512)S(1)}, f32[384]{0:T(512)}, u32[]{:S(2)}) copy-start(f32[384]{0:T(512)} %param.22) | copy-start | bytes 4612
  15.3 0.9 %copy-start.9 = (f32[96]{0:T(128)S(1)}, f32[96]{0:T(128)}, u32[]{:S(2)}) copy-start(f32[96]{0:T(128)} %param.19) | copy-start | bytes 1156
  15.3 0.9 %copy-start.10 = (f32[96]{0:T(128)S(1)}, f32[96]{0:T(128)}, u32[]{:S(2)}) copy-start(f32[96]{0:T(128)} %param.20) | copy-start | bytes 1156
  15.4 0.9 %copy-start.11 = (f32[96]{0:T(128)S(1)}, f32[96]{0:T(128)}, u32[]{:S(2)}) copy-start(f32[96]{0:T(128)} %param.24) | copy-start | bytes 1156
  15.4 0.9 %copy-start.12 = (f32[96]{0:T(128)S(1)}, f32[96]{0:T(128)}, u32[]{:S(2)}) copy-start(f32[96]{0:T(128)} %param.25) | copy-start | bytes 1156
  15.4 2.4 %collective-permute-start.2 = (bf16[192,384]{1,0:T(8,128)(2,1)S(1)}, bf16[192,384]{1,0:T(8,128)(2,1)S(1)}, u32[]{:S(2)}, u32[]{:S(2)}) collective-permute-start(bf16[192,384]{1,0:T(8,128)(2,1)S(1)} %convert_bitcast_fusion.refs_6_), channel_id=1, source_target_pairs={{0,1},{1,0},{2,3},{3,2},{4,5},{5,4},{6,7},{7,6},{8,9},{9,8},{10,11... | collective-permute-start | bytes 442376 | tf_op jit(solution)/shard_map/ppermute | solution.py:710
  16.2 1.6 %collective-permute-start.1 = (bf16[192,384]{1,0:T(8,128)(2,1)S(1)}, bf16[192,384]{1,0:T(8,128)(2,1)S(1)}, u32[]{:S(2)}, u32[]{:S(2)}) collective-permute-start(bf16[192,384]{1,0:T(8,128)(2,1)S(1)} %convert_element_type.8.refs_4_), channel_id=1, source_target_pairs={{0,1},{1,0},{2,3},{3,2},{4,5},{5,4},{6,7},{7,6},{8,9},{9,8},{10,11... | collective-permute-start | bytes 442376 | tf_op jit(solution)/shard_map/ppermute | solution.py:710
  16.4 4.6 %copy-start.3 = (s32[6,8]{1,0:T(8,128)S(1)}, s32[6,8]{1,0:T(8,128)}, u32[]{:S(2)}) copy-start(s32[6,8]{1,0:T(8,128)} %refs_1_.9) | copy-start | bytes 580
  16.4 1.4 %collective-permute-start.3 = (f32[1,768]{1,0:T(1,128)S(1)}, f32[1,768]{1,0:T(1,128)S(1)}, u32[]{:S(2)}, u32[]{:S(2)}) collective-permute-start(f32[1,768]{1,0:T(1,128)S(1)} %reshape.31.refs_8_), channel_id=1, source_target_pairs={{0,1},{1,0},{2,3},{3,2},{4,5},{5,4},{6,7},{7,6},{8,9},{9,8},{10,11... | collective-permute-start | bytes 9224 | tf_op jit(solution)/shard_map/ppermute | solution.py:710
  22.6 1.5 %collective-permute-start.4 = (f32[432,96]{1,0:T(8,128)S(1)}, f32[432,96]{1,0:T(8,128)S(1)}, u32[]{:S(2)}, u32[]{:S(2)}) collective-permute-start(f32[432,96]{1,0:T(8,128)S(1)} %get-tuple-element.30), channel_id=1, source_target_pairs={{0,1},{1,0},{2,3},{3,2},{4,5},{5,4},{6,7},{7,6},{8,9},{9,8},{10,11... | collective-permute-start | bytes 497672 | tf_op jit(solution)/shard_map/ppermute | solution.py:710
  28.5 1.8 %collective-permute-start.5 = (bf16[1584,128]{1,0:T(8,128)(2,1)S(1)}, bf16[1584,128]{1,0:T(8,128)(2,1)S(1)}, u32[]{:S(2)}, u32[]{:S(2)}) collective-permute-start(bf16[1584,128]{1,0:T(8,128)(2,1)S(1)} %get-tuple-element.33), channel_id=1, source_target_pairs={{0,1},{1,0},{2,3},{3,2},{4,5},{5,4},{6,7},{7,6},{8,9},{9,8},{10,11... | collective-permute-start | bytes 1216520 | tf_op jit(solution)/shard_map/ppermute | solution.py:710
  32.1 21.0 %all-to-all-start.1 = ((bf16[8,312,128]{2,1,0:T(8,128)(2,1)}), bf16[8,312,128]{2,1,0:T(8,128)(2,1)S(1)}, u32[]{:S(2)}, u32[]{:S(2)}) async-start(bf16[8,312,128]{2,1,0:T(8,128)(2,1)} %bitcast.4), calls=%async_computation.1 | async-start | bytes 1277952 | tf_op jit(solution)/shard_map/all_to_all | solution.py:706
  35.7 5.6 %collective-permute-start.6 = (bf16[432,96]{1,0:T(8,128)(2,1)S(1)}, bf16[432,96]{1,0:T(8,128)(2,1)S(1)}, u32[]{:S(2)}, u32[]{:S(2)}) collective-permute-start(bf16[432,96]{1,0:T(8,128)(2,1)S(1)} %get-tuple-element.35), channel_id=1, source_target_pairs={{0,1},{1,0},{2,3},{3,2},{4,5},{5,4},{6,7},{7,6},{8,9},{9,8},{10,11... | collective-permute-start | bytes 248840 | tf_op jit(solution)/shard_map/ppermute | solution.py:710
  39.4 5.7 %collective-permute-start.7 = (f32[7,7,96]{2,1,0:T(8,128)S(1)}, f32[7,7,96]{2,1,0:T(8,128)S(1)}, u32[]{:S(2)}, u32[]{:S(2)}) collective-permute-start(f32[7,7,96]{2,1,0:T(8,128)S(1)} %shard_map.170.refs_1_), channel_id=1, source_target_pairs={{0,2},{2,0},{4,6},{6,4},{8,10},{10,8},{12,14},{14,12},{1,3},{3,1},... | collective-permute-start | bytes 56456 | tf_op jit(solution)/shard_map/ppermute | solution.py:715
  53.1 6.3 %collective-permute-start.10 = (bf16[208,128]{1,0:T(8,128)(2,1)S(1)}, bf16[208,128]{1,0:T(8,128)(2,1)S(1)}, u32[]{:S(2)}, u32[]{:S(2)}) collective-permute-start(bf16[208,128]{1,0:T(8,128)(2,1)S(1)} %shard_map.171.refs_0_), channel_id=1, source_target_pairs={{0,12},{2,14},{4,8},{6,10},{8,4},{10,6},{12,0},{14,2},{1,13},{3,15... | collective-permute-start | bytes 159752 | tf_op jit(solution)/shard_map/ppermute | solution.py:715
  54.4 6.0 %collective-permute-start.9 = (bf16[208,128]{1,0:T(8,128)(2,1)S(1)}, bf16[208,128]{1,0:T(8,128)(2,1)S(1)}, u32[]{:S(2)}, u32[]{:S(2)}) collective-permute-start(bf16[208,128]{1,0:T(8,128)(2,1)S(1)} %shard_map.171.refs_0_), channel_id=1, source_target_pairs={{0,8},{2,10},{4,12},{6,14},{8,0},{10,2},{12,4},{14,6},{1,9},{3,11}... | collective-permute-start | bytes 159752 | tf_op jit(solution)/shard_map/ppermute | solution.py:715
  55.3 5.2 %collective-permute-start.8 = (bf16[208,128]{1,0:T(8,128)(2,1)S(1)}, bf16[208,128]{1,0:T(8,128)(2,1)S(1)}, u32[]{:S(2)}, u32[]{:S(2)}) collective-permute-start(bf16[208,128]{1,0:T(8,128)(2,1)S(1)} %shard_map.171.refs_0_), channel_id=1, source_target_pairs={{0,4},{2,6},{4,0},{6,2},{8,12},{10,14},{12,8},{14,10},{1,5},{3,7},... | collective-permute-start | bytes 159752 | tf_op jit(solution)/shard_map/ppermute | solution.py:715
  61.1 5.1 %collective-permute-start.11 = (bf16[576,128]{1,0:T(8,128)(2,1)S(1)}, bf16[576,128]{1,0:T(8,128)(2,1)S(1)}, u32[]{:S(2)}, u32[]{:S(2)}) collective-permute-start(bf16[576,128]{1,0:T(8,128)(2,1)S(1)} %get-tuple-element.39.refs_5_.refs_0_), channel_id=1, source_target_pairs={{0,2},{2,0},{4,6},{6,4},{8,10},{10,8},{12,14},{14,12},{1,3},{3,1},... | collective-permute-start | bytes 442376 | tf_op jit(solution)/shard_map/ppermute | solution.py:715

commit v5 on v4

--- a/solution.py
+++ b/solution.py
@@ -283,8 +283,9 @@
             at = which * z.half
             own = pl.multiple_of(core * z.half, 16)
             far = pl.multiple_of((1 - core) * z.half, 16)
-            keep[at : at + z.half, :] = work[pl.ds(own, z.half), :].astype(BF16)
-            send[at : at + z.half, :] = work[pl.ds(far, z.half), :].astype(BF16)
+            for ref, half in ((keep, own), (send, far)):
+                ref[at : at + z.half, 0 : z.ch] = work[pl.ds(half, z.half), :].astype(BF16)
+                ref[at : at + z.half, z.ch : LANES] = jnp.zeros((z.half, z.extra), BF16)
         grown[...] = jnp.zeros_like(grown)
         fill_inner(z, grown, tile_data)
         start = jnp.broadcast_to(bias[...], (z.side * 8, z.ch))
@@ -294,7 +295,7 @@
             total = conv_row(z, grown, taps, row, start, False)
             out[pl.ds(pl.multiple_of(row * z.side * 8, 8), z.side * 8), :] = total
 
-    rows = shaped((2 * z.half, z.ch), BF16)
+    rows = shaped((2 * z.half, LANES), BF16)
     return call(
         body,
         (rows, rows, shaped((z.pixels * 8, z.ch), F32), shaped(slots.shape, jnp.int32)),
@@ -318,10 +319,11 @@
             for col, piece in enumerate(rim_row(z, grown, taps, row, start, False)):
                 at = (row * z.side + col) * z.tiles
                 whole[at : at + z.tiles, :] = piece[0 : z.tiles]
-        own[...] = whole[pl.ds(pl.multiple_of(core * z.half, 8), z.half), :]
-        far[...] = whole[pl.ds(pl.multiple_of((1 - core) * z.half, 8), z.half), :]
-
-    out = shaped((z.half, z.ch), F32)
+        for out, half in ((own, core), (far, 1 - core)):
+            out[:, 0 : z.ch] = whole[pl.ds(pl.multiple_of(half * z.half, 8), z.half), :]
+            out[:, z.ch : LANES] = jnp.zeros((z.half, z.extra), F32)
+
+    out = shaped((z.half, LANES), F32)
     return call(
         body,
         (out, out),
@@ -336,38 +338,53 @@
 DOWN = (((0,), (0,)), ((), ()))
 
 
-def join(first, own, far):
-    return jnp.where(
-        first, jnp.concatenate([own, far], axis=1), jnp.concatenate([far, own], axis=1)
-    )
-
-
-def both_vectors(z, first, v_own, v_far, index):
-    at = index * z.ch
-    return join(first, v_own[:, at : at + z.ch], v_far[:, at : at + z.ch])
+def arrange_weights(z, w_in, w_out):
+    hid = z.hidden
+
+    def body(w_in, w_out, in_mine, out_mine, in_theirs, out_theirs):
+        first = lax.axis_index("sub") == 0
+        for w, mine, theirs in ((w_in, in_mine, in_theirs), (w_out, out_mine, out_theirs)):
+            low, high = w[0 : z.ch, :], w[z.ch : 2 * z.ch, :]
+            own = jnp.where(first, low, high).astype(BF16)
+            far = jnp.where(first, high, low).astype(BF16)
+            empty = jnp.zeros((z.extra, hid), BF16)
+            for out, blocks in ((mine, (own, far)), (theirs, (far, own))):
+                for place, block in enumerate(blocks):
+                    at = place * LANES
+                    out[at : at + z.ch, :] = block
+                    out[at + z.ch : at + LANES, :] = empty
+
+    return call(body, (shaped((2 * LANES, hid), BF16),) * 4, [w_in, w_out])
 
 
 def block_pass(z, spatial, rows, w_in, w_out, vectors):
     hid = z.hidden
-    wide = 2 * z.ch
-
-    def body(sp_own, sp_far, row_own, row_far, wi_own, wi_far, wo_own, wo_far, v_own,
-             v_far, g_own, block_own, block_far, keep, send, normed_s, branch_s, pre_s, gact_s, act_s, gpre_s, xhat_s, inv_s):
-        first = lax.axis_index("sub") == 0
-        gain, shift, b_out, layer_scale = [
-            both_vectors(z, first, v_own, v_far, index) for index in range(4)
-        ]
-        flat = join(first, sp_own[...], sp_far[...])
-        centre = flat - jnp.sum(flat, axis=1, keepdims=True) * (1.0 / wide)
-        var = jnp.sum(centre * centre, axis=1, keepdims=True) * (1.0 / wide)
+    wide = 2 * LANES
+    every = 2 * z.ch
+
+    def body(sp_own, sp_far, row_own, row_far, wi_own, wi_far, wo_own, wo_far, v_own, v_far,
+             g_own, block_own, block_far, keep, send, normed_s, branch_s, pre_s, gact_s, act_s,
+             gpre_s, xhat_s, inv_s):
+        def vector(index):
+            at = index * z.ch
+            empty = jnp.zeros((1, z.extra), F32)
+            own, far = v_own[:, at : at + z.ch], v_far[:, at : at + z.ch]
+            return jnp.concatenate([own, empty, far, empty], axis=1)
+
+        gain, shift, b_out, layer_scale = [vector(index) for index in range(4)]
+        lanes = lax.broadcasted_iota(jnp.int32, (1, wide), 1)
+        flat = jnp.concatenate([sp_own[...], sp_far[...]], axis=1)
+        centre = flat - jnp.sum(flat, axis=1, keepdims=True) * (1.0 / every)
+        centre = jnp.where(lanes % LANES < z.ch, centre, 0.0)
+        var = jnp.sum(centre * centre, axis=1, keepdims=True) * (1.0 / every)
         inverse = lax.rsqrt(var + eps_norm)
         xhat = centre * inverse
         xhat_s[...] = xhat
         inv_s[...] = inverse
         normed_s[...] = (xhat * gain + shift).astype(BF16)
         normed = normed_s[...]
-        cot = join(first, row_own[z.half :, :].astype(F32), row_far[z.half :, :].astype(F32))
-        branch_s[...] = (layer_scale * cot).astype(BF16)
+        cot = jnp.concatenate([row_own[z.half :, :], row_far[z.half :, :]], axis=1)
+        branch_s[...] = (layer_scale * cot.astype(F32)).astype(BF16)
         g_branch = branch_s[...]
         for side, (wi, wo, vec) in enumerate(((wi_own, wo_own, v_own), (wi_far, wo_far, v_far))):
             at = side * hid
@@ -375,41 +392,34 @@
             pre_s[:, at : at + hid] = jnp.dot(normed, wi[...], preferred_element_type=F32) + b_in
             gact_s[:, at : at + hid] = jnp.dot(g_branch, wo[...], preferred_element_type=F32)
 
-        @pl.loop(0, z.half // 16)
+        @pl.loop(0, z.half // 48, unroll=1)
         def _(step):
-            spot = pl.ds(pl.multiple_of(step * 16, 16), 16)
-            pre = pre_s[spot, :]
-            cdf = 0.5 * (1.0 + lax.erf(pre * root_half))
-            act_s[spot, :] = (pre * cdf).astype(BF16)
-            slope = cdf + pre * jnp.exp(-0.5 * pre * pre) * inv_root_tau
-            gpre_s[spot, :] = (gact_s[spot, :] * slope).astype(BF16)
+            spot = pl.ds(pl.multiple_of(step * 48, 48), 48)
+            for low in range(0, 2 * hid, 256):
+                part = slice(low, low + 256)
+                pre = pre_s[spot, part]
+                cdf = 0.5 * (1.0 + lax.erf(pre * root_half))
+                act_s[spot, part] = (pre * cdf).astype(BF16)
+                slope = cdf + pre * jnp.exp(-0.5 * pre * pre) * inv_root_tau
+                gpre_s[spot, part] = (gact_s[spot, part] * slope).astype(BF16)
 
         g_normed = lax.dot_general(
             gpre_s[:, 0:hid], wi_own[...], ACROSS, preferred_element_type=F32
         ) + lax.dot_general(gpre_s[:, hid:], wi_far[...], ACROSS, preferred_element_type=F32)
         xhat = xhat_s[...]
         leading = g_normed * gain
-        mean_h = jnp.sum(leading, axis=1, keepdims=True) * (1.0 / wide)
-        mean_hx = jnp.sum(leading * xhat, axis=1, keepdims=True) * (1.0 / wide)
-        g_rows = inv_s[...] * (leading - mean_h - xhat * mean_hx)
-        branch = (
+        mean_h = jnp.sum(leading, axis=1, keepdims=True) * (1.0 / every)
+        mean_hx = jnp.sum(leading * xhat, axis=1, keepdims=True) * (1.0 / every)
+        g_rows = (inv_s[...] * (leading - mean_h - xhat * mean_hx)).astype(BF16)
+        g_own[...] = g_rows[:, 0:LANES]
+        send[0 : z.half, :] = g_rows[:, LANES:]
+        branch = layer_scale * (
             lax.dot_general(act_s[:, 0:hid], wo_own[...], ACROSS, preferred_element_type=F32)
             + lax.dot_general(act_s[:, hid:], wo_far[...], ACROSS, preferred_element_type=F32)
             + b_out
         )
-        inner = join(
-            first, row_own[0 : z.half, :].astype(F32), row_far[0 : z.half, :].astype(F32)
-        )
-        block = inner + layer_scale * branch
-
-        def part(value, mine):
-            low, high = value[:, 0 : z.ch], value[:, z.ch :]
-            return jnp.where(first == mine, low, high).astype(BF16)
-
-        g_own[...] = part(g_rows, True)
-        block_own[...] = part(block, True)
-        send[0 : z.half, 0 : z.ch] = part(g_rows, False)
-        block_far[...] = part(block, False)
+        block_own[...] = (row_own[0 : z.half, :].astype(F32) + branch[:, 0:LANES]).astype(BF16)
+        block_far[...] = (row_far[0 : z.half, :].astype(F32) + branch[:, LANES:]).astype(BF16)
         for side in range(2):
             at = side * hid
             ref, low = (keep, 0) if side == 0 else (send, z.half)
@@ -418,11 +428,12 @@
                     left, right[:, at : at + hid], DOWN, preferred_element_type=F32
                 )
                 for group in range(hid // LANES):
-                    lanes = slice(group * LANES, (group + 1) * LANES)
-                    ref[low : low + wide, :] = grad[:, lanes].astype(ref.dtype)
-                    low += wide
-
-    rows_out = shaped((z.half, z.ch), BF16)
+                    part = slice(group * LANES, (group + 1) * LANES)
+                    for place in (0, LANES) if side == 0 else (LANES, 0):
+                        ref[low : low + z.ch, :] = grad[place : place + z.ch, part].astype(ref.dtype)
+                        low += z.ch
+
+    rows_out = shaped((z.half, LANES), BF16)
     return call(
         body,
         (
@@ -456,7 +467,7 @@
 
 def second_strips(z, slots, g_own, keep, received):
     def body(slots, g_own, keep, received, out, plain, strips, box):
-        both_halves(z, plain, g_own[...], received[0 : z.half, 0 : z.ch])
+        both_halves(z, plain, g_own[:, 0 : z.ch], received[0 : z.half, 0 : z.ch])
         for owner in range(z.owners):
             at = owner * z.share
             low = z.half + at
@@ -491,7 +502,7 @@
         empty = jnp.zeros((z.wide * z.wide, z.ch), F32)
         for tile in range(z.tiles, 8):
             grown[pl.ds(tile, z.wide * z.wide, stride=8), :] = empty
-        both_halves(z, plain, g_own[...], received[0 : z.half, 0 : z.ch])
+        both_halves(z, plain, g_own[:, 0 : z.ch], received[0 : z.half, 0 : z.ch])
         g_field[...] = jnp.zeros_like(g_field)
         for tile in range(z.tiles):
             g_field[pl.ds(tile, z.pixels, stride=8), :] = plain[
@@ -550,12 +561,12 @@
 
 def second_inner(z, g_own, received, block, cotangent, taps):
     def body(g_own, received, block_own, block_far, cotangent, taps, out, block_out, plain, grown, cot):
-        both_halves(z, plain, block_own[...], block_far[...])
+        both_halves(z, plain, block_own[:, 0 : z.ch], block_far[:, 0 : z.ch])
         for tile in range(z.tiles):
             for row in range(z.side):
                 spot = pl.ds(row * z.side * z.tiles + tile, z.side, stride=z.tiles)
                 block_out[tile, row] = plain[spot, :].astype(BF16)
-        both_halves(z, plain, g_own[...], received[0 : z.half, 0 : z.ch])
+        both_halves(z, plain, g_own[:, 0 : z.ch], received[0 : z.half, 0 : z.ch])
         grown[...] = jnp.zeros_like(grown)
         for tile in range(z.tiles):
             for row in range(z.side):
@@ -582,8 +593,25 @@
     )
 
 
-def second_rim(z, slots, tissue, inbox, inner, taps, after):
-    def body(slots, tissue, inbox, inner, taps, out, box, flat, grown, totals):
+def second_rim(z, slots, tissue, inbox, inner, taps, messages, after):
+    count = len(messages)
+
+    def body(slots, tissue, inbox, inner, taps, *refs):
+        messages, (out, *refs) = refs[:count], refs[count:]
+        if count:
+            grad_taps, box, flat, grown, totals, work = refs
+            line = lax.axis_index("tiles") // 2
+            for step, message in enumerate(messages):
+                at = pl.multiple_of(jnp.bitwise_xor(line, step) * 56, 8)
+                work[pl.ds(at, 49), :] = message[z.taps_at : z.taps_at + 49, 0 : z.ch].astype(F32)
+            for a in range(7):
+                total = work[a * 7 : a * 7 + 7, :]
+                for place in range(1, count):
+                    low = place * 56 + a * 7
+                    total = total + work[low : low + 7, :]
+                grad_taps[a] = total
+        else:
+            box, flat, grown, totals = refs
         box[...] = inbox[...].astype(F32)
         assemble(z, box, z.box2, z.halo_at, slots, tissue, flat, grown)
         for row in range(z.side):
@@ -595,18 +623,18 @@
                 spot = pl.ds(row * z.side * 8 + tile, z.side, stride=8)
                 out[tile, row] = totals[spot, :].astype(BF16)
 
+    outs = (shaped((z.tiles, z.side, z.side, z.ch), BF16), shaped((7, 7, z.ch), F32))
+    scratch = [
+        boxes(z, z.box2),
+        flat_strips(z),
+        field(z),
+        pltpu.VMEM((z.pixels * 8, z.ch), F32),
+        pltpu.VMEM((count * 56, z.ch), F32),
+    ]
+    if not count:
+        outs, scratch = outs[0], scratch[:-1]
     return call(
-        body,
-        shaped((z.tiles, z.side, z.side, z.ch), BF16),
-        [slots, tissue, inbox, inner, taps],
-        2,
-        [
-            boxes(z, z.box2),
-            flat_strips(z),
-            field(z),
-            pltpu.VMEM((z.pixels * 8, z.ch), F32),
-        ],
-        after=after,
+        body, outs, [slots, tissue, inbox, inner, taps, *messages], 2, scratch, after=after
     )
 
 
@@ -628,77 +656,76 @@
     count = len(messages)
 
     def body(*refs):
-        messages, (out, taps, work) = refs[:count], refs[count:]
+        messages, (out,) = refs[:count], refs[count:]
         line = lax.axis_index("tiles") // 2
         for step, message in enumerate(messages):
-            place = jnp.bitwise_xor(line, step)
-            at = pl.multiple_of(place * z.share, 16)
+            at = pl.multiple_of(jnp.bitwise_xor(line, step) * z.share, 16)
             out[pl.ds(at, z.share), :] = message[0 : z.share, :]
-            at = pl.multiple_of(place * 56, 8)
-            work[pl.ds(at, 49), :] = message[z.taps_at : z.taps_at + 49, 0 : z.ch].astype(F32)
-        for a in range(7):
-            total = work[a * 7 : a * 7 + 7, :]
-            for place in range(1, count):
-                low = place * 56 + a * 7
-                total = total + work[low : low + 7, :]
-            taps[a] = total
-
+
+    return call(body, shaped((count * z.share, LANES), BF16), messages)
+
+
+def finish_share(z, grads, owner, share):
+    core = lax.axis_index("sub")
+    wide = 2 * z.ch
+    groups = z.hidden // LANES
+    row, stop = owner * z.share, (owner + 1) * z.share
+    while row < stop:
+        group, place = divmod(row, wide)
+        side, place = divmod(place, z.ch)
+        count = min(stop - row, z.ch - place)
+        at = row - owner * z.share
+        block = core if side == 0 else 1 - core
+        spot = pl.ds(pl.multiple_of(block * z.ch, 8) + place, count)
+        low = group % groups * LANES
+        grads[group // groups][spot, low : low + LANES] = share(at, count)
+        row += count
+
+
+def finish(z, inbox, taps, scale):
+    groups = z.hidden // LANES
+
+    def body(inbox, taps_own, taps_far, grad_in, grad_out, grad_taps, work):
+        grad_taps[...] = taps_own[...] + taps_far[...]
+        for owner in range(z.owners):
+            at = owner * z.box3
+            work[owner * z.share : (owner + 1) * z.share, :] = (
+                inbox[at : at + z.share, :].astype(F32) * scale
+            )
+        core = lax.axis_index("sub")
+        for index, grad in enumerate((grad_in, grad_out)):
+            for group in range(groups):
+                for side, block in enumerate((core, 1 - core)):
+                    low = ((index * groups + group) * 2 + side) * z.ch
+                    spot = pl.ds(pl.multiple_of(block * z.ch, 8), z.ch)
+                    lanes = slice(group * LANES, (group + 1) * LANES)
+                    grad[spot, lanes] = work[low : low + z.ch, :]
+
+    out = shaped((2 * z.ch, z.hidden), F32)
     return call(
         body,
-        (shaped((count * z.share, LANES), BF16), shaped((7, 7, z.ch), F32)),
-        messages,
-        scratch=[pltpu.VMEM((count * 56, z.ch), F32)],
+        (out, out, shaped((7, 7, z.ch), F32)),
+        [inbox, *taps],
+        scratch=[pltpu.VMEM((z.weight_rows, LANES), F32)],
     )
 
 
 def finish_columns(z, own, far, scale):
-    hid = z.hidden
-    wide = 2 * z.ch
-    groups = hid // LANES
-
     def body(own, far, grad_in, grad_out):
         first = lax.axis_index("tiles") % 2 == 0
         for owner in range(z.owners):
-            row = owner * z.share
-            stop = row + z.share
-            while row < stop:
-                group, place = divmod(row, wide)
-                count = min(stop - row, wide - place)
-                at = owner // 2 * z.share + row - owner * z.share
-                out = grad_in if group < groups else grad_out
-                low = group % groups * LANES
-                mine, other = own[at : at + count, :], far[at : at + count, :]
-                value = jnp.where(first == (owner % 2 == 0), mine.astype(F32), other.astype(F32))
-                out[place : place + count, low : low + LANES] = value * scale
-                row += count
-
-    out = shaped((wide, hid), F32)
+
+            def share(at, count, owner=owner):
+                low = owner // 2 * z.share + at
+                mine = own[low : low + count, :].astype(F32)
+                other = far[low : low + count, :].astype(F32)
+                pair = (mine, other) if owner % 2 == 0 else (other, mine)
+                return jnp.where(first, *pair) * scale
+
+            finish_share(z, (grad_in, grad_out), owner, share)
+
+    out = shaped((2 * z.ch, z.hidden), F32)
     return call(body, (out, out), [own, far])
-
-
-def finish(z, inbox, taps, scale):
-    hid = z.hidden
-    wide = 2 * z.ch
-    groups = hid // LANES
-
-    def body(inbox, taps_own, taps_far, grad_in, grad_out, grad_taps):
-        grad_taps[...] = taps_own[...] + taps_far[...]
-        for owner in range(z.owners):
-            row = owner * z.share
-            stop = row + z.share
-            while row < stop:
-                group, place = divmod(row, wide)
-                count = min(stop - row, wide - place)
-                at = owner * z.box3 + row - owner * z.share
-                out = grad_in if group < groups else grad_out
-                low = group % groups * LANES
-                out[place : place + count, low : low + LANES] = (
-                    inbox[at : at + count, :].astype(F32) * scale
-                )
-                row += count
-
-    out = shaped((wide, hid), F32)
-    return call(body, (out, out, shaped((7, 7, z.ch), F32)), [inbox, *taps])
 
 
 def exchange_tiles(z, box):
@@ -746,15 +773,14 @@
     outbox, slots = first_strips(z, neighbour, tile_data)
     inbox = exchange_tiles(z, outbox)
 
-    w_in16 = w_in.astype(BF16)
-    w_out16 = w_out.T.astype(BF16)
+    in_mine, out_mine, in_theirs, out_theirs = arrange_weights(z, w_in, w_out.T)
     vectors = jnp.concatenate([layer_norm_gain, layer_norm_bias, b_out, layer_scale, b_in])
     vectors = vectors.reshape(1, -1)
     rows_keep, rows_send, inner, slots = local_part(
         z, slots, tile_data, cotangent, kernel, conv_bias.reshape(1, z.ch)
     )
-    w_in_both = (w_in16, swap_sub(w_in16))
-    w_out_both = (w_out16, swap_sub(w_out16))
+    w_in_both = (in_mine, swap_sub(in_theirs))
+    w_out_both = (out_mine, swap_sub(out_theirs))
     v_both = (vectors, swap_sub(vectors))
     rows_both = (rows_keep, swap_sub(rows_send))
     ready = (rows_both[1], w_in_both[1], w_out_both[1], v_both[1])
@@ -773,14 +799,16 @@
         message = share_message(z, inbox2, taps_both, (inner2,))
         steps = range(2, z.owners, 2)
         messages = [message] + [swap_tiles(z, message, step) for step in steps]
-        own, grad_kernel = column(z, messages)
+        own = column(z, messages)
         far = swap_tiles(z, own, 1)
-        tile_grad = second_rim(z, slots, tissue, inbox2, inner2, kernel, (own,))
+        tile_grad, grad_kernel = second_rim(
+            z, slots, tissue, inbox2, inner2, kernel, messages, (own,)
+        )
         grad_in, grad_out = finish_columns(z, own, far, scale)
     else:
         taps_own, taps_far = sum_tiles(z, taps)
         inbox3 = exchange_tiles(z, sum_shares(z, inbox2, (taps_own, inner2)))
-        tile_grad = second_rim(z, slots, tissue, inbox2, inner2, kernel, ())
+        tile_grad = second_rim(z, slots, tissue, inbox2, inner2, kernel, (), ())
         grad_in, grad_out, grad_kernel = finish(z, inbox3, (taps_own, taps_far), scale)
     return block_out, tile_grad, grad_in, grad_out.T, grad_kernel
 

time: 67.5 us -> 65.4 us (0.969)
  Pallas kernels: 25.4 us -> 24.1 us
    pallas_call x11 -> x12, Pallas kernels: 25.4 us -> 24.1 us  [call(): pl.pallas_call(run, out_shape=outs, in_specs=[pl.BlockSpec(memory_space=s...]
  transfers between devices with their start and end apart: 14 -> 14, of which waited for: 8 -> 8; matrix products, arithmetic and copies ran while one was open for 0% -> 0% of each run, Pallas kernels for 21% -> 22%
where the time goes in v5:
time: 65.4 us; the launch traced here: 65.1 us
  Pallas kernels  24.1 us (37%)
  starting transfers between devices  20.4 us (31%)
  waiting for transfers between devices  18.9 us (29%)
  local copies, waits for them, and re-layouts  0.84 us (1%)
  between operations  0.81 us (1%)
    pallas_call x12, Pallas kernels, call(): pl.pallas_call(run, out_shape=outs, in_specs=[pl.BlockSpec(memory_space=s...  24.1 us
    all_to_all x2, starting transfers between devices, exchange_tiles(): lax.all_to_all(boxes, 'tiles', split_axis=0, concat_axis=0, tiled=True)  11 us
    all_to_all x2, waiting for transfers between devices, exchange_tiles(): lax.all_to_all(boxes, 'tiles', split_axis=0, concat_axis=0, tiled=True)  10.8 us
    ppermute x5, starting transfers between devices, swap_tiles(): return lax.ppermute(piece, 'tiles', pairs)  7.77 us
    ppermute x5, waiting for transfers between devices, swap_tiles(): return lax.ppermute(piece, 'tiles', pairs)  4.27 us
    ppermute x7, waiting for transfers between devices, swap_sub(): return lax.ppermute(piece, 'sub', [(0, 1), (1, 0)])  3.91 us
    ppermute x7, starting transfers between devices, swap_sub(): return lax.ppermute(piece, 'sub', [(0, 1), (1, 0)])  1.64 us
  transfers between devices with their start and end apart: 14, of which 8 were waited for; matrix products, arithmetic and copies ran while one was open for 0% of the time, Pallas kernels for 22%

profile of v5, /device:TPU:0, one launch (start us, length us, event | category | flops | bytes accessed | tf_op | source)
XLA Modules:
  0.0 65.1 jit_solution(3245190124051607849)
XLA Ops:
  0.6 2.2 %shard_map.164 = (bf16[1344,128]{1,0:T(8,128)(2,1)}, s32[144]{0:T(256)}) custom-call(s32[6,8]{1,0:T(8,128)} %refs_0_.2, bf16[6,12,12,96]{3,2,1,0:T(8,128)(2,1)} %refs_3_.3), custom_call_target="tpu_custom_call" | custom-call | bytes 166080 | tf_op jit(solution)/shard_map/pallas_call | solution.py:35
  2.9 0.0 copy-start
  2.9 0.0 copy-start.1
  2.9 0.0 copy-start.2
  2.9 7.4 %all-to-all-start = ((bf16[8,168,128]{2,1,0:T(8,128)(2,1)}), bf16[8,168,128]{2,1,0:T(8,128)(2,1)S(1)}, u32[]{:S(2)}, u32[]{:S(2)}) async-start(bf16[8,168,128]{2,1,0:T(8,128)(2,1)} %bitcast.13), calls=%async_computation | async-start | bytes 688128 | tf_op jit(solution)/shard_map/all_to_all | solution.py:733
  10.3 0.0 copy-start.6
  10.3 0.0 copy-start.7
  10.3 0.0 copy-done
  10.3 0.0 copy-done.1
  10.3 0.0 copy-done.2
  10.4 0.6 copy-done.6
  11.0 0.0 copy-done.7
  11.0 0.0 copy-start.3
  11.0 0.0 copy-start.4
  11.0 4.3 %shard_map.165 = (bf16[864,128]{1,0:T(8,128)(2,1)S(1)}, bf16[864,128]{1,0:T(8,128)(2,1)S(1)}, f32[1152,96]{1,0:T(8,128)S(1)}, s32[144]{0:T(256)S(1)}) custom-call(s32[144]{0:T(256)S(1)} %copy-done.6, bf16[6,12,12,96]{3,2,1,0:T(8,128)(2,1)S(1)} %copy-done, bf16[6,12,12,96]{3,2,1,0:T(8,128)(2,1)S(1)} %copy-done.1, f32[7,7,96]{2,1,0:T(8,128)S(1)} %copy-done.2, ...), custom_call_target="tpu_custom_call" | custom-call | flops 8128512 | bytes 351552 | tf_op jit(solution)/shard_map/pallas_call | solution.py:35
  15.3 0.1 collective-permute-start
  15.4 0.0 copy-done.3
  15.4 0.0 copy-done.4
  15.4 0.0 copy-start.12
  15.4 0.7 %shard_map.166 = (bf16[256,384]{1,0:T(8,128)(2,1)S(1)}, bf16[256,384]{1,0:T(8,128)(2,1)S(1)}, bf16[256,384]{1,0:T(8,128)(2,1)}, bf16[256,384]{1,0:T(8,128)(2,1)S(1)}) custom-call(f32[192,384]{1,0:T(8,128)S(1)} %copy-done.3, f32[192,384]{1,0:T(8,128)S(1)} %bitcast.11), custom_call_target="tpu_custom_call" | custom-call | bytes 589824 | tf_op jit(solution)/shard_map/pallas_call | solution.py:35
  16.1 0.0 copy-start.8
  16.1 0.0 copy-start.9
  16.1 0.0 copy-start.10
  16.1 0.0 copy-start.11
  16.1 0.5 collective-permute-start.1
  16.7 0.1 collective-permute-start.2
  16.8 0.0 copy-done.12
  16.8 0.1 copy-done.8
  16.8 0.0 copy-done.9
  16.8 0.0 copy-done.10
  16.8 0.0 copy-done.11
  16.8 0.1 concatenate.3
  16.9 0.5 collective-permute-start.3
  17.5 0.8 %collective-permute-done.3.refs_8_.refs_9_ = f32[1,768]{1,0:T(1,128)S(1)} collective-permute-done((f32[1,768]{1,0:T(1,128)S(1)}, f32[1,768]{1,0:T(1,128)S(1)}, u32[]{:S(2)}, u32[]{:S(2)}) %collective-permute-start.3) | collective-permute-done | bytes 3104 | tf_op jit(solution)/shard_map/ppermute | solution.py:737
  18.3 0.0 collective-permute-done.1.refs_6_.refs_5_
  18.3 0.0 collective-permute-done.2.refs_7_
  18.3 0.0 collective-permute-done.refs_5_.refs_3_
  18.3 2.7 %all-to-all-done = bf16[8,168,128]{2,1,0:T(8,128)(2,1)S(1)} async-done(((bf16[8,168,128]{2,1,0:T(8,128)(2,1)}), bf16[8,168,128]{2,1,0:T(8,128)(2,1)S(1)}, u32[]{:S(2)}, u32[]{:S(2)}) %all-to-all-start) | async-done | bytes 344096 | tf_op jit(solution)/shard_map/all_to_all | solution.py:733
  21.0 0.0 copy-done.5
  21.0 1.7 %shard_map.167 = (f32[432,128]{1,0:T(8,128)S(1)}, f32[432,128]{1,0:T(8,128)S(1)}) custom-call(s32[144]{0:T(256)S(1)} %get-tuple-element.29.refs_0_, s32[6,8]{1,0:T(8,128)S(1)} %copy-done.5, bf16[1344,128]{1,0:T(8,128)(2,1)S(1)} %bitcast.9, f32[1152,96]{1,0:T(8,128)S(1)} %get-tuple-element.31.refs_3_, f32[7,7,96]{2,1,0:T(8,128)S(1)} %copy-done.2, ...), custom_call_target="tpu_custom_call" | custom-call | bytes 806016 | tf_op jit(solution)/shard_map/pallas_call | solution.py:35
  22.7 0.1 collective-permute-start.4
  22.7 1.5 %collective-permute-done.4.refs_1_ = f32[432,128]{1,0:T(8,128)S(1)} collective-permute-done((f32[432,128]{1,0:T(8,128)S(1)}, f32[432,128]{1,0:T(8,128)S(1)}, u32[]{:S(2)}, u32[]{:S(2)}) %collective-permute-start.4) | collective-permute-done | bytes 221216 | tf_op jit(solution)/shard_map/ppermute | solution.py:737
  24.2 2.8 %shard_map.168 = (bf16[432,128]{1,0:T(8,128)(2,1)S(1)}, bf16[432,128]{1,0:T(8,128)(2,1)S(1)}, bf16[432,128]{1,0:T(8,128)(2,1)S(1)}, f32[1152,128]{1,0:T(8,128)S(1)}, bf16[1584,128]{1,0:T(8,128)(2,1)S(1)}) custom-call(f32[432,128]{1,0:T(8,128)S(1)} %get-tuple-element.35.refs_0_, f32[432,128]{1,0:T(8,128)S(1)} %collective-permute-done.4.refs_1_, ...), custom_call_target="tpu_custom_call" | custom-call | flops 1019215872 | bytes 1677312 | tf_op jit(solution)/shard_map/pallas_call | solution.py:35
  27.0 0.2 collective-permute-start.5
  27.2 1.6 %collective-permute-done.5.refs_1_.refs_3_.refs_5_ = bf16[1584,128]{1,0:T(8,128)(2,1)S(1)} collective-permute-done((bf16[1584,128]{1,0:T(8,128)(2,1)S(1)}, bf16[1584,128]{1,0:T(8,128)(2,1)S(1)}, u32[]{:S(2)}, u32[]{:S(2)}) %collective-permute-start.5) | collective-permute-done | bytes 405536 | tf_op jit(solution)/shard_map/ppermute | solution.py:737
  28.8 1.8 %shard_map.170 = bf16[2496,128]{1,0:T(8,128)(2,1)} custom-call(s32[144]{0:T(256)S(1)} %get-tuple-element.29.refs_0_, bf16[432,128]{1,0:T(8,128)(2,1)S(1)} %get-tuple-element.40.refs_0_.refs_1_.refs_4_, f32[1152,128]{1,0:T(8,128)S(1)} %get-tuple-element.45.refs_2_, bf16[1584,128]{1,0:T(8,128)(2,1)S(1)} %collective-permute-done.5.refs_1_.refs_3_.refs_5_), custom_call_target="tpu_custom_call" | custom-call | bytes 1106496 | tf_op jit(solution)/shard_map/pallas_call | solution.py:35
  30.6 3.6 %all-to-all-start.1 = ((bf16[8,312,128]{2,1,0:T(8,128)(2,1)}), bf16[8,312,128]{2,1,0:T(8,128)(2,1)S(1)}, u32[]{:S(2)}, u32[]{:S(2)}) async-start(bf16[8,312,128]{2,1,0:T(8,128)(2,1)} %bitcast.4), calls=%async_computation.1 | async-start | bytes 1277952 | tf_op jit(solution)/shard_map/all_to_all | solution.py:733
  34.2 0.2 collective-permute-start.6
  34.4 3.5 %shard_map.171.refs_1_ = f32[7,7,96]{2,1,0:T(8,128)S(1)} custom-call(s32[144]{0:T(256)S(1)} %get-tuple-element.29.refs_0_, s32[6,8]{1,0:T(8,128)S(1)} %copy-done.5, bf16[1344,128]{1,0:T(8,128)(2,1)S(1)} %bitcast.10, bf16[6,12,12,96]{3,2,1,0:T(8,128)(2,1)S(1)} %copy-done, bf16[432,128]{1,0:T(8,128)(2,1)S(1)} %get-tuple-element.40.refs_0_.refs_1_.refs_4_, ...), custom_call_target="tpu_custom_call" | custom-call | flops 8128512 | bytes 1026816 | tf_op jit(solution)/shard_map/pallas_call | solution.py:35
  37.9 1.9 %collective-permute-start.7 = (f32[7,7,96]{2,1,0:T(8,128)S(1)}, f32[7,7,96]{2,1,0:T(8,128)S(1)}, u32[]{:S(2)}, u32[]{:S(2)}) collective-permute-start(f32[7,7,96]{2,1,0:T(8,128)S(1)} %shard_map.171.refs_1_), channel_id=1, source_target_pairs={{0,2},{2,0},{4,6},{6,4},{8,10},{10,8},{12,14},{14,12},{1,3},{3,1},... | collective-permute-start | bytes 56456 | tf_op jit(solution)/shard_map/ppermute | solution.py:742
  39.8 0.0 collective-permute-done.6.refs_3_
  39.8 3.7 %shard_map.169 = (f32[1152,96]{1,0:T(8,128)S(1)}, bf16[6,12,12,96]{3,2,1,0:T(8,128)(2,1)}) custom-call(bf16[432,128]{1,0:T(8,128)(2,1)S(1)} %get-tuple-element.40.refs_0_.refs_1_.refs_4_, bf16[1584,128]{1,0:T(8,128)(2,1)S(1)} %collective-permute-done.5.refs_1_.refs_3_.refs_5_, bf16[432,128]{1,0:T(8,128)(2,1)S(1)} %get-tuple-element.42.refs_2_, ...), custom_call_target="tpu_custom_call" | custom-call | flops 8128512 | bytes 921984 | tf_op jit(solution)/shard_map/pallas_call | solution.py:35
  43.5 0.0 collective-permute-done.7.refs_2_
  43.5 8.1 %all-to-all-done.1 = bf16[8,312,128]{2,1,0:T(8,128)(2,1)S(1)} async-done(((bf16[8,312,128]{2,1,0:T(8,128)(2,1)}), bf16[8,312,128]{2,1,0:T(8,128)(2,1)S(1)}, u32[]{:S(2)}, u32[]{:S(2)}) %all-to-all-start.1) | async-done | bytes 639008 | tf_op jit(solution)/shard_map/all_to_all | solution.py:733
  51.7 1.3 %collective-permute-start.10 = (bf16[208,128]{1,0:T(8,128)(2,1)S(1)}, bf16[208,128]{1,0:T(8,128)(2,1)S(1)}, u32[]{:S(2)}, u32[]{:S(2)}) collective-permute-start(bf16[208,128]{1,0:T(8,128)(2,1)S(1)} %shard_map.172.refs_0_.refs_5_), channel_id=1, source_target_pairs={{0,12},{2,14},{4,8},{6,10},{8,4},{10,6},{12,0},{14,2},{1,13},{3,15... | collective-permute-start | bytes 159752 | tf_op jit(solution)/shard_map/ppermute | solution.py:742
  52.9 0.9 %collective-permute-start.9 = (bf16[208,128]{1,0:T(8,128)(2,1)S(1)}, bf16[208,128]{1,0:T(8,128)(2,1)S(1)}, u32[]{:S(2)}, u32[]{:S(2)}) collective-permute-start(bf16[208,128]{1,0:T(8,128)(2,1)S(1)} %shard_map.172.refs_0_.refs_5_), channel_id=1, source_target_pairs={{0,8},{2,10},{4,12},{6,14},{8,0},{10,2},{12,4},{14,6},{1,9},{3,11}... | collective-permute-start | bytes 159752 | tf_op jit(solution)/shard_map/ppermute | solution.py:742
  53.8 2.3 %collective-permute-start.8 = (bf16[208,128]{1,0:T(8,128)(2,1)S(1)}, bf16[208,128]{1,0:T(8,128)(2,1)S(1)}, u32[]{:S(2)}, u32[]{:S(2)}) collective-permute-start(bf16[208,128]{1,0:T(8,128)(2,1)S(1)} %shard_map.172.refs_0_.refs_5_), channel_id=1, source_target_pairs={{0,4},{2,6},{4,0},{6,2},{8,12},{10,14},{12,8},{14,10},{1,5},{3,7},... | collective-permute-start | bytes 159752 | tf_op jit(solution)/shard_map/ppermute | solution.py:742
  56.1 1.9 %collective-permute-done.10.refs_3_.refs_8_ = bf16[208,128]{1,0:T(8,128)(2,1)S(1)} collective-permute-done((bf16[208,128]{1,0:T(8,128)(2,1)S(1)}, bf16[208,128]{1,0:T(8,128)(2,1)S(1)}, u32[]{:S(2)}, u32[]{:S(2)}) %collective-permute-start.10) | collective-permute-done | bytes 53280 | tf_op jit(solution)/shard_map/ppermute | solution.py:742
  58.0 1.0 %collective-permute-done.9.refs_2_.refs_7_ = bf16[208,128]{1,0:T(8,128)(2,1)S(1)} collective-permute-done((bf16[208,128]{1,0:T(8,128)(2,1)S(1)}, bf16[208,128]{1,0:T(8,128)(2,1)S(1)}, u32[]{:S(2)}, u32[]{:S(2)}) %collective-permute-start.9) | collective-permute-done | bytes 53280 | tf_op jit(solution)/shard_map/ppermute | solution.py:742
  59.0 0.0 collective-permute-done.8.refs_1_.refs_6_
  59.0 1.4 %collective-permute-start.11 = (bf16[576,128]{1,0:T(8,128)(2,1)S(1)}, bf16[576,128]{1,0:T(8,128)(2,1)S(1)}, u32[]{:S(2)}, u32[]{:S(2)}) collective-permute-start(bf16[576,128]{1,0:T(8,128)(2,1)S(1)} %shard_map.173.refs_9_.refs_0_), channel_id=1, source_target_pairs={{0,2},{2,0},{4,6},{6,4},{8,10},{10,8},{12,14},{14,12},{1,3},{3,1},... | collective-permute-start | bytes 442376 | tf_op jit(solution)/shard_map/ppermute | solution.py:742
  60.4 2.4 %shard_map.174 = (bf16[6,12,12,96]{3,2,1,0:T(8,128)(2,1)}, f32[7,7,96]{2,1,0:T(8,128)}) custom-call(s32[144]{0:T(256)S(1)} %get-tuple-element.29.refs_0_, s32[6,8]{1,0:T(8,128)S(1)} %copy-done.5, bf16[2496,128]{1,0:T(8,128)(2,1)S(1)} %bitcast.8, f32[1152,96]{1,0:T(8,128)S(1)} %get-tuple-element.46.refs_3_, f32[7,7,96]{2,1,0:T(8,128)S(1)} %copy-done.2, ...), custom_call_target="tpu_custom_call" | custom-call | bytes 1313920 | tf_op jit(solution)/shard_map/pallas_call | solution.py:35
  62.8 1.4 %collective-permute-done.11.refs_1_ = bf16[576,128]{1,0:T(8,128)(2,1)S(1)} collective-permute-done((bf16[576,128]{1,0:T(8,128)(2,1)S(1)}, bf16[576,128]{1,0:T(8,128)(2,1)S(1)}, u32[]{:S(2)}, u32[]{:S(2)}) %collective-permute-start.11) | collective-permute-done | bytes 147488 | tf_op jit(solution)/shard_map/ppermute | solution.py:742
  64.2 0.9 %shard_map.175 = (f32[192,384]{1,0:T(8,128)}, f32[192,384]{1,0:T(8,128)}) custom-call(bf16[576,128]{1,0:T(8,128)(2,1)S(1)} %shard_map.173.refs_9_.refs_0_, bf16[576,128]{1,0:T(8,128)(2,1)S(1)} %collective-permute-done.11.refs_1_), custom_call_target="tpu_custom_call" | custom-call | bytes 294912 | tf_op jit(solution)/shard_map/pallas_call | solution.py:35
  (4 shorter events, 0.1 us)
Async XLA Ops:
  2.9 7.5 %copy-start = (bf16[6,12,12,96]{3,2,1,0:T(8,128)(2,1)S(1)}, bf16[6,12,12,96]{3,2,1,0:T(8,128)(2,1)}, u32[]{:S(2)}) copy-start(bf16[6,12,12,96]{3,2,1,0:T(8,128)(2,1)} %refs_3_.3) | copy-start | bytes 497668
  2.9 7.4 %copy-start.1 = (bf16[6,12,12,96]{3,2,1,0:T(8,128)(2,1)S(1)}, bf16[6,12,12,96]{3,2,1,0:T(8,128)(2,1)}, u32[]{:S(2)}) copy-start(bf16[6,12,12,96]{3,2,1,0:T(8,128)(2,1)} %refs_4_.4) | copy-start | bytes 497668
  2.9 7.4 %copy-start.2 = (f32[7,7,96]{2,1,0:T(8,128)S(1)}, f32[7,7,96]{2,1,0:T(8,128)}, u32[]{:S(2)}) copy-start(f32[7,7,96]{2,1,0:T(8,128)} %refs_4_.5) | copy-start | bytes 56452
  2.9 18.1 %all-to-all-start = ((bf16[8,168,128]{2,1,0:T(8,128)(2,1)}), bf16[8,168,128]{2,1,0:T(8,128)(2,1)S(1)}, u32[]{:S(2)}, u32[]{:S(2)}) async-start(bf16[8,168,128]{2,1,0:T(8,128)(2,1)} %bitcast.13), calls=%async_computation | async-start | bytes 688128 | tf_op jit(solution)/shard_map/all_to_all | solution.py:733
  10.3 0.7 %copy-start.6 = (s32[144]{0:T(256)S(1)}, s32[144]{0:T(256)}, u32[]{:S(2)}) copy-start(s32[144]{0:T(256)} %get-tuple-element.28.refs_0_) | copy-start | bytes 1732
  10.3 0.7 %copy-start.7 = (f32[96]{0:T(128)S(1)}, f32[96]{0:T(128)}, u32[]{:S(2)}) copy-start(f32[96]{0:T(128)} %param.18) | copy-start | bytes 1156
  11.0 4.4 %copy-start.3 = (f32[192,384]{1,0:T(8,128)S(1)}, f32[192,384]{1,0:T(8,128)}, u32[]{:S(2)}) copy-start(f32[192,384]{1,0:T(8,128)} %refs_0_.3) | copy-start | bytes 884740
  11.0 4.4 %copy-start.4 = (f32[384,192]{0,1:T(8,128)S(1)}, f32[384,192]{0,1:T(8,128)}, u32[]{:S(2)}) copy-start(f32[384,192]{0,1:T(8,128)} %param.23) | copy-start | bytes 884740
  15.3 3.0 %collective-permute-start = (bf16[864,128]{1,0:T(8,128)(2,1)S(1)}, bf16[864,128]{1,0:T(8,128)(2,1)S(1)}, u32[]{:S(2)}, u32[]{:S(2)}) collective-permute-start(bf16[864,128]{1,0:T(8,128)(2,1)S(1)} %get-tuple-element.32), channel_id=1, source_target_pairs={{0,1},{1,0},{2,3},{3,2},{4,5},{5,4},{6,7},{7,6},{8,9},{9,8},{10,11... | collective-permute-start | bytes 663560 | tf_op jit(solution)/shard_map/ppermute | solution.py:737
  15.4 1.4 %copy-start.12 = (f32[96]{0:T(128)S(1)}, f32[96]{0:T(128)}, u32[]{:S(2)}) copy-start(f32[96]{0:T(128)} %param.25) | copy-start | bytes 1156
  16.1 0.7 %copy-start.8 = (f32[384]{0:T(512)S(1)}, f32[384]{0:T(512)}, u32[]{:S(2)}) copy-start(f32[384]{0:T(512)} %param.22) | copy-start | bytes 4612
  16.1 0.7 %copy-start.9 = (f32[96]{0:T(128)S(1)}, f32[96]{0:T(128)}, u32[]{:S(2)}) copy-start(f32[96]{0:T(128)} %param.19) | copy-start | bytes 1156
  16.1 0.7 %copy-start.10 = (f32[96]{0:T(128)S(1)}, f32[96]{0:T(128)}, u32[]{:S(2)}) copy-start(f32[96]{0:T(128)} %param.20) | copy-start | bytes 1156
  16.1 0.7 %copy-start.11 = (f32[96]{0:T(128)S(1)}, f32[96]{0:T(128)}, u32[]{:S(2)}) copy-start(f32[96]{0:T(128)} %param.24) | copy-start | bytes 1156
  16.1 2.1 %collective-permute-start.1 = (bf16[256,384]{1,0:T(8,128)(2,1)}, bf16[256,384]{1,0:T(8,128)(2,1)S(1)}, u32[]{:S(2)}, u32[]{:S(2)}) collective-permute-start(bf16[256,384]{1,0:T(8,128)(2,1)} %get-tuple-element.33), channel_id=1, source_target_pairs={{0,1},{1,0},{2,3},{3,2},{4,5},{5,4},{6,7},{7,6},{8,9},{9,8},{10,11... | collective-permute-start | bytes 589832 | tf_op jit(solution)/shard_map/ppermute | solution.py:737
  16.7 1.6 %collective-permute-start.2 = (bf16[256,384]{1,0:T(8,128)(2,1)S(1)}, bf16[256,384]{1,0:T(8,128)(2,1)S(1)}, u32[]{:S(2)}, u32[]{:S(2)}) collective-permute-start(bf16[256,384]{1,0:T(8,128)(2,1)S(1)} %get-tuple-element.34), channel_id=1, source_target_pairs={{0,1},{1,0},{2,3},{3,2},{4,5},{5,4},{6,7},{7,6},{8,9},{9,8},{10,11... | collective-permute-start | bytes 589832 | tf_op jit(solution)/shard_map/ppermute | solution.py:737
  16.9 4.1 %copy-start.5 = (s32[6,8]{1,0:T(8,128)S(1)}, s32[6,8]{1,0:T(8,128)}, u32[]{:S(2)}) copy-start(s32[6,8]{1,0:T(8,128)} %refs_1_.9) | copy-start | bytes 580
  16.9 1.4 %collective-permute-start.3 = (f32[1,768]{1,0:T(1,128)S(1)}, f32[1,768]{1,0:T(1,128)S(1)}, u32[]{:S(2)}, u32[]{:S(2)}) collective-permute-start(f32[1,768]{1,0:T(1,128)S(1)} %reshape.31.refs_8_), channel_id=1, source_target_pairs={{0,1},{1,0},{2,3},{3,2},{4,5},{5,4},{6,7},{7,6},{8,9},{9,8},{10,11... | collective-permute-start | bytes 9224 | tf_op jit(solution)/shard_map/ppermute | solution.py:737
  22.7 1.5 %collective-permute-start.4 = (f32[432,128]{1,0:T(8,128)S(1)}, f32[432,128]{1,0:T(8,128)S(1)}, u32[]{:S(2)}, u32[]{:S(2)}) collective-permute-start(f32[432,128]{1,0:T(8,128)S(1)} %get-tuple-element.36), channel_id=1, source_target_pairs={{0,1},{1,0},{2,3},{3,2},{4,5},{5,4},{6,7},{7,6},{8,9},{9,8},{10,11... | collective-permute-start | bytes 663560 | tf_op jit(solution)/shard_map/ppermute | solution.py:737
  27.0 1.8 %collective-permute-start.5 = (bf16[1584,128]{1,0:T(8,128)(2,1)S(1)}, bf16[1584,128]{1,0:T(8,128)(2,1)S(1)}, u32[]{:S(2)}, u32[]{:S(2)}) collective-permute-start(bf16[1584,128]{1,0:T(8,128)(2,1)S(1)} %get-tuple-element.41), channel_id=1, source_target_pairs={{0,1},{1,0},{2,3},{3,2},{4,5},{5,4},{6,7},{7,6},{8,9},{9,8},{10,11... | collective-permute-start | bytes 1216520 | tf_op jit(solution)/shard_map/ppermute | solution.py:737
  30.6 21.0 %all-to-all-start.1 = ((bf16[8,312,128]{2,1,0:T(8,128)(2,1)}), bf16[8,312,128]{2,1,0:T(8,128)(2,1)S(1)}, u32[]{:S(2)}, u32[]{:S(2)}) async-start(bf16[8,312,128]{2,1,0:T(8,128)(2,1)} %bitcast.4), calls=%async_computation.1 | async-start | bytes 1277952 | tf_op jit(solution)/shard_map/all_to_all | solution.py:733
  34.2 5.6 %collective-permute-start.6 = (bf16[432,128]{1,0:T(8,128)(2,1)S(1)}, bf16[432,128]{1,0:T(8,128)(2,1)S(1)}, u32[]{:S(2)}, u32[]{:S(2)}) collective-permute-start(bf16[432,128]{1,0:T(8,128)(2,1)S(1)} %get-tuple-element.43), channel_id=1, source_target_pairs={{0,1},{1,0},{2,3},{3,2},{4,5},{5,4},{6,7},{7,6},{8,9},{9,8},{10,11... | collective-permute-start | bytes 331784 | tf_op jit(solution)/shard_map/ppermute | solution.py:737
  37.9 5.6 %collective-permute-start.7 = (f32[7,7,96]{2,1,0:T(8,128)S(1)}, f32[7,7,96]{2,1,0:T(8,128)S(1)}, u32[]{:S(2)}, u32[]{:S(2)}) collective-permute-start(f32[7,7,96]{2,1,0:T(8,128)S(1)} %shard_map.171.refs_1_), channel_id=1, source_target_pairs={{0,2},{2,0},{4,6},{6,4},{8,10},{10,8},{12,14},{14,12},{1,3},{3,1},... | collective-permute-start | bytes 56456 | tf_op jit(solution)/shard_map/ppermute | solution.py:742
  51.7 6.3 %collective-permute-start.10 = (bf16[208,128]{1,0:T(8,128)(2,1)S(1)}, bf16[208,128]{1,0:T(8,128)(2,1)S(1)}, u32[]{:S(2)}, u32[]{:S(2)}) collective-permute-start(bf16[208,128]{1,0:T(8,128)(2,1)S(1)} %shard_map.172.refs_0_.refs_5_), channel_id=1, source_target_pairs={{0,12},{2,14},{4,8},{6,10},{8,4},{10,6},{12,0},{14,2},{1,13},{3,15... | collective-permute-start | bytes 159752 | tf_op jit(solution)/shard_map/ppermute | solution.py:742
  52.9 6.0 %collective-permute-start.9 = (bf16[208,128]{1,0:T(8,128)(2,1)S(1)}, bf16[208,128]{1,0:T(8,128)(2,1)S(1)}, u32[]{:S(2)}, u32[]{:S(2)}) collective-permute-start(bf16[208,128]{1,0:T(8,128)(2,1)S(1)} %shard_map.172.refs_0_.refs_5_), channel_id=1, source_target_pairs={{0,8},{2,10},{4,12},{6,14},{8,0},{10,2},{12,4},{14,6},{1,9},{3,11}... | collective-permute-start | bytes 159752 | tf_op jit(solution)/shard_map/ppermute | solution.py:742
  53.8 5.2 %collective-permute-start.8 = (bf16[208,128]{1,0:T(8,128)(2,1)S(1)}, bf16[208,128]{1,0:T(8,128)(2,1)S(1)}, u32[]{:S(2)}, u32[]{:S(2)}) collective-permute-start(bf16[208,128]{1,0:T(8,128)(2,1)S(1)} %shard_map.172.refs_0_.refs_5_), channel_id=1, source_target_pairs={{0,4},{2,6},{4,0},{6,2},{8,12},{10,14},{12,8},{14,10},{1,5},{3,7},... | collective-permute-start | bytes 159752 | tf_op jit(solution)/shard_map/ppermute | solution.py:742
  59.0 5.2 %collective-permute-start.11 = (bf16[576,128]{1,0:T(8,128)(2,1)S(1)}, bf16[576,128]{1,0:T(8,128)(2,1)S(1)}, u32[]{:S(2)}, u32[]{:S(2)}) collective-permute-start(bf16[576,128]{1,0:T(8,128)(2,1)S(1)} %shard_map.173.refs_9_.refs_0_), channel_id=1, source_target_pairs={{0,2},{2,0},{4,6},{6,4},{8,10},{10,8},{12,14},{14,12},{1,3},{3,1},... | collective-permute-start | bytes 442376 | tf_op jit(solution)/shard_map/ppermute | solution.py:742

commit v6 on v5

--- a/solution.py
+++ b/solution.py
@@ -75,7 +75,7 @@
         self.box3 = round_up(self.share, 8)
         self.taps_at = round_up(self.share, 16)
         self.message = round_up(self.taps_at + 49, 16)
-        self.paired = owners in (4, 8)
+        self.paired = owners == 8
 
     def owner_of(self, link):
         factor = -(-65536 // self.tiles)
@@ -205,7 +205,7 @@
 
 
 def field(z):
-    return pltpu.VMEM((z.wide * z.wide * 8, z.ch), F32)
+    return pltpu.VMEM((z.wide * z.wide * 8 + 256, z.ch), F32)
 
 
 def boxes(z, box):
@@ -213,15 +213,15 @@
 
 
 def flat_strips(z):
-    return pltpu.VMEM((z.links * 40, z.ch), F32)
+    return pltpu.VMEM((z.links * 40 + 8, z.ch), F32)
 
 
 def packed_strips(z):
-    return pltpu.VMEM((z.tiles * 4 * 32, LANES), F32)
+    return pltpu.VMEM((z.tiles * 4 * 32 + 8, LANES), F32)
 
 
 def pixel_major(z):
-    return pltpu.VMEM((z.rows, z.ch), F32)
+    return pltpu.VMEM((z.rows + 320, z.ch), F32)
 
 
 def first_strips(z, neighbour, tile_data):
@@ -538,7 +538,7 @@
             flat_strips(z),
             field(z),
             pixel_major(z),
-            pltpu.VMEM((z.pixels * 8, z.ch), F32),
+            pltpu.VMEM((z.pixels * 8 + 64, z.ch), F32),
             pltpu.VMEM((49 * 8, z.ch), F32),
         ],
         flops=2 * 49 * z.rows * z.ch,
@@ -588,7 +588,7 @@
         ),
         [g_own, received, *block, cotangent, taps],
         0,
-        [pixel_major(z), field(z), pltpu.VMEM((z.pixels * 8, z.ch), F32)],
+        [pixel_major(z), field(z), pltpu.VMEM((z.pixels * 8 + 64, z.ch), F32)],
         flops=2 * 49 * z.rows * z.ch,
     )
 
@@ -628,7 +628,7 @@
         boxes(z, z.box2),
         flat_strips(z),
         field(z),
-        pltpu.VMEM((z.pixels * 8, z.ch), F32),
+        pltpu.VMEM((z.pixels * 8 + 64, z.ch), F32),
         pltpu.VMEM((count * 56, z.ch), F32),
     ]
     if not count:

time: 65.4 us -> 65.4 us (level)
  no operation moved by 1% of the time
where the time goes in v6:
time: 65.4 us; the launch traced here: 65.1 us
  Pallas kernels  24.1 us (37%)
  starting transfers between devices  20.4 us (31%)
  waiting for transfers between devices  18.9 us (29%)
  local copies, waits for them, and re-layouts  0.84 us (1%)
  between operations  0.81 us (1%)
    pallas_call x12, Pallas kernels, call(): pl.pallas_call(run, out_shape=outs, in_specs=[pl.BlockSpec(memory_space=s...  24.1 us
    all_to_all x2, starting transfers between devices, exchange_tiles(): lax.all_to_all(boxes, 'tiles', split_axis=0, concat_axis=0, tiled=True)  11 us
    all_to_all x2, waiting for transfers between devices, exchange_tiles(): lax.all_to_all(boxes, 'tiles', split_axis=0, concat_axis=0, tiled=True)  10.8 us
    ppermute x5, starting transfers between devices, swap_tiles(): return lax.ppermute(piece, 'tiles', pairs)  7.77 us
    ppermute x5, waiting for transfers between devices, swap_tiles(): return lax.ppermute(piece, 'tiles', pairs)  4.28 us
    ppermute x7, waiting for transfers between devices, swap_sub(): return lax.ppermute(piece, 'sub', [(0, 1), (1, 0)])  3.91 us
    ppermute x7, starting transfers between devices, swap_sub(): return lax.ppermute(piece, 'sub', [(0, 1), (1, 0)])  1.65 us
  transfers between devices with their start and end apart: 14, of which 8 were waited for; matrix products, arithmetic and copies ran while one was open for 0% of the time, Pallas kernels for 22%

profile of v6, /device:TPU:0, one launch (start us, length us, event | category | flops | bytes accessed | tf_op | source)
XLA Modules:
  0.0 65.1 jit_solution(16465033583462391272)
XLA Ops:
  0.6 2.2 %shard_map.164 = (bf16[1344,128]{1,0:T(8,128)(2,1)}, s32[144]{0:T(256)}) custom-call(s32[6,8]{1,0:T(8,128)} %refs_0_.2, bf16[6,12,12,96]{3,2,1,0:T(8,128)(2,1)} %refs_3_.3), custom_call_target="tpu_custom_call" | custom-call | bytes 166080 | tf_op jit(solution)/shard_map/pallas_call | solution.py:35
  2.9 0.0 copy-start
  2.9 0.0 copy-start.1
  2.9 0.0 copy-start.2
  2.9 7.4 %all-to-all-start = ((bf16[8,168,128]{2,1,0:T(8,128)(2,1)}), bf16[8,168,128]{2,1,0:T(8,128)(2,1)S(1)}, u32[]{:S(2)}, u32[]{:S(2)}) async-start(bf16[8,168,128]{2,1,0:T(8,128)(2,1)} %bitcast.13), calls=%async_computation | async-start | bytes 688128 | tf_op jit(solution)/shard_map/all_to_all | solution.py:733
  10.3 0.0 copy-start.6
  10.3 0.0 copy-start.7
  10.3 0.0 copy-done
  10.3 0.0 copy-done.1
  10.4 0.0 copy-done.2
  10.4 0.6 copy-done.6
  11.0 0.0 copy-done.7
  11.0 0.0 copy-start.3
  11.0 0.0 copy-start.4
  11.0 4.3 %shard_map.165 = (bf16[864,128]{1,0:T(8,128)(2,1)S(1)}, bf16[864,128]{1,0:T(8,128)(2,1)S(1)}, f32[1152,96]{1,0:T(8,128)S(1)}, s32[144]{0:T(256)S(1)}) custom-call(s32[144]{0:T(256)S(1)} %copy-done.6, bf16[6,12,12,96]{3,2,1,0:T(8,128)(2,1)S(1)} %copy-done, bf16[6,12,12,96]{3,2,1,0:T(8,128)(2,1)S(1)} %copy-done.1, f32[7,7,96]{2,1,0:T(8,128)S(1)} %copy-done.2, ...), custom_call_target="tpu_custom_call" | custom-call | flops 8128512 | bytes 351552 | tf_op jit(solution)/shard_map/pallas_call | solution.py:35
  15.3 0.1 collective-permute-start
  15.4 0.0 copy-done.3
  15.4 0.0 copy-done.4
  15.4 0.0 copy-start.12
  15.4 0.7 %shard_map.166 = (bf16[256,384]{1,0:T(8,128)(2,1)S(1)}, bf16[256,384]{1,0:T(8,128)(2,1)S(1)}, bf16[256,384]{1,0:T(8,128)(2,1)}, bf16[256,384]{1,0:T(8,128)(2,1)S(1)}) custom-call(f32[192,384]{1,0:T(8,128)S(1)} %copy-done.3, f32[192,384]{1,0:T(8,128)S(1)} %bitcast.11), custom_call_target="tpu_custom_call" | custom-call | bytes 589824 | tf_op jit(solution)/shard_map/pallas_call | solution.py:35
  16.1 0.0 copy-start.8
  16.1 0.0 copy-start.9
  16.1 0.0 copy-start.10
  16.1 0.0 copy-start.11
  16.1 0.5 collective-permute-start.1
  16.7 0.1 collective-permute-start.2
  16.8 0.0 copy-done.12
  16.8 0.1 copy-done.8
  16.8 0.0 copy-done.9
  16.8 0.0 copy-done.10
  16.8 0.0 copy-done.11
  16.8 0.1 concatenate.3
  16.9 0.5 collective-permute-start.3
  17.5 0.8 %collective-permute-done.3.refs_8_.refs_9_ = f32[1,768]{1,0:T(1,128)S(1)} collective-permute-done((f32[1,768]{1,0:T(1,128)S(1)}, f32[1,768]{1,0:T(1,128)S(1)}, u32[]{:S(2)}, u32[]{:S(2)}) %collective-permute-start.3) | collective-permute-done | bytes 3104 | tf_op jit(solution)/shard_map/ppermute | solution.py:737
  18.3 0.0 collective-permute-done.1.refs_6_.refs_5_
  18.3 0.0 collective-permute-done.2.refs_7_
  18.3 0.0 collective-permute-done.refs_5_.refs_3_
  18.3 2.7 %all-to-all-done = bf16[8,168,128]{2,1,0:T(8,128)(2,1)S(1)} async-done(((bf16[8,168,128]{2,1,0:T(8,128)(2,1)}), bf16[8,168,128]{2,1,0:T(8,128)(2,1)S(1)}, u32[]{:S(2)}, u32[]{:S(2)}) %all-to-all-start) | async-done | bytes 344096 | tf_op jit(solution)/shard_map/all_to_all | solution.py:733
  21.0 0.0 copy-done.5
  21.0 1.7 %shard_map.167 = (f32[432,128]{1,0:T(8,128)S(1)}, f32[432,128]{1,0:T(8,128)S(1)}) custom-call(s32[144]{0:T(256)S(1)} %get-tuple-element.29.refs_0_, s32[6,8]{1,0:T(8,128)S(1)} %copy-done.5, bf16[1344,128]{1,0:T(8,128)(2,1)S(1)} %bitcast.9, f32[1152,96]{1,0:T(8,128)S(1)} %get-tuple-element.31.refs_3_, f32[7,7,96]{2,1,0:T(8,128)S(1)} %copy-done.2, ...), custom_call_target="tpu_custom_call" | custom-call | bytes 806016 | tf_op jit(solution)/shard_map/pallas_call | solution.py:35
  22.7 0.1 collective-permute-start.4
  22.7 1.5 %collective-permute-done.4.refs_1_ = f32[432,128]{1,0:T(8,128)S(1)} collective-permute-done((f32[432,128]{1,0:T(8,128)S(1)}, f32[432,128]{1,0:T(8,128)S(1)}, u32[]{:S(2)}, u32[]{:S(2)}) %collective-permute-start.4) | collective-permute-done | bytes 221216 | tf_op jit(solution)/shard_map/ppermute | solution.py:737
  24.2 2.8 %shard_map.168 = (bf16[432,128]{1,0:T(8,128)(2,1)S(1)}, bf16[432,128]{1,0:T(8,128)(2,1)S(1)}, bf16[432,128]{1,0:T(8,128)(2,1)S(1)}, f32[1152,128]{1,0:T(8,128)S(1)}, bf16[1584,128]{1,0:T(8,128)(2,1)S(1)}) custom-call(f32[432,128]{1,0:T(8,128)S(1)} %get-tuple-element.35.refs_0_, f32[432,128]{1,0:T(8,128)S(1)} %collective-permute-done.4.refs_1_, ...), custom_call_target="tpu_custom_call" | custom-call | flops 1019215872 | bytes 1677312 | tf_op jit(solution)/shard_map/pallas_call | solution.py:35
  27.0 0.2 collective-permute-start.5
  27.2 1.6 %collective-permute-done.5.refs_1_.refs_3_.refs_5_ = bf16[1584,128]{1,0:T(8,128)(2,1)S(1)} collective-permute-done((bf16[1584,128]{1,0:T(8,128)(2,1)S(1)}, bf16[1584,128]{1,0:T(8,128)(2,1)S(1)}, u32[]{:S(2)}, u32[]{:S(2)}) %collective-permute-start.5) | collective-permute-done | bytes 405536 | tf_op jit(solution)/shard_map/ppermute | solution.py:737
  28.8 1.8 %shard_map.170 = bf16[2496,128]{1,0:T(8,128)(2,1)} custom-call(s32[144]{0:T(256)S(1)} %get-tuple-element.29.refs_0_, bf16[432,128]{1,0:T(8,128)(2,1)S(1)} %get-tuple-element.40.refs_0_.refs_1_.refs_4_, f32[1152,128]{1,0:T(8,128)S(1)} %get-tuple-element.45.refs_2_, bf16[1584,128]{1,0:T(8,128)(2,1)S(1)} %collective-permute-done.5.refs_1_.refs_3_.refs_5_), custom_call_target="tpu_custom_call" | custom-call | bytes 1106496 | tf_op jit(solution)/shard_map/pallas_call | solution.py:35
  30.6 3.6 %all-to-all-start.1 = ((bf16[8,312,128]{2,1,0:T(8,128)(2,1)}), bf16[8,312,128]{2,1,0:T(8,128)(2,1)S(1)}, u32[]{:S(2)}, u32[]{:S(2)}) async-start(bf16[8,312,128]{2,1,0:T(8,128)(2,1)} %bitcast.4), calls=%async_computation.1 | async-start | bytes 1277952 | tf_op jit(solution)/shard_map/all_to_all | solution.py:733
  34.2 0.2 collective-permute-start.6
  34.4 3.5 %shard_map.171.refs_1_ = f32[7,7,96]{2,1,0:T(8,128)S(1)} custom-call(s32[144]{0:T(256)S(1)} %get-tuple-element.29.refs_0_, s32[6,8]{1,0:T(8,128)S(1)} %copy-done.5, bf16[1344,128]{1,0:T(8,128)(2,1)S(1)} %bitcast.10, bf16[6,12,12,96]{3,2,1,0:T(8,128)(2,1)S(1)} %copy-done, bf16[432,128]{1,0:T(8,128)(2,1)S(1)} %get-tuple-element.40.refs_0_.refs_1_.refs_4_, ...), custom_call_target="tpu_custom_call" | custom-call | flops 8128512 | bytes 1026816 | tf_op jit(solution)/shard_map/pallas_call | solution.py:35
  37.9 1.9 %collective-permute-start.7 = (f32[7,7,96]{2,1,0:T(8,128)S(1)}, f32[7,7,96]{2,1,0:T(8,128)S(1)}, u32[]{:S(2)}, u32[]{:S(2)}) collective-permute-start(f32[7,7,96]{2,1,0:T(8,128)S(1)} %shard_map.171.refs_1_), channel_id=1, source_target_pairs={{0,2},{2,0},{4,6},{6,4},{8,10},{10,8},{12,14},{14,12},{1,3},{3,1},... | collective-permute-start | bytes 56456 | tf_op jit(solution)/shard_map/ppermute | solution.py:742
  39.8 0.0 collective-permute-done.6.refs_3_
  39.8 3.7 %shard_map.169 = (f32[1152,96]{1,0:T(8,128)S(1)}, bf16[6,12,12,96]{3,2,1,0:T(8,128)(2,1)}) custom-call(bf16[432,128]{1,0:T(8,128)(2,1)S(1)} %get-tuple-element.40.refs_0_.refs_1_.refs_4_, bf16[1584,128]{1,0:T(8,128)(2,1)S(1)} %collective-permute-done.5.refs_1_.refs_3_.refs_5_, bf16[432,128]{1,0:T(8,128)(2,1)S(1)} %get-tuple-element.42.refs_2_, ...), custom_call_target="tpu_custom_call" | custom-call | flops 8128512 | bytes 921984 | tf_op jit(solution)/shard_map/pallas_call | solution.py:35
  43.5 0.0 collective-permute-done.7.refs_2_
  43.5 8.1 %all-to-all-done.1 = bf16[8,312,128]{2,1,0:T(8,128)(2,1)S(1)} async-done(((bf16[8,312,128]{2,1,0:T(8,128)(2,1)}), bf16[8,312,128]{2,1,0:T(8,128)(2,1)S(1)}, u32[]{:S(2)}, u32[]{:S(2)}) %all-to-all-start.1) | async-done | bytes 639008 | tf_op jit(solution)/shard_map/all_to_all | solution.py:733
  51.6 1.3 %collective-permute-start.10 = (bf16[208,128]{1,0:T(8,128)(2,1)S(1)}, bf16[208,128]{1,0:T(8,128)(2,1)S(1)}, u32[]{:S(2)}, u32[]{:S(2)}) collective-permute-start(bf16[208,128]{1,0:T(8,128)(2,1)S(1)} %shard_map.172.refs_0_.refs_5_), channel_id=1, source_target_pairs={{0,12},{2,14},{4,8},{6,10},{8,4},{10,6},{12,0},{14,2},{1,13},{3,15... | collective-permute-start | bytes 159752 | tf_op jit(solution)/shard_map/ppermute | solution.py:742
  52.9 0.9 %collective-permute-start.9 = (bf16[208,128]{1,0:T(8,128)(2,1)S(1)}, bf16[208,128]{1,0:T(8,128)(2,1)S(1)}, u32[]{:S(2)}, u32[]{:S(2)}) collective-permute-start(bf16[208,128]{1,0:T(8,128)(2,1)S(1)} %shard_map.172.refs_0_.refs_5_), channel_id=1, source_target_pairs={{0,8},{2,10},{4,12},{6,14},{8,0},{10,2},{12,4},{14,6},{1,9},{3,11}... | collective-permute-start | bytes 159752 | tf_op jit(solution)/shard_map/ppermute | solution.py:742
  53.8 2.3 %collective-permute-start.8 = (bf16[208,128]{1,0:T(8,128)(2,1)S(1)}, bf16[208,128]{1,0:T(8,128)(2,1)S(1)}, u32[]{:S(2)}, u32[]{:S(2)}) collective-permute-start(bf16[208,128]{1,0:T(8,128)(2,1)S(1)} %shard_map.172.refs_0_.refs_5_), channel_id=1, source_target_pairs={{0,4},{2,6},{4,0},{6,2},{8,12},{10,14},{12,8},{14,10},{1,5},{3,7},... | collective-permute-start | bytes 159752 | tf_op jit(solution)/shard_map/ppermute | solution.py:742
  56.1 1.9 %collective-permute-done.10.refs_3_.refs_8_ = bf16[208,128]{1,0:T(8,128)(2,1)S(1)} collective-permute-done((bf16[208,128]{1,0:T(8,128)(2,1)S(1)}, bf16[208,128]{1,0:T(8,128)(2,1)S(1)}, u32[]{:S(2)}, u32[]{:S(2)}) %collective-permute-start.10) | collective-permute-done | bytes 53280 | tf_op jit(solution)/shard_map/ppermute | solution.py:742
  58.0 1.0 %collective-permute-done.9.refs_2_.refs_7_ = bf16[208,128]{1,0:T(8,128)(2,1)S(1)} collective-permute-done((bf16[208,128]{1,0:T(8,128)(2,1)S(1)}, bf16[208,128]{1,0:T(8,128)(2,1)S(1)}, u32[]{:S(2)}, u32[]{:S(2)}) %collective-permute-start.9) | collective-permute-done | bytes 53280 | tf_op jit(solution)/shard_map/ppermute | solution.py:742
  59.0 0.0 collective-permute-done.8.refs_1_.refs_6_
  59.0 1.4 %collective-permute-start.11 = (bf16[576,128]{1,0:T(8,128)(2,1)S(1)}, bf16[576,128]{1,0:T(8,128)(2,1)S(1)}, u32[]{:S(2)}, u32[]{:S(2)}) collective-permute-start(bf16[576,128]{1,0:T(8,128)(2,1)S(1)} %shard_map.173.refs_9_.refs_0_), channel_id=1, source_target_pairs={{0,2},{2,0},{4,6},{6,4},{8,10},{10,8},{12,14},{14,12},{1,3},{3,1},... | collective-permute-start | bytes 442376 | tf_op jit(solution)/shard_map/ppermute | solution.py:742
  60.4 2.4 %shard_map.174 = (bf16[6,12,12,96]{3,2,1,0:T(8,128)(2,1)}, f32[7,7,96]{2,1,0:T(8,128)}) custom-call(s32[144]{0:T(256)S(1)} %get-tuple-element.29.refs_0_, s32[6,8]{1,0:T(8,128)S(1)} %copy-done.5, bf16[2496,128]{1,0:T(8,128)(2,1)S(1)} %bitcast.8, f32[1152,96]{1,0:T(8,128)S(1)} %get-tuple-element.46.refs_3_, f32[7,7,96]{2,1,0:T(8,128)S(1)} %copy-done.2, ...), custom_call_target="tpu_custom_call" | custom-call | bytes 1313920 | tf_op jit(solution)/shard_map/pallas_call | solution.py:35
  62.8 1.4 %collective-permute-done.11.refs_1_ = bf16[576,128]{1,0:T(8,128)(2,1)S(1)} collective-permute-done((bf16[576,128]{1,0:T(8,128)(2,1)S(1)}, bf16[576,128]{1,0:T(8,128)(2,1)S(1)}, u32[]{:S(2)}, u32[]{:S(2)}) %collective-permute-start.11) | collective-permute-done | bytes 147488 | tf_op jit(solution)/shard_map/ppermute | solution.py:742
  64.2 0.9 %shard_map.175 = (f32[192,384]{1,0:T(8,128)}, f32[192,384]{1,0:T(8,128)}) custom-call(bf16[576,128]{1,0:T(8,128)(2,1)S(1)} %shard_map.173.refs_9_.refs_0_, bf16[576,128]{1,0:T(8,128)(2,1)S(1)} %collective-permute-done.11.refs_1_), custom_call_target="tpu_custom_call" | custom-call | bytes 294912 | tf_op jit(solution)/shard_map/pallas_call | solution.py:35
  (4 shorter events, 0.1 us)
Async XLA Ops:
  2.9 7.5 %copy-start = (bf16[6,12,12,96]{3,2,1,0:T(8,128)(2,1)S(1)}, bf16[6,12,12,96]{3,2,1,0:T(8,128)(2,1)}, u32[]{:S(2)}) copy-start(bf16[6,12,12,96]{3,2,1,0:T(8,128)(2,1)} %refs_3_.3) | copy-start | bytes 497668
  2.9 7.5 %copy-start.1 = (bf16[6,12,12,96]{3,2,1,0:T(8,128)(2,1)S(1)}, bf16[6,12,12,96]{3,2,1,0:T(8,128)(2,1)}, u32[]{:S(2)}) copy-start(bf16[6,12,12,96]{3,2,1,0:T(8,128)(2,1)} %refs_4_.4) | copy-start | bytes 497668
  2.9 7.5 %copy-start.2 = (f32[7,7,96]{2,1,0:T(8,128)S(1)}, f32[7,7,96]{2,1,0:T(8,128)}, u32[]{:S(2)}) copy-start(f32[7,7,96]{2,1,0:T(8,128)} %refs_4_.5) | copy-start | bytes 56452
  2.9 18.1 %all-to-all-start = ((bf16[8,168,128]{2,1,0:T(8,128)(2,1)}), bf16[8,168,128]{2,1,0:T(8,128)(2,1)S(1)}, u32[]{:S(2)}, u32[]{:S(2)}) async-start(bf16[8,168,128]{2,1,0:T(8,128)(2,1)} %bitcast.13), calls=%async_computation | async-start | bytes 688128 | tf_op jit(solution)/shard_map/all_to_all | solution.py:733
  10.3 0.7 %copy-start.6 = (s32[144]{0:T(256)S(1)}, s32[144]{0:T(256)}, u32[]{:S(2)}) copy-start(s32[144]{0:T(256)} %get-tuple-element.28.refs_0_) | copy-start | bytes 1732
  10.3 0.7 %copy-start.7 = (f32[96]{0:T(128)S(1)}, f32[96]{0:T(128)}, u32[]{:S(2)}) copy-start(f32[96]{0:T(128)} %param.18) | copy-start | bytes 1156
  11.0 4.4 %copy-start.3 = (f32[192,384]{1,0:T(8,128)S(1)}, f32[192,384]{1,0:T(8,128)}, u32[]{:S(2)}) copy-start(f32[192,384]{1,0:T(8,128)} %refs_0_.3) | copy-start | bytes 884740
  11.0 4.4 %copy-start.4 = (f32[384,192]{0,1:T(8,128)S(1)}, f32[384,192]{0,1:T(8,128)}, u32[]{:S(2)}) copy-start(f32[384,192]{0,1:T(8,128)} %param.23) | copy-start | bytes 884740
  15.3 3.0 %collective-permute-start = (bf16[864,128]{1,0:T(8,128)(2,1)S(1)}, bf16[864,128]{1,0:T(8,128)(2,1)S(1)}, u32[]{:S(2)}, u32[]{:S(2)}) collective-permute-start(bf16[864,128]{1,0:T(8,128)(2,1)S(1)} %get-tuple-element.32), channel_id=1, source_target_pairs={{0,1},{1,0},{2,3},{3,2},{4,5},{5,4},{6,7},{7,6},{8,9},{9,8},{10,11... | collective-permute-start | bytes 663560 | tf_op jit(solution)/shard_map/ppermute | solution.py:737
  15.4 1.4 %copy-start.12 = (f32[96]{0:T(128)S(1)}, f32[96]{0:T(128)}, u32[]{:S(2)}) copy-start(f32[96]{0:T(128)} %param.25) | copy-start | bytes 1156
  16.1 0.7 %copy-start.8 = (f32[384]{0:T(512)S(1)}, f32[384]{0:T(512)}, u32[]{:S(2)}) copy-start(f32[384]{0:T(512)} %param.22) | copy-start | bytes 4612
  16.1 0.7 %copy-start.9 = (f32[96]{0:T(128)S(1)}, f32[96]{0:T(128)}, u32[]{:S(2)}) copy-start(f32[96]{0:T(128)} %param.19) | copy-start | bytes 1156
  16.1 0.7 %copy-start.10 = (f32[96]{0:T(128)S(1)}, f32[96]{0:T(128)}, u32[]{:S(2)}) copy-start(f32[96]{0:T(128)} %param.20) | copy-start | bytes 1156
  16.1 0.7 %copy-start.11 = (f32[96]{0:T(128)S(1)}, f32[96]{0:T(128)}, u32[]{:S(2)}) copy-start(f32[96]{0:T(128)} %param.24) | copy-start | bytes 1156
  16.1 2.1 %collective-permute-start.1 = (bf16[256,384]{1,0:T(8,128)(2,1)}, bf16[256,384]{1,0:T(8,128)(2,1)S(1)}, u32[]{:S(2)}, u32[]{:S(2)}) collective-permute-start(bf16[256,384]{1,0:T(8,128)(2,1)} %get-tuple-element.33), channel_id=1, source_target_pairs={{0,1},{1,0},{2,3},{3,2},{4,5},{5,4},{6,7},{7,6},{8,9},{9,8},{10,11... | collective-permute-start | bytes 589832 | tf_op jit(solution)/shard_map/ppermute | solution.py:737
  16.7 1.6 %collective-permute-start.2 = (bf16[256,384]{1,0:T(8,128)(2,1)S(1)}, bf16[256,384]{1,0:T(8,128)(2,1)S(1)}, u32[]{:S(2)}, u32[]{:S(2)}) collective-permute-start(bf16[256,384]{1,0:T(8,128)(2,1)S(1)} %get-tuple-element.34), channel_id=1, source_target_pairs={{0,1},{1,0},{2,3},{3,2},{4,5},{5,4},{6,7},{7,6},{8,9},{9,8},{10,11... | collective-permute-start | bytes 589832 | tf_op jit(solution)/shard_map/ppermute | solution.py:737
  16.9 4.1 %copy-start.5 = (s32[6,8]{1,0:T(8,128)S(1)}, s32[6,8]{1,0:T(8,128)}, u32[]{:S(2)}) copy-start(s32[6,8]{1,0:T(8,128)} %refs_1_.9) | copy-start | bytes 580
  16.9 1.4 %collective-permute-start.3 = (f32[1,768]{1,0:T(1,128)S(1)}, f32[1,768]{1,0:T(1,128)S(1)}, u32[]{:S(2)}, u32[]{:S(2)}) collective-permute-start(f32[1,768]{1,0:T(1,128)S(1)} %reshape.31.refs_8_), channel_id=1, source_target_pairs={{0,1},{1,0},{2,3},{3,2},{4,5},{5,4},{6,7},{7,6},{8,9},{9,8},{10,11... | collective-permute-start | bytes 9224 | tf_op jit(solution)/shard_map/ppermute | solution.py:737
  22.7 1.5 %collective-permute-start.4 = (f32[432,128]{1,0:T(8,128)S(1)}, f32[432,128]{1,0:T(8,128)S(1)}, u32[]{:S(2)}, u32[]{:S(2)}) collective-permute-start(f32[432,128]{1,0:T(8,128)S(1)} %get-tuple-element.36), channel_id=1, source_target_pairs={{0,1},{1,0},{2,3},{3,2},{4,5},{5,4},{6,7},{7,6},{8,9},{9,8},{10,11... | collective-permute-start | bytes 663560 | tf_op jit(solution)/shard_map/ppermute | solution.py:737
  27.0 1.8 %collective-permute-start.5 = (bf16[1584,128]{1,0:T(8,128)(2,1)S(1)}, bf16[1584,128]{1,0:T(8,128)(2,1)S(1)}, u32[]{:S(2)}, u32[]{:S(2)}) collective-permute-start(bf16[1584,128]{1,0:T(8,128)(2,1)S(1)} %get-tuple-element.41), channel_id=1, source_target_pairs={{0,1},{1,0},{2,3},{3,2},{4,5},{5,4},{6,7},{7,6},{8,9},{9,8},{10,11... | collective-permute-start | bytes 1216520 | tf_op jit(solution)/shard_map/ppermute | solution.py:737
  30.6 21.0 %all-to-all-start.1 = ((bf16[8,312,128]{2,1,0:T(8,128)(2,1)}), bf16[8,312,128]{2,1,0:T(8,128)(2,1)S(1)}, u32[]{:S(2)}, u32[]{:S(2)}) async-start(bf16[8,312,128]{2,1,0:T(8,128)(2,1)} %bitcast.4), calls=%async_computation.1 | async-start | bytes 1277952 | tf_op jit(solution)/shard_map/all_to_all | solution.py:733
  34.2 5.6 %collective-permute-start.6 = (bf16[432,128]{1,0:T(8,128)(2,1)S(1)}, bf16[432,128]{1,0:T(8,128)(2,1)S(1)}, u32[]{:S(2)}, u32[]{:S(2)}) collective-permute-start(bf16[432,128]{1,0:T(8,128)(2,1)S(1)} %get-tuple-element.43), channel_id=1, source_target_pairs={{0,1},{1,0},{2,3},{3,2},{4,5},{5,4},{6,7},{7,6},{8,9},{9,8},{10,11... | collective-permute-start | bytes 331784 | tf_op jit(solution)/shard_map/ppermute | solution.py:737
  37.9 5.6 %collective-permute-start.7 = (f32[7,7,96]{2,1,0:T(8,128)S(1)}, f32[7,7,96]{2,1,0:T(8,128)S(1)}, u32[]{:S(2)}, u32[]{:S(2)}) collective-permute-start(f32[7,7,96]{2,1,0:T(8,128)S(1)} %shard_map.171.refs_1_), channel_id=1, source_target_pairs={{0,2},{2,0},{4,6},{6,4},{8,10},{10,8},{12,14},{14,12},{1,3},{3,1},... | collective-permute-start | bytes 56456 | tf_op jit(solution)/shard_map/ppermute | solution.py:742
  51.6 6.3 %collective-permute-start.10 = (bf16[208,128]{1,0:T(8,128)(2,1)S(1)}, bf16[208,128]{1,0:T(8,128)(2,1)S(1)}, u32[]{:S(2)}, u32[]{:S(2)}) collective-permute-start(bf16[208,128]{1,0:T(8,128)(2,1)S(1)} %shard_map.172.refs_0_.refs_5_), channel_id=1, source_target_pairs={{0,12},{2,14},{4,8},{6,10},{8,4},{10,6},{12,0},{14,2},{1,13},{3,15... | collective-permute-start | bytes 159752 | tf_op jit(solution)/shard_map/ppermute | solution.py:742
  52.9 6.0 %collective-permute-start.9 = (bf16[208,128]{1,0:T(8,128)(2,1)S(1)}, bf16[208,128]{1,0:T(8,128)(2,1)S(1)}, u32[]{:S(2)}, u32[]{:S(2)}) collective-permute-start(bf16[208,128]{1,0:T(8,128)(2,1)S(1)} %shard_map.172.refs_0_.refs_5_), channel_id=1, source_target_pairs={{0,8},{2,10},{4,12},{6,14},{8,0},{10,2},{12,4},{14,6},{1,9},{3,11}... | collective-permute-start | bytes 159752 | tf_op jit(solution)/shard_map/ppermute | solution.py:742
  53.8 5.2 %collective-permute-start.8 = (bf16[208,128]{1,0:T(8,128)(2,1)S(1)}, bf16[208,128]{1,0:T(8,128)(2,1)S(1)}, u32[]{:S(2)}, u32[]{:S(2)}) collective-permute-start(bf16[208,128]{1,0:T(8,128)(2,1)S(1)} %shard_map.172.refs_0_.refs_5_), channel_id=1, source_target_pairs={{0,4},{2,6},{4,0},{6,2},{8,12},{10,14},{12,8},{14,10},{1,5},{3,7},... | collective-permute-start | bytes 159752 | tf_op jit(solution)/shard_map/ppermute | solution.py:742
  59.0 5.2 %collective-permute-start.11 = (bf16[576,128]{1,0:T(8,128)(2,1)S(1)}, bf16[576,128]{1,0:T(8,128)(2,1)S(1)}, u32[]{:S(2)}, u32[]{:S(2)}) collective-permute-start(bf16[576,128]{1,0:T(8,128)(2,1)S(1)} %shard_map.173.refs_9_.refs_0_), channel_id=1, source_target_pairs={{0,2},{2,0},{4,6},{6,4},{8,10},{10,8},{12,14},{14,12},{1,3},{3,1},... | collective-permute-start | bytes 442376 | tf_op jit(solution)/shard_map/ppermute | solution.py:742

commit v7 on v6

--- a/solution.py
+++ b/solution.py
@@ -74,7 +74,7 @@
         self.box2 = round_up(self.halo_at + self.capacity * self.strip, 8)
         self.box3 = round_up(self.share, 8)
         self.taps_at = round_up(self.share, 16)
-        self.message = round_up(self.taps_at + 49, 16)
+        self.message = self.taps_at + 40
         self.paired = owners == 8
 
     def owner_of(self, link):
@@ -603,7 +603,13 @@
             line = lax.axis_index("tiles") // 2
             for step, message in enumerate(messages):
                 at = pl.multiple_of(jnp.bitwise_xor(line, step) * 56, 8)
-                work[pl.ds(at, 49), :] = message[z.taps_at : z.taps_at + 49, 0 : z.ch].astype(F32)
+                packed = message[z.taps_at : z.taps_at + 40, :].astype(F32)
+                work[pl.ds(at, 37), :] = packed[0:37, 0 : z.ch]
+                for group in range(z.groups):
+                    lanes = slice(group * z.extra, (group + 1) * z.extra)
+                    work[pl.ds(at + 37, 12), lanes] = packed[
+                        group * 12 : (group + 1) * 12, z.ch : LANES
+                    ]
             for a in range(7):
                 total = work[a * 7 : a * 7 + 7, :]
                 for place in range(1, count):
@@ -629,7 +635,7 @@
         flat_strips(z),
         field(z),
         pltpu.VMEM((z.pixels * 8 + 64, z.ch), F32),
-        pltpu.VMEM((count * 56, z.ch), F32),
+        pltpu.VMEM((count * 56 + 16, z.ch), F32),
     ]
     if not count:
         outs, scratch = outs[0], scratch[:-1]
@@ -639,17 +645,21 @@
 
 
 def share_message(z, inbox, taps, after):
-    def body(inbox, taps_own, taps_far, out):
+    def body(inbox, taps_own, taps_far, out, work):
         total = inbox[0 : z.share, :].astype(F32)
         for owner in range(1, z.owners):
             at = owner * z.box2
             total = total + inbox[at : at + z.share, :].astype(F32)
         out[0 : z.share, :] = total.astype(BF16)
-        rows = [taps_own[a] + taps_far[a] for a in range(7)]
-        low = z.taps_at
-        out[low : low + 49, 0 : z.ch] = jnp.concatenate(rows, axis=0).astype(BF16)
-
-    return call(body, shaped((z.message, LANES), BF16), [inbox, *taps], after=after)
+        rows = jnp.concatenate([taps_own[a] + taps_far[a] for a in range(7)], axis=0)
+        work[...] = jnp.zeros_like(work)
+        work[0:37, 0 : z.ch] = rows[0:37]
+        for group in range(z.groups):
+            lanes = slice(group * z.extra, (group + 1) * z.extra)
+            work[group * 12 : (group + 1) * 12, z.ch : LANES] = rows[37:49, lanes]
+        out[z.taps_at : z.taps_at + 40, :] = work[0:40, :].astype(BF16)
+
+    return call(body, shaped((z.message, LANES), BF16), [inbox, *taps], scratch=[pltpu.VMEM((48, LANES), F32)], after=after)
 
 
 def column(z, messages):

time: 65.4 us -> 65.1 us (level)
  transfers between devices with their start and end apart: 14 -> 14, of which waited for: 8 -> 9; matrix products, arithmetic and copies ran while one was open for 0% -> 0% of each run, Pallas kernels for 22% -> 23%
where the time goes in v7:
time: 65.1 us; the launch traced here: 64.8 us
  Pallas kernels  24.2 us (37%)
  starting transfers between devices  20.6 us (32%)
  waiting for transfers between devices  18.4 us (28%)
  local copies, waits for them, and re-layouts  0.84 us (1%)
  between operations  0.8 us (1%)
    pallas_call x12, Pallas kernels, call(): pl.pallas_call(run, out_shape=outs, in_specs=[pl.BlockSpec(memory_space=s...  24.2 us
    all_to_all x2, starting transfers between devices, exchange_tiles(): lax.all_to_all(boxes, 'tiles', split_axis=0, concat_axis=0, tiled=True)  11 us
    all_to_all x2, waiting for transfers between devices, exchange_tiles(): lax.all_to_all(boxes, 'tiles', split_axis=0, concat_axis=0, tiled=True)  10.8 us
    ppermute x5, starting transfers between devices, swap_tiles(): return lax.ppermute(piece, 'tiles', pairs)  7.94 us
    ppermute x7, waiting for transfers between devices, swap_sub(): return lax.ppermute(piece, 'sub', [(0, 1), (1, 0)])  3.9 us
    ppermute x5, waiting for transfers between devices, swap_tiles(): return lax.ppermute(piece, 'tiles', pairs)  3.74 us
    ppermute x7, starting transfers between devices, swap_sub(): return lax.ppermute(piece, 'sub', [(0, 1), (1, 0)])  1.66 us
  transfers between devices with their start and end apart: 14, of which 9 were waited for; matrix products, arithmetic and copies ran while one was open for 0% of the time, Pallas kernels for 23%

profile of v7, /device:TPU:0, one launch (start us, length us, event | category | flops | bytes accessed | tf_op | source)
XLA Modules:
  0.0 64.8 jit_solution(15097573624469637865)
XLA Ops:
  0.6 2.2 %shard_map.164 = (bf16[1344,128]{1,0:T(8,128)(2,1)}, s32[144]{0:T(256)}) custom-call(s32[6,8]{1,0:T(8,128)} %refs_0_.2, bf16[6,12,12,96]{3,2,1,0:T(8,128)(2,1)} %refs_3_.3), custom_call_target="tpu_custom_call" | custom-call | bytes 166080 | tf_op jit(solution)/shard_map/pallas_call | solution.py:35
  2.9 0.0 copy-start
  2.9 0.0 copy-start.1
  2.9 0.0 copy-start.2
  2.9 7.4 %all-to-all-start = ((bf16[8,168,128]{2,1,0:T(8,128)(2,1)}), bf16[8,168,128]{2,1,0:T(8,128)(2,1)S(1)}, u32[]{:S(2)}, u32[]{:S(2)}) async-start(bf16[8,168,128]{2,1,0:T(8,128)(2,1)} %bitcast.13), calls=%async_computation | async-start | bytes 688128 | tf_op jit(solution)/shard_map/all_to_all | solution.py:743
  10.3 0.0 copy-start.7
  10.3 0.0 copy-done
  10.3 0.0 copy-done.1
  10.3 0.0 copy-done.2
  10.4 0.6 copy-done.6
  11.0 0.0 copy-done.7
  11.0 0.0 copy-start.3
  11.0 0.0 copy-start.4
  11.0 4.3 %shard_map.165 = (bf16[864,128]{1,0:T(8,128)(2,1)S(1)}, bf16[864,128]{1,0:T(8,128)(2,1)S(1)}, f32[1152,96]{1,0:T(8,128)S(1)}, s32[144]{0:T(256)S(1)}) custom-call(s32[144]{0:T(256)S(1)} %copy-done.6, bf16[6,12,12,96]{3,2,1,0:T(8,128)(2,1)S(1)} %copy-done, bf16[6,12,12,96]{3,2,1,0:T(8,128)(2,1)S(1)} %copy-done.1, f32[7,7,96]{2,1,0:T(8,128)S(1)} %copy-done.2, ...), custom_call_target="tpu_custom_call" | custom-call | flops 8128512 | bytes 351552 | tf_op jit(solution)/shard_map/pallas_call | solution.py:35
  15.3 0.1 collective-permute-start
  15.4 0.0 copy-done.3
  15.4 0.0 copy-done.4
  15.4 0.0 copy-start.12
  15.4 0.7 %shard_map.166 = (bf16[256,384]{1,0:T(8,128)(2,1)S(1)}, bf16[256,384]{1,0:T(8,128)(2,1)S(1)}, bf16[256,384]{1,0:T(8,128)(2,1)}, bf16[256,384]{1,0:T(8,128)(2,1)S(1)}) custom-call(f32[192,384]{1,0:T(8,128)S(1)} %copy-done.3, f32[192,384]{1,0:T(8,128)S(1)} %bitcast.11), custom_call_target="tpu_custom_call" | custom-call | bytes 589824 | tf_op jit(solution)/shard_map/pallas_call | solution.py:35
  16.1 0.0 copy-start.8
  16.1 0.0 copy-start.9
  16.1 0.0 copy-start.10
  16.1 0.0 copy-start.11
  16.1 0.5 collective-permute-start.1
  16.7 0.1 collective-permute-start.2
  16.8 0.0 copy-done.12
  16.8 0.1 copy-done.8
  16.8 0.0 copy-done.9
  16.8 0.0 copy-done.10
  16.8 0.0 copy-done.11
  16.8 0.1 concatenate.3
  16.9 0.5 collective-permute-start.3
  17.5 0.8 %collective-permute-done.3.refs_8_.refs_9_ = f32[1,768]{1,0:T(1,128)S(1)} collective-permute-done((f32[1,768]{1,0:T(1,128)S(1)}, f32[1,768]{1,0:T(1,128)S(1)}, u32[]{:S(2)}, u32[]{:S(2)}) %collective-permute-start.3) | collective-permute-done | bytes 3104 | tf_op jit(solution)/shard_map/ppermute | solution.py:747
  18.3 0.0 collective-permute-done.1.refs_6_.refs_5_
  18.3 0.0 collective-permute-done.2.refs_7_
  18.3 0.0 collective-permute-done.refs_5_.refs_3_
  18.3 2.7 %all-to-all-done = bf16[8,168,128]{2,1,0:T(8,128)(2,1)S(1)} async-done(((bf16[8,168,128]{2,1,0:T(8,128)(2,1)}), bf16[8,168,128]{2,1,0:T(8,128)(2,1)S(1)}, u32[]{:S(2)}, u32[]{:S(2)}) %all-to-all-start) | async-done | bytes 344096 | tf_op jit(solution)/shard_map/all_to_all | solution.py:743
  21.0 0.0 copy-done.5
  21.0 1.7 %shard_map.167 = (f32[432,128]{1,0:T(8,128)S(1)}, f32[432,128]{1,0:T(8,128)S(1)}) custom-call(s32[144]{0:T(256)S(1)} %get-tuple-element.29.refs_0_, s32[6,8]{1,0:T(8,128)S(1)} %copy-done.5, bf16[1344,128]{1,0:T(8,128)(2,1)S(1)} %bitcast.9, f32[1152,96]{1,0:T(8,128)S(1)} %get-tuple-element.31.refs_3_, f32[7,7,96]{2,1,0:T(8,128)S(1)} %copy-done.2, ...), custom_call_target="tpu_custom_call" | custom-call | bytes 806016 | tf_op jit(solution)/shard_map/pallas_call | solution.py:35
  22.7 0.1 collective-permute-start.4
  22.7 1.5 %collective-permute-done.4.refs_1_ = f32[432,128]{1,0:T(8,128)S(1)} collective-permute-done((f32[432,128]{1,0:T(8,128)S(1)}, f32[432,128]{1,0:T(8,128)S(1)}, u32[]{:S(2)}, u32[]{:S(2)}) %collective-permute-start.4) | collective-permute-done | bytes 221216 | tf_op jit(solution)/shard_map/ppermute | solution.py:747
  24.2 2.8 %shard_map.168 = (bf16[432,128]{1,0:T(8,128)(2,1)S(1)}, bf16[432,128]{1,0:T(8,128)(2,1)S(1)}, bf16[432,128]{1,0:T(8,128)(2,1)S(1)}, f32[1152,128]{1,0:T(8,128)S(1)}, bf16[1584,128]{1,0:T(8,128)(2,1)S(1)}) custom-call(f32[432,128]{1,0:T(8,128)S(1)} %get-tuple-element.35.refs_0_, f32[432,128]{1,0:T(8,128)S(1)} %collective-permute-done.4.refs_1_, ...), custom_call_target="tpu_custom_call" | custom-call | flops 1019215872 | bytes 1677312 | tf_op jit(solution)/shard_map/pallas_call | solution.py:35
  27.0 0.2 collective-permute-start.5
  27.2 1.6 %collective-permute-done.5.refs_1_.refs_3_.refs_5_ = bf16[1584,128]{1,0:T(8,128)(2,1)S(1)} collective-permute-done((bf16[1584,128]{1,0:T(8,128)(2,1)S(1)}, bf16[1584,128]{1,0:T(8,128)(2,1)S(1)}, u32[]{:S(2)}, u32[]{:S(2)}) %collective-permute-start.5) | collective-permute-done | bytes 405536 | tf_op jit(solution)/shard_map/ppermute | solution.py:747
  28.8 1.8 %shard_map.170 = bf16[2496,128]{1,0:T(8,128)(2,1)} custom-call(s32[144]{0:T(256)S(1)} %get-tuple-element.29.refs_0_, bf16[432,128]{1,0:T(8,128)(2,1)S(1)} %get-tuple-element.40.refs_0_.refs_1_.refs_4_, f32[1152,128]{1,0:T(8,128)S(1)} %get-tuple-element.45.refs_2_, bf16[1584,128]{1,0:T(8,128)(2,1)S(1)} %collective-permute-done.5.refs_1_.refs_3_.refs_5_), custom_call_target="tpu_custom_call" | custom-call | bytes 1106496 | tf_op jit(solution)/shard_map/pallas_call | solution.py:35
  30.6 3.6 %all-to-all-start.1 = ((bf16[8,312,128]{2,1,0:T(8,128)(2,1)}), bf16[8,312,128]{2,1,0:T(8,128)(2,1)S(1)}, u32[]{:S(2)}, u32[]{:S(2)}) async-start(bf16[8,312,128]{2,1,0:T(8,128)(2,1)} %bitcast.4), calls=%async_computation.1 | async-start | bytes 1277952 | tf_op jit(solution)/shard_map/all_to_all | solution.py:743
  34.2 0.2 collective-permute-start.6
  34.4 3.5 %shard_map.171.refs_1_ = f32[7,7,96]{2,1,0:T(8,128)S(1)} custom-call(s32[144]{0:T(256)S(1)} %get-tuple-element.29.refs_0_, s32[6,8]{1,0:T(8,128)S(1)} %copy-done.5, bf16[1344,128]{1,0:T(8,128)(2,1)S(1)} %bitcast.10, bf16[6,12,12,96]{3,2,1,0:T(8,128)(2,1)S(1)} %copy-done, bf16[432,128]{1,0:T(8,128)(2,1)S(1)} %get-tuple-element.40.refs_0_.refs_1_.refs_4_, ...), custom_call_target="tpu_custom_call" | custom-call | flops 8128512 | bytes 1026816 | tf_op jit(solution)/shard_map/pallas_call | solution.py:35
  37.9 1.9 %collective-permute-start.7 = (f32[7,7,96]{2,1,0:T(8,128)S(1)}, f32[7,7,96]{2,1,0:T(8,128)S(1)}, u32[]{:S(2)}, u32[]{:S(2)}) collective-permute-start(f32[7,7,96]{2,1,0:T(8,128)S(1)} %shard_map.171.refs_1_), channel_id=1, source_target_pairs={{0,2},{2,0},{4,6},{6,4},{8,10},{10,8},{12,14},{14,12},{1,3},{3,1},... | collective-permute-start | bytes 56456 | tf_op jit(solution)/shard_map/ppermute | solution.py:752
  39.8 0.0 collective-permute-done.6.refs_3_
  39.8 3.7 %shard_map.169 = (f32[1152,96]{1,0:T(8,128)S(1)}, bf16[6,12,12,96]{3,2,1,0:T(8,128)(2,1)}) custom-call(bf16[432,128]{1,0:T(8,128)(2,1)S(1)} %get-tuple-element.40.refs_0_.refs_1_.refs_4_, bf16[1584,128]{1,0:T(8,128)(2,1)S(1)} %collective-permute-done.5.refs_1_.refs_3_.refs_5_, bf16[432,128]{1,0:T(8,128)(2,1)S(1)} %get-tuple-element.42.refs_2_, ...), custom_call_target="tpu_custom_call" | custom-call | flops 8128512 | bytes 921984 | tf_op jit(solution)/shard_map/pallas_call | solution.py:35
  43.5 0.0 collective-permute-done.7.refs_2_
  43.5 8.1 %all-to-all-done.1 = bf16[8,312,128]{2,1,0:T(8,128)(2,1)S(1)} async-done(((bf16[8,312,128]{2,1,0:T(8,128)(2,1)}), bf16[8,312,128]{2,1,0:T(8,128)(2,1)S(1)}, u32[]{:S(2)}, u32[]{:S(2)}) %all-to-all-start.1) | async-done | bytes 639008 | tf_op jit(solution)/shard_map/all_to_all | solution.py:743
  51.6 0.1 shard_map.172.refs_0_.refs_5_
  51.7 1.3 %collective-permute-start.10 = (bf16[184,128]{1,0:T(8,128)(2,1)S(1)}, bf16[184,128]{1,0:T(8,128)(2,1)S(1)}, u32[]{:S(2)}, u32[]{:S(2)}) collective-permute-start(bf16[184,128]{1,0:T(8,128)(2,1)S(1)} %shard_map.172.refs_0_.refs_5_), channel_id=1, source_target_pairs={{0,12},{2,14},{4,8},{6,10},{8,4},{10,6},{12,0},{14,2},{1,13},{3,15... | collective-permute-start | bytes 141320 | tf_op jit(solution)/shard_map/ppermute | solution.py:752
  53.0 0.9 %collective-permute-start.9 = (bf16[184,128]{1,0:T(8,128)(2,1)S(1)}, bf16[184,128]{1,0:T(8,128)(2,1)S(1)}, u32[]{:S(2)}, u32[]{:S(2)}) collective-permute-start(bf16[184,128]{1,0:T(8,128)(2,1)S(1)} %shard_map.172.refs_0_.refs_5_), channel_id=1, source_target_pairs={{0,8},{2,10},{4,12},{6,14},{8,0},{10,2},{12,4},{14,6},{1,9},{3,11}... | collective-permute-start | bytes 141320 | tf_op jit(solution)/shard_map/ppermute | solution.py:752
  53.8 2.3 %collective-permute-start.8 = (bf16[184,128]{1,0:T(8,128)(2,1)S(1)}, bf16[184,128]{1,0:T(8,128)(2,1)S(1)}, u32[]{:S(2)}, u32[]{:S(2)}) collective-permute-start(bf16[184,128]{1,0:T(8,128)(2,1)S(1)} %shard_map.172.refs_0_.refs_5_), channel_id=1, source_target_pairs={{0,4},{2,6},{4,0},{6,2},{8,12},{10,14},{12,8},{14,10},{1,5},{3,7},... | collective-permute-start | bytes 141320 | tf_op jit(solution)/shard_map/ppermute | solution.py:752
  56.1 1.7 %collective-permute-done.10.refs_3_.refs_8_ = bf16[184,128]{1,0:T(8,128)(2,1)S(1)} collective-permute-done((bf16[184,128]{1,0:T(8,128)(2,1)S(1)}, bf16[184,128]{1,0:T(8,128)(2,1)S(1)}, u32[]{:S(2)}, u32[]{:S(2)}) %collective-permute-start.10) | collective-permute-done | bytes 47136 | tf_op jit(solution)/shard_map/ppermute | solution.py:752
  57.9 0.6 collective-permute-done.9.refs_2_.refs_7_
  58.4 0.2 collective-permute-done.8.refs_1_.refs_6_
  58.7 1.6 %collective-permute-start.11 = (bf16[576,128]{1,0:T(8,128)(2,1)S(1)}, bf16[576,128]{1,0:T(8,128)(2,1)S(1)}, u32[]{:S(2)}, u32[]{:S(2)}) collective-permute-start(bf16[576,128]{1,0:T(8,128)(2,1)S(1)} %shard_map.173.refs_9_.refs_0_), channel_id=1, source_target_pairs={{0,2},{2,0},{4,6},{6,4},{8,10},{10,8},{12,14},{14,12},{1,3},{3,1},... | collective-permute-start | bytes 442376 | tf_op jit(solution)/shard_map/ppermute | solution.py:752
  60.2 2.4 %shard_map.174 = (bf16[6,12,12,96]{3,2,1,0:T(8,128)(2,1)}, f32[7,7,96]{2,1,0:T(8,128)}) custom-call(s32[144]{0:T(256)S(1)} %get-tuple-element.29.refs_0_, s32[6,8]{1,0:T(8,128)S(1)} %copy-done.5, bf16[2496,128]{1,0:T(8,128)(2,1)S(1)} %bitcast.8, f32[1152,96]{1,0:T(8,128)S(1)} %get-tuple-element.46.refs_3_, f32[7,7,96]{2,1,0:T(8,128)S(1)} %copy-done.2, ...), custom_call_target="tpu_custom_call" | custom-call | bytes 1289344 | tf_op jit(solution)/shard_map/pallas_call | solution.py:35
  62.7 1.2 %collective-permute-done.11.refs_1_ = bf16[576,128]{1,0:T(8,128)(2,1)S(1)} collective-permute-done((bf16[576,128]{1,0:T(8,128)(2,1)S(1)}, bf16[576,128]{1,0:T(8,128)(2,1)S(1)}, u32[]{:S(2)}, u32[]{:S(2)}) %collective-permute-start.11) | collective-permute-done | bytes 147488 | tf_op jit(solution)/shard_map/ppermute | solution.py:752
  63.9 0.9 %shard_map.175 = (f32[192,384]{1,0:T(8,128)}, f32[192,384]{1,0:T(8,128)}) custom-call(bf16[576,128]{1,0:T(8,128)(2,1)S(1)} %shard_map.173.refs_9_.refs_0_, bf16[576,128]{1,0:T(8,128)(2,1)S(1)} %collective-permute-done.11.refs_1_), custom_call_target="tpu_custom_call" | custom-call | bytes 294912 | tf_op jit(solution)/shard_map/pallas_call | solution.py:35
  (4 shorter events, 0.0 us)
Async XLA Ops:
  2.9 7.5 %copy-start = (bf16[6,12,12,96]{3,2,1,0:T(8,128)(2,1)S(1)}, bf16[6,12,12,96]{3,2,1,0:T(8,128)(2,1)}, u32[]{:S(2)}) copy-start(bf16[6,12,12,96]{3,2,1,0:T(8,128)(2,1)} %refs_3_.3) | copy-start | bytes 497668
  2.9 7.5 %copy-start.1 = (bf16[6,12,12,96]{3,2,1,0:T(8,128)(2,1)S(1)}, bf16[6,12,12,96]{3,2,1,0:T(8,128)(2,1)}, u32[]{:S(2)}) copy-start(bf16[6,12,12,96]{3,2,1,0:T(8,128)(2,1)} %refs_4_.4) | copy-start | bytes 497668
  2.9 7.4 %copy-start.2 = (f32[7,7,96]{2,1,0:T(8,128)S(1)}, f32[7,7,96]{2,1,0:T(8,128)}, u32[]{:S(2)}) copy-start(f32[7,7,96]{2,1,0:T(8,128)} %refs_4_.5) | copy-start | bytes 56452
  2.9 18.1 %all-to-all-start = ((bf16[8,168,128]{2,1,0:T(8,128)(2,1)}), bf16[8,168,128]{2,1,0:T(8,128)(2,1)S(1)}, u32[]{:S(2)}, u32[]{:S(2)}) async-start(bf16[8,168,128]{2,1,0:T(8,128)(2,1)} %bitcast.13), calls=%async_computation | async-start | bytes 688128 | tf_op jit(solution)/shard_map/all_to_all | solution.py:743
  10.3 0.7 %copy-start.6 = (s32[144]{0:T(256)S(1)}, s32[144]{0:T(256)}, u32[]{:S(2)}) copy-start(s32[144]{0:T(256)} %get-tuple-element.28.refs_0_) | copy-start | bytes 1732
  10.3 0.7 %copy-start.7 = (f32[96]{0:T(128)S(1)}, f32[96]{0:T(128)}, u32[]{:S(2)}) copy-start(f32[96]{0:T(128)} %param.18) | copy-start | bytes 1156
  11.0 4.4 %copy-start.3 = (f32[192,384]{1,0:T(8,128)S(1)}, f32[192,384]{1,0:T(8,128)}, u32[]{:S(2)}) copy-start(f32[192,384]{1,0:T(8,128)} %refs_0_.3) | copy-start | bytes 884740
  11.0 4.4 %copy-start.4 = (f32[384,192]{0,1:T(8,128)S(1)}, f32[384,192]{0,1:T(8,128)}, u32[]{:S(2)}) copy-start(f32[384,192]{0,1:T(8,128)} %param.23) | copy-start | bytes 884740
  15.3 3.0 %collective-permute-start = (bf16[864,128]{1,0:T(8,128)(2,1)S(1)}, bf16[864,128]{1,0:T(8,128)(2,1)S(1)}, u32[]{:S(2)}, u32[]{:S(2)}) collective-permute-start(bf16[864,128]{1,0:T(8,128)(2,1)S(1)} %get-tuple-element.32), channel_id=1, source_target_pairs={{0,1},{1,0},{2,3},{3,2},{4,5},{5,4},{6,7},{7,6},{8,9},{9,8},{10,11... | collective-permute-start | bytes 663560 | tf_op jit(solution)/shard_map/ppermute | solution.py:747
  15.4 1.4 %copy-start.12 = (f32[96]{0:T(128)S(1)}, f32[96]{0:T(128)}, u32[]{:S(2)}) copy-start(f32[96]{0:T(128)} %param.25) | copy-start | bytes 1156
  16.1 0.7 %copy-start.8 = (f32[384]{0:T(512)S(1)}, f32[384]{0:T(512)}, u32[]{:S(2)}) copy-start(f32[384]{0:T(512)} %param.22) | copy-start | bytes 4612
  16.1 0.7 %copy-start.9 = (f32[96]{0:T(128)S(1)}, f32[96]{0:T(128)}, u32[]{:S(2)}) copy-start(f32[96]{0:T(128)} %param.19) | copy-start | bytes 1156
  16.1 0.7 %copy-start.10 = (f32[96]{0:T(128)S(1)}, f32[96]{0:T(128)}, u32[]{:S(2)}) copy-start(f32[96]{0:T(128)} %param.20) | copy-start | bytes 1156
  16.1 0.7 %copy-start.11 = (f32[96]{0:T(128)S(1)}, f32[96]{0:T(128)}, u32[]{:S(2)}) copy-start(f32[96]{0:T(128)} %param.24) | copy-start | bytes 1156
  16.1 2.1 %collective-permute-start.1 = (bf16[256,384]{1,0:T(8,128)(2,1)}, bf16[256,384]{1,0:T(8,128)(2,1)S(1)}, u32[]{:S(2)}, u32[]{:S(2)}) collective-permute-start(bf16[256,384]{1,0:T(8,128)(2,1)} %get-tuple-element.33), channel_id=1, source_target_pairs={{0,1},{1,0},{2,3},{3,2},{4,5},{5,4},{6,7},{7,6},{8,9},{9,8},{10,11... | collective-permute-start | bytes 589832 | tf_op jit(solution)/shard_map/ppermute | solution.py:747
  16.7 1.6 %collective-permute-start.2 = (bf16[256,384]{1,0:T(8,128)(2,1)S(1)}, bf16[256,384]{1,0:T(8,128)(2,1)S(1)}, u32[]{:S(2)}, u32[]{:S(2)}) collective-permute-start(bf16[256,384]{1,0:T(8,128)(2,1)S(1)} %get-tuple-element.34), channel_id=1, source_target_pairs={{0,1},{1,0},{2,3},{3,2},{4,5},{5,4},{6,7},{7,6},{8,9},{9,8},{10,11... | collective-permute-start | bytes 589832 | tf_op jit(solution)/shard_map/ppermute | solution.py:747
  16.9 4.1 %copy-start.5 = (s32[6,8]{1,0:T(8,128)S(1)}, s32[6,8]{1,0:T(8,128)}, u32[]{:S(2)}) copy-start(s32[6,8]{1,0:T(8,128)} %refs_1_.9) | copy-start | bytes 580
  16.9 1.4 %collective-permute-start.3 = (f32[1,768]{1,0:T(1,128)S(1)}, f32[1,768]{1,0:T(1,128)S(1)}, u32[]{:S(2)}, u32[]{:S(2)}) collective-permute-start(f32[1,768]{1,0:T(1,128)S(1)} %reshape.31.refs_8_), channel_id=1, source_target_pairs={{0,1},{1,0},{2,3},{3,2},{4,5},{5,4},{6,7},{7,6},{8,9},{9,8},{10,11... | collective-permute-start | bytes 9224 | tf_op jit(solution)/shard_map/ppermute | solution.py:747
  22.7 1.5 %collective-permute-start.4 = (f32[432,128]{1,0:T(8,128)S(1)}, f32[432,128]{1,0:T(8,128)S(1)}, u32[]{:S(2)}, u32[]{:S(2)}) collective-permute-start(f32[432,128]{1,0:T(8,128)S(1)} %get-tuple-element.36), channel_id=1, source_target_pairs={{0,1},{1,0},{2,3},{3,2},{4,5},{5,4},{6,7},{7,6},{8,9},{9,8},{10,11... | collective-permute-start | bytes 663560 | tf_op jit(solution)/shard_map/ppermute | solution.py:747
  27.0 1.8 %collective-permute-start.5 = (bf16[1584,128]{1,0:T(8,128)(2,1)S(1)}, bf16[1584,128]{1,0:T(8,128)(2,1)S(1)}, u32[]{:S(2)}, u32[]{:S(2)}) collective-permute-start(bf16[1584,128]{1,0:T(8,128)(2,1)S(1)} %get-tuple-element.41), channel_id=1, source_target_pairs={{0,1},{1,0},{2,3},{3,2},{4,5},{5,4},{6,7},{7,6},{8,9},{9,8},{10,11... | collective-permute-start | bytes 1216520 | tf_op jit(solution)/shard_map/ppermute | solution.py:747
  30.6 21.0 %all-to-all-start.1 = ((bf16[8,312,128]{2,1,0:T(8,128)(2,1)}), bf16[8,312,128]{2,1,0:T(8,128)(2,1)S(1)}, u32[]{:S(2)}, u32[]{:S(2)}) async-start(bf16[8,312,128]{2,1,0:T(8,128)(2,1)} %bitcast.4), calls=%async_computation.1 | async-start | bytes 1277952 | tf_op jit(solution)/shard_map/all_to_all | solution.py:743
  34.2 5.6 %collective-permute-start.6 = (bf16[432,128]{1,0:T(8,128)(2,1)S(1)}, bf16[432,128]{1,0:T(8,128)(2,1)S(1)}, u32[]{:S(2)}, u32[]{:S(2)}) collective-permute-start(bf16[432,128]{1,0:T(8,128)(2,1)S(1)} %get-tuple-element.43), channel_id=1, source_target_pairs={{0,1},{1,0},{2,3},{3,2},{4,5},{5,4},{6,7},{7,6},{8,9},{9,8},{10,11... | collective-permute-start | bytes 331784 | tf_op jit(solution)/shard_map/ppermute | solution.py:747
  37.9 5.7 %collective-permute-start.7 = (f32[7,7,96]{2,1,0:T(8,128)S(1)}, f32[7,7,96]{2,1,0:T(8,128)S(1)}, u32[]{:S(2)}, u32[]{:S(2)}) collective-permute-start(f32[7,7,96]{2,1,0:T(8,128)S(1)} %shard_map.171.refs_1_), channel_id=1, source_target_pairs={{0,2},{2,0},{4,6},{6,4},{8,10},{10,8},{12,14},{14,12},{1,3},{3,1},... | collective-permute-start | bytes 56456 | tf_op jit(solution)/shard_map/ppermute | solution.py:752
  51.7 6.2 %collective-permute-start.10 = (bf16[184,128]{1,0:T(8,128)(2,1)S(1)}, bf16[184,128]{1,0:T(8,128)(2,1)S(1)}, u32[]{:S(2)}, u32[]{:S(2)}) collective-permute-start(bf16[184,128]{1,0:T(8,128)(2,1)S(1)} %shard_map.172.refs_0_.refs_5_), channel_id=1, source_target_pairs={{0,12},{2,14},{4,8},{6,10},{8,4},{10,6},{12,0},{14,2},{1,13},{3,15... | collective-permute-start | bytes 141320 | tf_op jit(solution)/shard_map/ppermute | solution.py:752
  53.0 5.5 %collective-permute-start.9 = (bf16[184,128]{1,0:T(8,128)(2,1)S(1)}, bf16[184,128]{1,0:T(8,128)(2,1)S(1)}, u32[]{:S(2)}, u32[]{:S(2)}) collective-permute-start(bf16[184,128]{1,0:T(8,128)(2,1)S(1)} %shard_map.172.refs_0_.refs_5_), channel_id=1, source_target_pairs={{0,8},{2,10},{4,12},{6,14},{8,0},{10,2},{12,4},{14,6},{1,9},{3,11}... | collective-permute-start | bytes 141320 | tf_op jit(solution)/shard_map/ppermute | solution.py:752
  53.8 4.8 %collective-permute-start.8 = (bf16[184,128]{1,0:T(8,128)(2,1)S(1)}, bf16[184,128]{1,0:T(8,128)(2,1)S(1)}, u32[]{:S(2)}, u32[]{:S(2)}) collective-permute-start(bf16[184,128]{1,0:T(8,128)(2,1)S(1)} %shard_map.172.refs_0_.refs_5_), channel_id=1, source_target_pairs={{0,4},{2,6},{4,0},{6,2},{8,12},{10,14},{12,8},{14,10},{1,5},{3,7},... | collective-permute-start | bytes 141320 | tf_op jit(solution)/shard_map/ppermute | solution.py:752
  58.7 5.2 %collective-permute-start.11 = (bf16[576,128]{1,0:T(8,128)(2,1)S(1)}, bf16[576,128]{1,0:T(8,128)(2,1)S(1)}, u32[]{:S(2)}, u32[]{:S(2)}) collective-permute-start(bf16[576,128]{1,0:T(8,128)(2,1)S(1)} %shard_map.173.refs_9_.refs_0_), channel_id=1, source_target_pairs={{0,2},{2,0},{4,6},{6,4},{8,10},{10,8},{12,14},{14,12},{1,3},{3,1},... | collective-permute-start | bytes 442376 | tf_op jit(solution)/shard_map/ppermute | solution.py:752
